TPU v7x, 512 devices: a whole 4x8x8 slice. The times are simulated.
512 devices in a mesh: energy: 64 (over y_hi, x, z), slab: 8 (over y_lo, core).
Axes of the slice: x: 4, y: 8 (y_hi: 2, y_lo: 4; y = y_hi * 4 + y_lo), z: 8, core: 2. Of those that a mesh axis runs over, the one named last changes fastest.
Arguments:
- green_local: bfloat16 [128, 8, 2, 512, 512], P('energy', 'slab'), may hold values from -2.5 to 2.5
- coupling: bfloat16 [8, 512, 512], P('slab', 'energy'), may hold values from -0.21875 to 0.21875
- masks: int32 [8, 4, 4], P('slab'), may hold values 0 or 1
- incident: bfloat16 [128, 8, 512, 2, 128], P('energy', 'slab'), may hold values from -3 to 3
- energy_index: int32 [128], P('energy'), may hold values from 0 to 255
Outputs:
- wave_field: bfloat16 [128, 8, 512, 2, 128], P('energy', 'slab')
- outflow: bfloat16 [128, 8, 512, 2, 128], P('energy', 'slab')
- density: float32 [8, 512, 2, 512], P('slab', 'energy')
All inputs are finite; a program needn't handle non-finite values. No bound on the sum of `masks` on one device may be relied on, other than what follows from the above.
Results may differ from a plain program's by a relative error of at most 0.027.
Values may be sent and summed in bfloat16 or wider, within the bound.
No kernel may reach another device: no remote copies, remote signals or barrier semaphores. Data moves between devices by JAX's collectives and lax.ppermute only.
A program may use at most 64 MiB of HBM per device.

v0:
```python
import jax
import jax.numpy as jnp
from jax import lax
from jax.sharding import PartitionSpec as P


def shifted(block, axis, distance):
    devices = range(lax.axis_size(axis))
    route = [(i - distance, i) for i in devices if i - distance in devices]
    return lax.ppermute(block, axis, route)


def apply_green(green_block, vector):
    orbitals = green_block.shape[1]
    mode_count = vector.shape[2]
    product = jnp.dot(
        green_block.reshape(2 * orbitals, orbitals),
        vector.reshape(orbitals, 2 * mode_count),
        preferred_element_type=jnp.float32,
    )
    product = product.reshape(2, orbitals, 2, mode_count)
    real_part = product[0, :, 0] - product[1, :, 1]
    imag_part = product[0, :, 1] + product[1, :, 0]
    return jnp.stack([real_part, imag_part], axis=1).astype(jnp.bfloat16)


def couple_forward(matrix, vector):
    orbitals = vector.shape[0]
    product = jnp.dot(matrix, vector.reshape(orbitals, -1), preferred_element_type=jnp.float32)
    return product.reshape(vector.shape)


def couple_back(matrix, vector):
    orbitals = vector.shape[0]
    product = lax.dot_general(
        matrix,
        vector.reshape(orbitals, -1),
        (((0,), (0,)), ((), ())),
        preferred_element_type=jnp.float32,
    )
    return product.reshape(vector.shape)


def relax(green_block, source_here, left_term, matrix, right_wave):
    summed = (
        source_here.astype(jnp.float32)
        + left_term.astype(jnp.float32)
        + couple_forward(matrix, right_wave)
    )
    return apply_green(green_block, summed.astype(jnp.bfloat16))


def fermi(index_values, scale):
    exponent = (index_values.astype(jnp.float32) - 128.0) / 24.0
    return scale / (1.0 + jnp.exp(exponent))


def shards(green_local, coupling, masks, incident, energy_index):
    count_here = green_local.shape[0]
    orbitals = green_local.shape[3]
    mode_count = incident.shape[4]
    slab_count = lax.axis_size("slab")
    place_here = lax.axis_index("slab")
    energy_devices = lax.axis_size("energy")
    whole_rows = lax.all_gather(coupling, "energy", axis=1, tiled=True)[0]
    tile_size = orbitals // masks.shape[1]
    opened = jnp.repeat(jnp.repeat(masks[0], tile_size, axis=0), tile_size, axis=1)
    coupled = whole_rows * opened.astype(jnp.bfloat16)
    green_here = green_local[:, 0]
    source = incident[:, 0]
    first_waves = jax.vmap(apply_green)(green_here, source)
    right_start = shifted(first_waves, "slab", -1)
    step_count = slab_count * count_here

    def pick(step_index, position):
        energy = step_index // slab_count
        active = step_index % slab_count == position
        return (jnp.clip(energy, 0, count_here - 1), active)

    zero_wave = jnp.zeros((orbitals, 2, mode_count), jnp.bfloat16)
    left_terms = jnp.zeros((count_here, orbitals, 2, mode_count), jnp.bfloat16)

    def forward_step(step_index, loop_state):
        arrived = shifted(loop_state[0], "slab", 1)
        energy, active = pick(step_index, place_here)

        def forward_update(old_state):
            relaxed = relax(
                green_here[energy], source[energy], arrived, coupled, right_start[energy]
            )
            new_flux = couple_back(coupled, relaxed).astype(jnp.bfloat16)
            return (new_flux, old_state[1].at[energy].set(arrived))

        return lax.cond(active, forward_update, lambda old_state: old_state, loop_state)

    forward_state = lax.fori_loop(0, step_count, forward_step, (zero_wave, left_terms))
    left_terms = forward_state[1]
    wave_init = jnp.zeros((count_here, orbitals, 2, mode_count), jnp.bfloat16)

    def backward_step(step_index, loop_state):
        arrived = shifted(loop_state[0], "slab", -1)
        energy, active = pick(step_index, slab_count - 1 - place_here)

        def backward_update(old_state):
            relaxed = relax(
                green_here[energy], source[energy], left_terms[energy], coupled, arrived
            )
            return (relaxed, old_state[1].at[energy].set(relaxed))

        return lax.cond(active, backward_update, lambda old_state: old_state, loop_state)

    backward_state = lax.fori_loop(0, step_count, backward_step, (zero_wave, wave_init))
    wave_field = backward_state[1]
    outflow = jnp.einsum(
        "rc,erpk->ecpk", coupled, wave_field, preferred_element_type=jnp.float32
    ).astype(jnp.bfloat16)
    weights = fermi(energy_index, 4.0 / (count_here * energy_devices * mode_count))
    scaled = (wave_field.astype(jnp.float32) * weights[:, None, None, None]).astype(jnp.bfloat16)
    left_side = scaled.transpose(1, 0, 2, 3).reshape(orbitals, -1)
    right_real = wave_field.transpose(1, 0, 2, 3).reshape(orbitals, -1)
    right_imag = (
        jnp.stack([-wave_field[:, :, 1], wave_field[:, :, 0]], axis=2)
        .transpose(1, 0, 2, 3)
        .reshape(orbitals, -1)
    )
    real_part = lax.dot_general(
        left_side, right_real, (((1,), (1,)), ((), ())), preferred_element_type=jnp.float32
    )
    imag_part = lax.dot_general(
        left_side, right_imag, (((1,), (1,)), ((), ())), preferred_element_type=jnp.float32
    )
    density = lax.psum_scatter(
        jnp.stack([real_part, imag_part], axis=1), "energy", scatter_dimension=0, tiled=True
    )
    return (wave_field[:, None], outflow[:, None], density[None])


def solution(mesh):
    return jax.shard_map(
        shards,
        mesh=mesh,
        in_specs=(
            P("energy", "slab", None, None, None),
            P("slab", "energy", None),
            P("slab", None, None),
            P("energy", "slab", None, None, None),
            P("energy"),
        ),
        out_specs=(
            P("energy", "slab", None, None, None),
            P("energy", "slab", None, None, None),
            P("slab", "energy", None, None),
        ),
        check_vma=False,
    )
```

profile of v0, /device:TPU:8, one launch (start us, length us, event | category | flops | bytes accessed | tf_op | source)
XLA Modules:
  0.0 983.6 jit_solution(4490819426511844188)
XLA Ops:
  8.6 3.6 fusion.49
  12.2 2.3 reshape.325
  18.8 231.7 %all_gather.3 = bf16[1,512,512]{2,1,0:T(8,128)(2,1)S(1)} all-gather(bf16[1,8,512]{2,1,0:T(8,128)(2,1)S(1)} %copy-done.4), channel_id=1, replica_groups=mesh['energy'=64,'slab'=8] {'energy'}, dimensions={1}, use_global_device_ids=true | all-gather | bytes 532480 | tf_op jit(solution)/shard_map/all_gather | solution.py:65
  251.8 135.2 %while.36 = (s32[]{:T(128)}, bf16[512,2,128]{0,2,1:T(8,128)(2,1)S(1)}, bf16[2,512,2,128]{1,3,2,0:T(8,128)(2,1)S(1)}, s32[]{:T(128)}, bf16[2,2,512,512]{3,2,1,0:T...) while((s32[]{:T(128)}, ...), condition=%wide.region_4.5_spmd, body=%wide.region_0.4_spmd.sunk | while | flops 538181632 | bytes 9700913 | solution.py:96
  253.8 5.8 collective-permute-done
  261.4 5.8 collective-permute-done
  269.1 7.6 collective-permute-done
  276.7 4.3 conditional.4
  282.9 5.8 collective-permute-done
  290.6 5.7 collective-permute-done
  298.3 5.8 collective-permute-done
  304.1 3.8 collective-permute-start
  307.8 3.9 collective-permute-done
  311.7 3.8 collective-permute-start
  315.5 3.9 collective-permute-done
  319.4 3.8 collective-permute-start
  323.2 3.9 collective-permute-done
  327.1 3.8 collective-permute-start
  330.9 3.9 collective-permute-done
  334.8 3.8 collective-permute-start
  338.6 5.7 collective-permute-done
  344.3 4.3 conditional.4
  350.5 5.8 collective-permute-done
  358.2 5.7 collective-permute-done
  365.9 5.8 collective-permute-done
  371.6 3.8 collective-permute-start
  375.4 3.9 collective-permute-done
  379.3 3.8 collective-permute-start
  383.1 3.9 collective-permute-done
  387.1 150.1 %while.37 = (s32[]{:T(128)}, bf16[512,2,128]{2,0,1:T(8,128)(2,1)S(1)}, bf16[2,512,2,128]{3,1,2,0:T(8,128)(2,1)S(1)}, s32[]{:T(128)}, bf16[2,2,512,512]{3,2,1,0:T...) while((s32[]{:T(128)}, ...), condition=%wide.region_9.10_spmd, body=%wide.region_5.9_spmd.sunk | while | flops 404357152 | bytes 8652361 | solution.py:112
  389.2 3.9 collective-permute-done.1
  393.2 3.8 collective-permute-start.1
  397.0 3.9 collective-permute-done.1
  401.1 3.8 collective-permute-start.1
  404.9 3.9 collective-permute-done.1
  408.9 3.8 collective-permute-start.1
  412.7 3.9 collective-permute-done.1
  416.7 3.8 collective-permute-start.1
  420.6 3.9 collective-permute-done.1
  424.6 3.8 collective-permute-start.1
  428.4 16.8 %collective-permute-done.1 = bf16[512,2,128]{0,2,1:T(8,128)(2,1)S(1)} collective-permute-done((bf16[512,2,128]{0,2,1:T(8,128)(2,1)S(1)}, bf16[512,2,128]{0,2,1:T(8,128)(2,1)S(1)}, u32[]{:S(2)}, u32[]{:S(2)}) %collective-permute-start.1) | collective-permute-done | bytes 262176 | tf_op jit(solution)/shard_map/while/body/eval_jaxpr/ppermute | solution.py:10
  445.3 4.3 conditional.5
  446.0 2.0 fusion.20
  451.7 3.9 collective-permute-done.1
  455.7 8.1 collective-permute-start.1
  463.8 3.9 collective-permute-done.1
  467.8 3.8 collective-permute-start.1
  471.7 3.9 collective-permute-done.1
  475.7 3.8 collective-permute-start.1
  479.5 3.9 collective-permute-done.1
  483.5 3.8 collective-permute-start.1
  487.4 3.9 collective-permute-done.1
  491.4 3.8 collective-permute-start.1
  495.2 3.9 collective-permute-done.1
  499.2 3.8 collective-permute-start.1
  503.0 3.9 collective-permute-done.1
  507.0 3.8 collective-permute-start.1
  510.9 3.9 collective-permute-done.1
  514.7 4.3 conditional.5
  515.4 2.0 fusion.20
  521.1 3.9 collective-permute-done.1
  525.2 8.1 collective-permute-start.1
  533.3 3.9 collective-permute-done.1
  542.7 432.6 %reduce-scatter.2.cloned.1.call-done = f32[8,2,512]{2,0,1:T(8,128)} async-done(((f32[512,2,512]{2,0,1:T(8,128)}), f32[8,2,512]{2,0,1:T(8,128)}) %reduce-scatter.2.cloned.1.call-update) | async-done | bytes 32784 | tf_op jit(solution)/shard_map/reduce_scatter | solution.py:132
  (127 shorter events, 52.1 us)
Async XLA Ops:
  7.2 968.2 %reduce-scatter.2.cloned.1.call-start = ((), (), s32[]{:S(2)}) async-start(), calls=%async_computation.1 | async-start | bytes 2129920 | tf_op jit(solution)/shard_map/reduce_scatter | solution.py:132
  16.2 2.2 copy-start.5
  16.2 2.2 copy-start.6
  16.2 2.2 copy-start.1
  16.2 2.6 copy-start.4
  16.4 234.8 %collective-permute-start.2 = (bf16[2,512,2,128]{3,1,0,2:T(8,128)(2,1)S(1)}, bf16[2,512,2,128]{3,1,0,2:T(8,128)(2,1)S(1)}, u32[]{:S(2)}, u32[]{:S(2)}) collective-permute-start(bf16[2,512,2,128]{3,1,0,2:T(8,128)(2,1)S(1)} %pad_maximum_fusion.3), channel_id=1, source_target_pairs={{1,0},{2,1},{3,2},{4,3},{5,4},{6,5},{7,6},{9,8},{10,9},{11,10},{12... | collective-permute-start | bytes 1572872 | tf_op jit(solution)/shard_map/ppermute | solution.py:10
  251.8 7.7 collective-permute-start
  259.5 7.7 collective-permute-start
  267.2 9.5 collective-permute-start
  279.0 0.7 copy-start.2
  281.0 7.7 collective-permute-start
  288.7 7.7 collective-permute-start
  296.4 7.7 collective-permute-start
  304.1 7.7 collective-permute-start
  311.7 7.7 collective-permute-start
  319.4 7.7 collective-permute-start
  327.1 7.7 collective-permute-start
  334.8 9.5 collective-permute-start
  346.5 0.7 copy-start.2
  348.6 7.7 collective-permute-start
  356.3 7.7 collective-permute-start
  363.9 7.7 collective-permute-start
  371.6 7.7 collective-permute-start
  379.3 7.7 collective-permute-start
  387.3 5.8 collective-permute-start.1
  393.2 7.7 collective-permute-start.1
  401.1 7.7 collective-permute-start.1
  408.9 7.7 collective-permute-start.1
  416.7 7.7 collective-permute-start.1
  424.6 20.7 %collective-permute-start.1 = (bf16[512,2,128]{0,2,1:T(8,128)(2,1)S(1)}, bf16[512,2,128]{0,2,1:T(8,128)(2,1)S(1)}, u32[]{:S(2)}, u32[]{:S(2)}) collective-permute-start(bf16[512,2,128]{0,2,1:T(8,128)(2,1)S(1)} %copy.53), channel_id=1, source_target_pairs={{1,0},{2,1},{3,2},{4,3},{5,4},{6,5},{7,6},{9,8},{10,9},{11,10},{12... | collective-permute-start | bytes 786440 | tf_op jit(solution)/shard_map/while/body/eval_jaxpr/ppermute | solution.py:10
  445.3 0.7 copy-start
  446.0 2.1 copy-start.3
  449.7 5.8 collective-permute-start.1
  455.7 12.0 %collective-permute-start.1 = (bf16[512,2,128]{0,2,1:T(8,128)(2,1)S(1)}, bf16[512,2,128]{0,2,1:T(8,128)(2,1)S(1)}, u32[]{:S(2)}, u32[]{:S(2)}) collective-permute-start(bf16[512,2,128]{0,2,1:T(8,128)(2,1)S(1)} %copy.53), channel_id=1, source_target_pairs={{1,0},{2,1},{3,2},{4,3},{5,4},{6,5},{7,6},{9,8},{10,9},{11,10},{12... | collective-permute-start | bytes 786440 | tf_op jit(solution)/shard_map/while/body/eval_jaxpr/ppermute | solution.py:10
  467.8 7.7 collective-permute-start.1
  475.7 7.7 collective-permute-start.1
  483.5 7.7 collective-permute-start.1
  491.4 7.7 collective-permute-start.1
  499.2 7.7 collective-permute-start.1
  507.0 7.7 collective-permute-start.1
  514.7 0.7 copy-start
  515.4 2.1 copy-start.3
  519.2 5.8 collective-permute-start.1
  525.2 12.0 %collective-permute-start.1 = (bf16[512,2,128]{0,2,1:T(8,128)(2,1)S(1)}, bf16[512,2,128]{0,2,1:T(8,128)(2,1)S(1)}, u32[]{:S(2)}, u32[]{:S(2)}) collective-permute-start(bf16[512,2,128]{0,2,1:T(8,128)(2,1)S(1)} %copy.53), channel_id=1, source_target_pairs={{1,0},{2,1},{3,2},{4,3},{5,4},{6,5},{7,6},{9,8},{10,9},{11,10},{12... | collective-permute-start | bytes 786440 | tf_op jit(solution)/shard_map/while/body/eval_jaxpr/ppermute | solution.py:10
Sparse Core Ops, SparseCore 0:
  539.9 435.3 reduce-scatter.1
where the time goes:
time: 985 us; the launch traced here: 984 us
  waiting for transfers between devices  590 us (60%)
  blocking collectives  232 us (24%)
  starting transfers between devices  110 us (11%)
  local copies, waits for them, and re-layouts  15.4 us (2%)
  between operations  14.2 us (1%)
  matrix products  13.8 us (1%)
    reduce_scatter x1, waiting for transfers between devices, shards(): lax.psum_scatter(jnp.stack([real_part, imag_part], axis=1), 'energy', sca...  433 us
    all_gather x1, blocking collectives, shards(): whole_rows = lax.all_gather(coupling, 'energy', axis=1, tiled=True)[0]  232 us
    ppermute x33, waiting for transfers between devices, shifted(): return lax.ppermute(block, axis, route)  157 us
    ppermute x33, starting transfers between devices, shifted(): return lax.ppermute(block, axis, route)  110 us
  transfers between devices with their start and end apart: 34, of which 33 were waited for; matrix products, arithmetic and copies ran while one was open for 0% of the time, Pallas kernels for 0%

commit v1 on v0

v1 whole, which is shorter than its diff:
```python
import jax
import jax.numpy as jnp
from jax import lax
from jax.sharding import PartitionSpec as P

BF16 = jnp.bfloat16
F32 = jnp.float32


def chip_hop(block, distance):
    size = lax.axis_size("slab")
    route = [(i, i + 2 * distance) for i in range(size) if 0 <= i + 2 * distance < size]
    return lax.ppermute(block, "slab", route)


def chip_swap(block):
    size = lax.axis_size("slab")
    pairs = [[i, i + 1] for i in range(0, size, 2)]
    return lax.all_to_all(block, "slab", 0, 0, axis_index_groups=pairs, tiled=True)


def mul(left, right, dims=((1,), (0,))):
    return lax.dot_general(left, right, (dims, ((), ())), preferred_element_type=F32)


def complex_apply(matrix, vector):
    n = matrix.shape[1]
    k = vector.shape[1] // 2
    product = mul(matrix.reshape(2 * n, -1), vector)
    real = product[:n, :k] - product[n:, k:]
    imag = product[:n, k:] + product[n:, :k]
    return jnp.concatenate([real, imag], axis=1)


def complex_product(left, right):
    n = left.shape[1]
    stacked = left.reshape(2 * n, -1)
    pr = mul(stacked, right[0])
    pi = mul(stacked, right[1])
    return jnp.stack([pr[:n] - pi[n:], pi[:n] + pr[n:]]).astype(BF16)


def transposed_times(coupled, matrix):
    return jnp.stack([mul(coupled, matrix[0], ((0,), (0,))), mul(coupled, matrix[1], ((0,), (0,)))]).astype(BF16)


def times(matrix, coupled):
    n = matrix.shape[1]
    return mul(matrix.reshape(2 * n, n), coupled).reshape(2, n, n).astype(BF16)


def fermi(index_values, scale):
    exponent = (index_values.astype(F32) - 128.0) / 24.0
    return scale / (1.0 + jnp.exp(exponent))


def shards(green_local, coupling, masks, incident, energy_index):
    count = green_local.shape[0]
    n = green_local.shape[3]
    modes = incident.shape[4]
    devices = lax.axis_size("energy")
    rows = coupling.shape[1]
    tile = n // masks.shape[1]

    by_row = jnp.repeat(masks[0].astype(BF16), tile, axis=0)
    here = lax.dynamic_slice_in_dim(by_row, lax.axis_index("energy") * rows, rows, 0)
    mine = coupling[0] * jnp.repeat(here, tile, axis=1)
    whole = lax.all_to_all(jnp.tile(mine, (devices, 1)), "energy", 0, 0, tiled=True)

    green = chip_swap(green_local[:, 0])
    source = chip_swap(incident[:, 0].reshape(count, n, 2 * modes))
    green_a, green_b = green[0], green[1]
    source_a, source_b = source[0], source[1]
    first_a = complex_apply(green_a, source_a).astype(BF16)
    first_b = complex_apply(green_b, source_b).astype(BF16)
    first_next = chip_hop(first_a, -1)

    size = lax.axis_size("slab")
    pairs = [[i, i + 1] for i in range(0, size, 2)]
    both = lax.all_gather(whole, "slab", axis=0, axis_index_groups=pairs)
    c_a, c_b = both[0], both[1]

    base_a = source_a.astype(F32) + mul(c_a, first_b)
    base_b = source_b.astype(F32) + mul(c_b, first_next)
    step_a = transposed_times(c_a, green_a)
    step_b = transposed_times(c_b, green_b)
    passed = complex_apply(step_a, base_a.astype(BF16))
    start = complex_apply(step_b, (base_b + passed).astype(BF16))
    flux = chip_hop(start.astype(BF16), 1)
    through = complex_product(step_b, step_a)
    for _ in range(size // 2 - 2):
        flux = chip_hop((start + complex_apply(through, flux)).astype(BF16), 1)

    flux_a = complex_apply(step_a, (base_a + flux.astype(F32)).astype(BF16)).astype(BF16)
    left_a = source_a.astype(F32) + flux.astype(F32)
    left_b = source_b.astype(F32) + flux_a.astype(F32)
    back_a = times(green_a, c_a)
    back_b = times(green_b, c_b)
    back = complex_product(back_a, back_b)
    wave_b = complex_apply(green_b, left_b.astype(BF16)).astype(BF16)
    start = complex_apply(green_a, (left_a + mul(c_a, wave_b)).astype(BF16))
    wave_in = chip_hop(start.astype(BF16), -1)
    for _ in range(size // 2 - 2):
        wave_in = chip_hop((start + complex_apply(back, wave_in)).astype(BF16), -1)
    wave_b = complex_apply(green_b, (left_b + mul(c_b, wave_in)).astype(BF16)).astype(BF16)
    wave_a = complex_apply(green_a, (left_a + mul(c_a, wave_b)).astype(BF16)).astype(BF16)

    wave = chip_swap(jnp.stack([wave_a, wave_b]))
    weights = fermi(energy_index, 4.0 / (count * devices * modes))
    scaled = (wave.astype(F32) * weights[:, None, None]).astype(BF16)
    real = sum(mul(scaled[e], wave[e], ((1,), (1,))) for e in range(count))
    turned = jnp.concatenate([-wave[:, :, modes:], wave[:, :, :modes]], axis=2)
    imag = sum(mul(scaled[e], turned[e], ((1,), (1,))) for e in range(count))
    partial = jnp.concatenate([real, imag], axis=1).astype(BF16)
    parts = lax.all_to_all(partial, "energy", 0, 0, tiled=True).reshape(devices, n // devices, 2 * n)
    density = jnp.sum(parts.astype(F32), axis=0).reshape(1, n // devices, 2, n)

    own = whole
    outflow = jnp.stack([mul(own, wave[e], ((0,), (0,))) for e in range(count)]).astype(BF16)
    shape = (count, 1, n, 2, modes)
    return (wave.reshape(shape), outflow.reshape(shape), density)


def solution(mesh):
    return jax.shard_map(
        shards,
        mesh=mesh,
        in_specs=(
            P("energy", "slab", None, None, None),
            P("slab", "energy", None),
            P("slab", None, None),
            P("energy", "slab", None, None, None),
            P("energy"),
        ),
        out_specs=(
            P("energy", "slab", None, None, None),
            P("energy", "slab", None, None, None),
            P("slab", "energy", None, None),
        ),
        check_vma=False,
    )
```

time: 985 us -> 220 us (0.22)
  the two profiles are of different devices: /device:TPU:8 before, /device:TPU:14 now
where the time goes in v1:
time: 220 us; the launch traced here: 219 us
  waiting for transfers between devices  85.5 us (39%)
  starting transfers between devices  59.1 us (27%)
  matrix products  33.8 us (15%)
  between operations  14.7 us (7%)
  other arithmetic  12.5 us (6%)
  local copies, waits for them, and re-layouts  9.14 us (4%)
  blocking collectives  4.15 us (2%)
    dot_general x30, matrix products, mul(): lax.dot_general(left, right, (dims, ((), ())), preferred_element_type=F32)  33.8 us
    all_to_all x1, waiting for transfers between devices, shards(): lax.all_to_all(partial, 'energy', 0, 0, tiled=True)  28.9 us
    ppermute x7, waiting for transfers between devices, chip_hop(): return lax.ppermute(block, 'slab', route)  26.1 us
    all_to_all x1, waiting for transfers between devices, shards(): lax.all_to_all(jnp.tile(mine, (devices, 1)), 'energy', 0, 0, tiled=True)  20.2 us
    all_to_all x1, starting transfers between devices, shards(): lax.all_to_all(jnp.tile(mine, (devices, 1)), 'energy', 0, 0, tiled=True)  18.4 us
    ppermute x7, starting transfers between devices, chip_hop(): return lax.ppermute(block, 'slab', route)  18.3 us
    all_to_all x1, starting transfers between devices, shards(): lax.all_to_all(partial, 'energy', 0, 0, tiled=True)  14.9 us
    all_to_all x2, starting transfers between devices, chip_swap(): lax.all_to_all(block, 'slab', 0, 0, axis_index_groups=pairs, tiled=True)  7.4 us
  transfers between devices with their start and end apart: 12, of which 11 were waited for; matrix products, arithmetic and copies ran while one was open for 14% of the time, Pallas kernels for 0%

profile of v1, /device:TPU:14, one launch (start us, length us, event | category | flops | bytes accessed | tf_op | source)
XLA Modules:
  0.0 218.8 jit_solution(6228510612812487007)
XLA Ops:
  7.2 3.9 %all-to-all-start.2 = ((bf16[2,2,512,512]{3,2,1,0:T(8,128)(2,1)}), bf16[2,2,512,512]{3,2,1,0:T(8,128)(2,1)S(1)}, u32[]{:S(2)}, u32[]{:S(2)}) async-start(bf16[2,2,512,512]{3,2,1,0:T(8,128)(2,1)} %bitcast.207), calls=%async_computation.2 | async-start | bytes 4194304 | tf_op jit(solution)/shard_map/all_to_all | solution.py:19
  11.5 2.5 %all-to-all-done.2 = bf16[2,2,512,512]{3,2,1,0:T(8,128)(2,1)S(1)} async-done(((bf16[2,2,512,512]{3,2,1,0:T(8,128)(2,1)}), bf16[2,2,512,512]{3,2,1,0:T(8,128)(2,1)S(1)}, u32[]{:S(2)}, u32[]{:S(2)}) %all-to-all-start.2) | async-done | bytes 2097184 | tf_op jit(solution)/shard_map/all_to_all | solution.py:19
  14.0 0.9 tile.2
  14.9 18.4 %all-to-all-start.1 = ((bf16[64,8,512]{2,1,0:T(8,128)(2,1)}), bf16[64,8,512]{2,1,0:T(8,128)(2,1)}, u32[]{:S(2)}, u32[]{:S(2)}) async-start(bf16[64,8,512]{2,1,0:T(8,128)(2,1)} %tile.2), calls=%async_computation.1 | async-start | bytes 1048576 | tf_op jit(solution)/shard_map/all_to_all | solution.py:68
  33.3 1.1 reshape_squeeze.6
  34.4 1.7 fusion.113
  36.2 20.2 %all-to-all-done.1 = bf16[64,8,512]{2,1,0:T(8,128)(2,1)} async-done(((bf16[64,8,512]{2,1,0:T(8,128)(2,1)}), bf16[64,8,512]{2,1,0:T(8,128)(2,1)}, u32[]{:S(2)}, u32[]{:S(2)}) %all-to-all-start.1) | async-done | bytes 524320 | tf_op jit(solution)/shard_map/all_to_all | solution.py:68
  56.4 3.5 %all-to-all-start = ((bf16[2,512,256]{2,1,0:T(8,128)(2,1)}), bf16[2,512,256]{2,1,0:T(8,128)(2,1)S(1)}, u32[]{:S(2)}, u32[]{:S(2)}) async-start(bf16[2,512,256]{2,1,0:T(8,128)(2,1)} %reshape_squeeze.6), calls=%async_computation | async-start | bytes 1048576 | tf_op jit(solution)/shard_map/all_to_all | solution.py:19
  59.9 0.7 all-gather.2.cloned.1.call-update
  60.6 1.0 all-to-all-done
  61.6 0.5 fusion.94
  62.1 0.7 pad_maximum_fusion.7
  62.9 1.9 collective-permute-start
  64.8 0.5 fusion.89
  65.4 6.2 %all-gather.2.cloned.1.call-done = bf16[2,512,512]{2,1,0:T(8,128)(2,1)} async-done(((bf16[1,512,512]{2,1,0:T(8,128)(2,1)}), bf16[2,512,512]{2,1,0:T(8,128)(2,1)}) %all-gather.2.cloned.1.call-update) | async-done | bytes 1048592 | tf_op jit(solution)/shard_map/all_gather | solution.py:80
  71.6 1.7 convolution_bitcast_fusion.4
  73.4 1.6 convolution_bitcast_fusion.5
  75.2 0.5 convolution_bitcast_fusion.6
  75.6 0.5 convolution_bitcast_fusion.7
  76.2 2.0 fusion.27
  78.2 2.1 fusion.28
  80.6 0.4 fusion.92
  81.1 0.8 slice_subtract_fusion.12
  81.9 3.2 %fusion.12 = f32[1024,256]{1,0:T(8,128)} fusion(bf16[1024,512]{1,0:T(8,128)(2,1)S(1)} %bitcast.192, bf16[512,256]{0,1:T(8,128)(2,1)} %collective-permute-done, f32[512,128]{1,0:T(8,128)} %get-tuple-element.39, f32[512,128]{1,0:T(8,128)S(1)} %get-tuple-element.38, bf16[2,512,512]{2,1,0:T(8,128)(2,1)} %all-gather.2.cloned.1.call-done, ...), kind=kOutput, calls=%fused_computation.34 | convolution fusion | flops 403308544 | bytes 3670016 | tf_op jit(solution)/shard_map/dot_general | solution.py:23
  85.0 1.4 slice_subtract_fusion.11
  86.5 3.4 %collective-permute-start.1 = (bf16[512,256]{1,0:T(8,128)(2,1)S(1)}, bf16[512,256]{1,0:T(8,128)(2,1)S(1)}, u32[]{:S(2)}, u32[]{:S(2)}) collective-permute-start(bf16[512,256]{1,0:T(8,128)(2,1)S(1)} %fusion.40), channel_id=1, source_target_pairs={{0,2},{1,3},{2,4},{3,5},{4,6},{5,7},{8,10},{9,11},{10,12},{11,13},... | collective-permute-start | bytes 786440 | tf_op jit(solution)/shard_map/ppermute | solution.py:13
  89.9 1.9 fusion.19
  91.9 1.1 copy-done.1
  93.3 0.8 fusion
  94.1 0.8 convolution_convert_fusion.1
  94.9 2.0 collective-permute-done.1
  97.5 3.4 %collective-permute-start.2 = (bf16[512,256]{1,0:T(8,128)(2,1)S(1)}, bf16[512,256]{1,0:T(8,128)(2,1)S(1)}, u32[]{:S(2)}, u32[]{:S(2)}) collective-permute-start(bf16[512,256]{1,0:T(8,128)(2,1)S(1)} %fusion.32), channel_id=1, source_target_pairs={{0,2},{1,3},{2,4},{3,5},{4,6},{5,7},{8,10},{9,11},{10,12},{11,13},... | collective-permute-start | bytes 786440 | tf_op jit(solution)/shard_map/ppermute | solution.py:13
  100.9 2.1 fusion.25
  103.0 4.1 %collective-permute-done.2 = bf16[512,256]{1,0:T(8,128)(2,1)S(1)} collective-permute-done((bf16[512,256]{1,0:T(8,128)(2,1)S(1)}, bf16[512,256]{1,0:T(8,128)(2,1)S(1)}, u32[]{:S(2)}, u32[]{:S(2)}) %collective-permute-start.2) | collective-permute-done | bytes 262176 | tf_op jit(solution)/shard_map/ppermute | solution.py:13
  107.1 0.4 fusion.117
  107.6 3.7 %collective-permute-start.3 = (bf16[512,256]{1,0:T(8,128)(2,1)S(1)}, bf16[512,256]{1,0:T(8,128)(2,1)S(1)}, u32[]{:S(2)}, u32[]{:S(2)}) collective-permute-start(bf16[512,256]{1,0:T(8,128)(2,1)S(1)} %fusion.33), channel_id=1, source_target_pairs={{0,2},{1,3},{2,4},{3,5},{4,6},{5,7},{8,10},{9,11},{10,12},{11,13},... | collective-permute-start | bytes 786440 | tf_op jit(solution)/shard_map/ppermute | solution.py:13
  111.3 2.1 fusion.23
  113.4 3.0 %collective-permute-done.3 = bf16[512,256]{1,0:T(8,128)(2,1)S(1)} collective-permute-done((bf16[512,256]{1,0:T(8,128)(2,1)S(1)}, bf16[512,256]{1,0:T(8,128)(2,1)S(1)}, u32[]{:S(2)}, u32[]{:S(2)}) %collective-permute-start.3) | collective-permute-done | bytes 262176 | tf_op jit(solution)/shard_map/ppermute | solution.py:13
  116.4 0.4 fusion.47
  117.0 0.5 convolution_bitcast_fusion.3
  117.6 0.5 copy-done.5
  118.1 3.0 %convolution_bitcast_fusion.2 = f32[1024,256]{0,1:T(8,128)} fusion(bf16[1024,512]{1,0:T(8,128)(2,1)S(1)} %bitcast.197, bf16[512,256]{1,0:T(8,128)(2,1)S(1)} %collective-permute-done.3, bf16[512,128]{0,1:T(8,128)(2,1)S(1)} %get-tuple-element.29, bf16[512,128]{0,1:T(8,128)(2,1)S(1)} %get-tuple-element.28, ...), kind=kOutput, calls=%fused_computation.7 | convolution fusion | flops 403832832 | bytes 3407872 | tf_op jit(solution)/shard_map/dot_general | solution.py:23
  121.1 1.4 slice_subtract_fusion.6
  122.5 1.9 collective-permute-start.4
  124.5 1.9 fusion.21
  126.5 4.3 %collective-permute-done.4 = bf16[512,256]{0,1:T(8,128)(2,1)S(1)} collective-permute-done((bf16[512,256]{0,1:T(8,128)(2,1)S(1)}, bf16[512,256]{0,1:T(8,128)(2,1)S(1)}, u32[]{:S(2)}, u32[]{:S(2)}) %collective-permute-start.4) | collective-permute-done | bytes 262176 | tf_op jit(solution)/shard_map/ppermute | solution.py:13
  130.8 0.5 fusion.118
  131.5 2.1 collective-permute-start.5
  133.5 6.3 %collective-permute-done.5 = bf16[512,256]{0,1:T(8,128)(2,1)S(1)} collective-permute-done((bf16[512,256]{0,1:T(8,128)(2,1)S(1)}, bf16[512,256]{0,1:T(8,128)(2,1)S(1)}, u32[]{:S(2)}, u32[]{:S(2)}) %collective-permute-start.5) | collective-permute-done | bytes 262176 | tf_op jit(solution)/shard_map/ppermute | solution.py:13
  139.9 0.5 fusion.119
  140.5 1.9 collective-permute-start.6
  142.5 6.3 %collective-permute-done.6 = bf16[512,256]{0,1:T(8,128)(2,1)S(1)} collective-permute-done((bf16[512,256]{0,1:T(8,128)(2,1)S(1)}, bf16[512,256]{0,1:T(8,128)(2,1)S(1)}, u32[]{:S(2)}, u32[]{:S(2)}) %collective-permute-start.6) | collective-permute-done | bytes 262176 | tf_op jit(solution)/shard_map/ppermute | solution.py:13
  148.8 3.0 %convolution_bitcast_fusion.1 = f32[1024,256]{0,1:T(8,128)} fusion(bf16[1024,512]{1,0:T(8,128)(2,1)S(1)} %bitcast.202, bf16[512,256]{0,1:T(8,128)(2,1)S(1)} %collective-permute-done.6, bf16[2,512,512]{2,1,0:T(8,128)(2,1)} %all-gather.2.cloned.1.call-done, bf16[512,128]{1,0:T(8,128)(2,1)S(1)} %copy-done.15, bf16[512,128]{1,0:T(8,128)(2,1)S(1)} %get-tuple-element.30, ...), kind=kOutput, calls=%fused_computation.6 | convolution fusion | flops 403701760 | bytes 3407872 | tf_op jit(solution)/shard_map/dot_general | solution.py:23
  151.8 1.3 fusion.55
  153.0 2.0 convolution_bitcast_fusion
  155.2 4.2 %all_to_all.30 = bf16[2,512,256]{1,2,0:T(8,128)(2,1)S(1)} all-to-all(bf16[2,512,256]{1,2,0:T(8,128)(2,1)S(1)} %maximum_maximum_fusion), channel_id=1, replica_groups={{0,1},{2,3},{4,5},{6,7},{8,9},{10,11},{12,13},{14,15},{16,17},{18,19},{..., dimensions={0} | all-to-all | bytes 1048576 | tf_op jit(solution)/shard_map/all_to_all | solution.py:19
  160.9 1.1 pad_maximum_fusion.2
  162.0 14.9 %all-to-all-start.4 = ((bf16[64,8,1024]{2,1,0:T(8,128)(2,1)}), bf16[64,8,1024]{2,1,0:T(8,128)(2,1)S(1)}, u32[]{:S(2)}, u32[]{:S(2)}) async-start(bf16[64,8,1024]{2,1,0:T(8,128)(2,1)} %pad_maximum_fusion.2), calls=%async_computation.4 | async-start | bytes 2097152 | tf_op jit(solution)/shard_map/all_to_all | solution.py:115
  177.0 1.4 fusion.10
  178.4 1.4 fusion.11
  179.8 1.3 copy.81
  181.2 1.1 copy.80
  182.3 28.9 %all-to-all-done.4 = bf16[64,8,1024]{2,1,0:T(8,128)(2,1)S(1)} async-done(((bf16[64,8,1024]{2,1,0:T(8,128)(2,1)}), bf16[64,8,1024]{2,1,0:T(8,128)(2,1)S(1)}, u32[]{:S(2)}, u32[]{:S(2)}) %all-to-all-start.4) | async-done | bytes 1048608 | tf_op jit(solution)/shard_map/all_to_all | solution.py:115
  211.3 0.6 reshape.231
  (78 shorter events, 4.8 us)
Async XLA Ops:
  7.2 4.0 %copy-start.18 = (s32[1,4,4]{2,1,0:T(4,128)S(1)}, s32[1,4,4]{2,1,0:T(4,128)}, u32[]{:S(2)}) copy-start(s32[1,4,4]{2,1,0:T(4,128)} %param.7) | copy-start | bytes 196
  7.2 4.2 %copy-start.17 = (bf16[1,8,512]{2,1,0:T(8,128)(2,1)S(1)}, bf16[1,8,512]{2,1,0:T(8,128)(2,1)}, u32[]{:S(2)}) copy-start(bf16[1,8,512]{2,1,0:T(8,128)(2,1)} %param.6) | copy-start | bytes 24580
  7.2 26.1 %copy-start.16 = (bf16[2,1,512,2,128]{4,3,2,1,0:T(2,128)(2,1)S(1)}, bf16[2,1,512,2,128]{4,3,2,1,0:T(2,128)(2,1)}, u32[]{:S(2)}) copy-start(bf16[2,1,512,2,128]{4,3,2,1,0:T(2,128)(2,1)} %param.8) | copy-start | bytes 1572868
  7.2 6.8 %all-to-all-start.2 = ((bf16[2,2,512,512]{3,2,1,0:T(8,128)(2,1)}), bf16[2,2,512,512]{3,2,1,0:T(8,128)(2,1)S(1)}, u32[]{:S(2)}, u32[]{:S(2)}) async-start(bf16[2,2,512,512]{3,2,1,0:T(8,128)(2,1)} %bitcast.207), calls=%async_computation.2 | async-start | bytes 4194304 | tf_op jit(solution)/shard_map/all_to_all | solution.py:19
  14.0 19.3 %copy-start.8 = (bf16[2,2,512,512]{3,2,1,0:T(8,128)(2,1)}, bf16[2,2,512,512]{3,2,1,0:T(8,128)(2,1)S(1)}, u32[]{:S(2)}) copy-start(bf16[2,2,512,512]{3,2,1,0:T(8,128)(2,1)S(1)} %all-to-all-done.2) | copy-start | bytes 6291460
  14.9 41.5 %all-to-all-start.1 = ((bf16[64,8,512]{2,1,0:T(8,128)(2,1)}), bf16[64,8,512]{2,1,0:T(8,128)(2,1)}, u32[]{:S(2)}, u32[]{:S(2)}) async-start(bf16[64,8,512]{2,1,0:T(8,128)(2,1)} %tile.2), calls=%async_computation.1 | async-start | bytes 1048576 | tf_op jit(solution)/shard_map/all_to_all | solution.py:68
  36.2 28.6 %copy-start = (bf16[1,2,512,512]{3,2,1,0:T(8,128)(2,1)}, bf16[1,2,512,512]{3,2,1,0:T(8,128)(2,1)S(1)}, u32[]{:S(2)}) copy-start(bf16[1,2,512,512]{3,2,1,0:T(8,128)(2,1)S(1)} %get-tuple-element.17) | copy-start | bytes 3145732
  56.4 5.2 %all-to-all-start = ((bf16[2,512,256]{2,1,0:T(8,128)(2,1)}), bf16[2,512,256]{2,1,0:T(8,128)(2,1)S(1)}, u32[]{:S(2)}, u32[]{:S(2)}) async-start(bf16[2,512,256]{2,1,0:T(8,128)(2,1)} %reshape_squeeze.6), calls=%async_computation | async-start | bytes 1048576 | tf_op jit(solution)/shard_map/all_to_all | solution.py:19
  59.8 11.8 %all-gather.2.cloned.1.call-start = ((), (), s32[]{:S(2)}) async-start(), calls=%async_computation.5 | async-start | bytes 1572864 | tf_op jit(solution)/shard_map/all_gather | solution.py:80
  61.6 3.2 %copy-start.2 = (bf16[2,512,256]{2,1,0:T(8,128)(2,1)}, bf16[2,512,256]{2,1,0:T(8,128)(2,1)S(1)}, u32[]{:S(2)}) copy-start(bf16[2,512,256]{2,1,0:T(8,128)(2,1)S(1)} %all-to-all-done) | copy-start | bytes 1572868
  62.9 19.0 %collective-permute-start = (bf16[512,256]{0,1:T(8,128)(2,1)}, bf16[512,256]{0,1:T(8,128)(2,1)}, u32[]{:S(2)}, u32[]{:S(2)}) collective-permute-start(bf16[512,256]{0,1:T(8,128)(2,1)} %pad_maximum_fusion.7), channel_id=1, source_target_pairs={{2,0},{3,1},{4,2},{5,3},{6,4},{7,5},{10,8},{11,9},{12,10},{13,11},... | collective-permute-start | bytes 786440 | tf_op jit(solution)/shard_map/ppermute | solution.py:13
  71.6 1.8 copy-start.10
  73.4 1.8 copy-start.9
  78.2 2.1 copy-start.3
  80.6 1.2 copy-start.12
  85.0 4.8 %copy-start.7 = (f32[1024,512]{1,0:T(8,128)S(1)}, f32[1024,512]{1,0:T(8,128)}, u32[]{:S(2)}) copy-start(f32[1024,512]{1,0:T(8,128)} %fusion.27) | copy-start | bytes 6291460
  86.5 10.4 %collective-permute-start.1 = (bf16[512,256]{1,0:T(8,128)(2,1)S(1)}, bf16[512,256]{1,0:T(8,128)(2,1)S(1)}, u32[]{:S(2)}, u32[]{:S(2)}) collective-permute-start(bf16[512,256]{1,0:T(8,128)(2,1)S(1)} %fusion.40), channel_id=1, source_target_pairs={{0,2},{1,3},{2,4},{3,5},{4,6},{5,7},{8,10},{9,11},{10,12},{11,13},... | collective-permute-start | bytes 786440 | tf_op jit(solution)/shard_map/ppermute | solution.py:13
  91.8 1.2 copy-start.1
  91.8 1.5 copy-start.11
  97.5 9.6 %collective-permute-start.2 = (bf16[512,256]{1,0:T(8,128)(2,1)S(1)}, bf16[512,256]{1,0:T(8,128)(2,1)S(1)}, u32[]{:S(2)}, u32[]{:S(2)}) collective-permute-start(bf16[512,256]{1,0:T(8,128)(2,1)S(1)} %fusion.32), channel_id=1, source_target_pairs={{0,2},{1,3},{2,4},{3,5},{4,6},{5,7},{8,10},{9,11},{10,12},{11,13},... | collective-permute-start | bytes 786440 | tf_op jit(solution)/shard_map/ppermute | solution.py:13
  107.6 8.8 %copy-start.13 = (f32[512,256]{1,0:T(8,128)S(1)}, f32[512,256]{1,0:T(8,128)}, u32[]{:S(2)}) copy-start(f32[512,256]{1,0:T(8,128)} %copy-done.12) | copy-start | bytes 1572868
  107.6 8.8 %collective-permute-start.3 = (bf16[512,256]{1,0:T(8,128)(2,1)S(1)}, bf16[512,256]{1,0:T(8,128)(2,1)S(1)}, u32[]{:S(2)}, u32[]{:S(2)}) collective-permute-start(bf16[512,256]{1,0:T(8,128)(2,1)S(1)} %fusion.33), channel_id=1, source_target_pairs={{0,2},{1,3},{2,4},{3,5},{4,6},{5,7},{8,10},{9,11},{10,12},{11,13},... | collective-permute-start | bytes 786440 | tf_op jit(solution)/shard_map/ppermute | solution.py:13
  113.4 3.5 %copy-start.4 = (bf16[2,512,256]{2,1,0:T(8,128)(2,1)S(1)}, bf16[2,512,256]{2,1,0:T(8,128)(2,1)}, u32[]{:S(2)}) copy-start(bf16[2,512,256]{2,1,0:T(8,128)(2,1)} %copy-done.2) | copy-start | bytes 1572868
  117.0 4.1 %copy-start.14 = (bf16[512,128]{1,0:T(8,128)(2,1)}, bf16[512,128]{1,0:T(8,128)(2,1)S(1)}, u32[]{:S(2)}) copy-start(bf16[512,128]{1,0:T(8,128)(2,1)S(1)} %get-tuple-element.31) | copy-start | bytes 393220
  117.0 1.1 copy-start.5
  121.0 3.4 %copy-start.6 = (f32[1024,512]{1,0:T(8,128)S(1)}, f32[1024,512]{1,0:T(8,128)}, u32[]{:S(2)}) copy-start(f32[1024,512]{1,0:T(8,128)} %fusion.25) | copy-start | bytes 6291460
  122.5 8.3 %collective-permute-start.4 = (bf16[512,256]{0,1:T(8,128)(2,1)S(1)}, bf16[512,256]{0,1:T(8,128)(2,1)S(1)}, u32[]{:S(2)}, u32[]{:S(2)}) collective-permute-start(bf16[512,256]{0,1:T(8,128)(2,1)S(1)} %fusion.39), channel_id=1, source_target_pairs={{2,0},{3,1},{4,2},{5,3},{6,4},{7,5},{10,8},{11,9},{12,10},{13,11},... | collective-permute-start | bytes 786440 | tf_op jit(solution)/shard_map/ppermute | solution.py:13
  131.4 11.0 %copy-start.19 = (s32[2]{0:T(128)S(1)}, s32[2]{0:T(128)}, u32[]{:S(2)}) copy-start(s32[2]{0:T(128)} %param.9) | copy-start | bytes 28
  131.4 17.3 %copy-start.15 = (bf16[512,128]{1,0:T(8,128)(2,1)S(1)}, bf16[512,128]{1,0:T(8,128)(2,1)}, u32[]{:S(2)}) copy-start(bf16[512,128]{1,0:T(8,128)(2,1)} %copy-done.14) | copy-start | bytes 393220
  131.5 8.4 %collective-permute-start.5 = (bf16[512,256]{0,1:T(8,128)(2,1)S(1)}, bf16[512,256]{0,1:T(8,128)(2,1)S(1)}, u32[]{:S(2)}, u32[]{:S(2)}) collective-permute-start(bf16[512,256]{0,1:T(8,128)(2,1)S(1)} %fusion.34), channel_id=1, source_target_pairs={{2,0},{3,1},{4,2},{5,3},{6,4},{7,5},{10,8},{11,9},{12,10},{13,11},... | collective-permute-start | bytes 786440 | tf_op jit(solution)/shard_map/ppermute | solution.py:13
  140.5 8.3 %collective-permute-start.6 = (bf16[512,256]{0,1:T(8,128)(2,1)S(1)}, bf16[512,256]{0,1:T(8,128)(2,1)S(1)}, u32[]{:S(2)}, u32[]{:S(2)}) collective-permute-start(bf16[512,256]{0,1:T(8,128)(2,1)S(1)} %fusion.35), channel_id=1, source_target_pairs={{2,0},{3,1},{4,2},{5,3},{6,4},{7,5},{10,8},{11,9},{12,10},{13,11},... | collective-permute-start | bytes 786440 | tf_op jit(solution)/shard_map/ppermute | solution.py:13
  162.0 49.2 %all-to-all-start.4 = ((bf16[64,8,1024]{2,1,0:T(8,128)(2,1)}), bf16[64,8,1024]{2,1,0:T(8,128)(2,1)S(1)}, u32[]{:S(2)}, u32[]{:S(2)}) async-start(bf16[64,8,1024]{2,1,0:T(8,128)(2,1)} %pad_maximum_fusion.2), calls=%async_computation.4 | async-start | bytes 2097152 | tf_op jit(solution)/shard_map/all_to_all | solution.py:115
Sparse Core Ops, SparseCore 0:
  62.8 8.7 all-gather.1

commit v2 on v1

v2 whole, which is shorter than its diff:
```python
import jax
import jax.numpy as jnp
from jax import lax
from jax.experimental import pallas as pl
from jax.experimental.pallas import tpu as pltpu
from jax.sharding import PartitionSpec as P

BF16 = jnp.bfloat16
F32 = jnp.float32


def chip_hop(block, distance):
    size = lax.axis_size("slab")
    route = [(i, i + 2 * distance) for i in range(size) if 0 <= i + 2 * distance < size]
    return lax.ppermute(block, "slab", route)


def swap(block):
    route = [(i, i ^ 1) for i in range(lax.axis_size("slab"))]
    return lax.ppermute(block, "slab", route)


def pick(blocks, index):
    return lax.dynamic_index_in_dim(blocks, index, 0, keepdims=False)


def ordered(core, kept, got):
    even = core == 0
    return jnp.stack([jnp.where(even, kept, got), jnp.where(even, got, kept)])


def exchange(block, groups):
    return lax.all_to_all(block, "energy", 0, 0, axis_index_groups=groups, tiled=True)


def energy_grid(devices):
    return (2, 2, 2) if devices == 8 else (2, 4, devices // 8)


def mul(left, right):
    return lax.dot_general(left, right, (((1,), (0,)), ((), ())), preferred_element_type=F32)


def mul_transposed(left, right):
    return lax.dot_general(left, right, (((1,), (1,)), ((), ())), preferred_element_type=F32)


def turned(vector):
    k = vector.shape[1] // 2
    return jnp.concatenate([-vector[:, k:], vector[:, :k]], axis=1)


def apply(real, imag, vector):
    return mul(real, vector) + mul(imag, turned(vector))


def product(left, right, out):
    lr, li, rr, ri = left[0], left[1], right[0], right[1]
    out[0] = (mul(lr, rr) - mul(li, ri)).astype(BF16)
    out[1] = (mul(lr, ri) + mul(li, rr)).astype(BF16)


def begin_kernel(g, c, ct, src, first, following, base, start, send):
    base_a = src[0].astype(F32) + mul(c[0], first[1])
    base[...] = base_a
    field = apply(g[0, 0], g[0, 1], base_a.astype(BF16)).astype(BF16)
    summed = src[1].astype(F32) + mul(c[1], following[...]) + mul(ct[0], field)
    field = apply(g[1, 0], g[1, 1], summed.astype(BF16)).astype(BF16)
    flux = mul(ct[1], field)
    start[...] = flux
    send[...] = flux.astype(BF16)


def compose_kernel(g, ct, step_a, through, step_b):
    step_a[0] = mul(ct[0], g[0, 0]).astype(BF16)
    step_a[1] = mul(ct[0], g[0, 1]).astype(BF16)
    step_b[0] = mul(ct[1], g[1, 0]).astype(BF16)
    step_b[1] = mul(ct[1], g[1, 1]).astype(BF16)
    product(step_b, step_a, through)


def compose_back_kernel(g, c, back, back_a, back_b):
    back_a[0] = mul(g[0, 0], c[0]).astype(BF16)
    back_a[1] = mul(g[0, 1], c[0]).astype(BF16)
    back_b[0] = mul(g[1, 0], c[1]).astype(BF16)
    back_b[1] = mul(g[1, 1], c[1]).astype(BF16)
    product(back_a, back_b, back)


def hop_kernel(matrix, start, arrived, send):
    send[...] = (start[...] + apply(matrix[0], matrix[1], arrived[...])).astype(BF16)


def turn_kernel(g, c, step_a, src, base, flux, left, start, send):
    arrived = flux[...].astype(F32)
    summed = (base[...] + arrived).astype(BF16)
    flux_a = apply(step_a[0], step_a[1], summed)
    left_a = src[0].astype(F32) + arrived
    left_b = src[1].astype(F32) + flux_a
    left[0] = left_a
    left[1] = left_b
    field = apply(g[1, 0], g[1, 1], left_b.astype(BF16)).astype(BF16)
    summed = (left_a + mul(c[0], field)).astype(BF16)
    wave = apply(g[0, 0], g[0, 1], summed)
    start[...] = wave
    send[...] = wave.astype(BF16)


def finish_kernel(core, g, c, left, arrived, keep, send):
    summed = (left[1] + mul(c[1], arrived[...])).astype(BF16)
    wave_b = apply(g[1, 0], g[1, 1], summed).astype(BF16)
    summed = (left[0] + mul(c[0], wave_b)).astype(BF16)
    wave_a = apply(g[0, 0], g[0, 1], summed).astype(BF16)

    @pl.when(core[0] == 0)
    def _():
        keep[...] = wave_a
        send[...] = wave_b

    @pl.when(core[0] != 0)
    def _():
        keep[...] = wave_b
        send[...] = wave_a


def density_kernel(core, weights, kept, got, out):
    n, _ = kept.shape
    outer, inner, rows, _ = out.shape
    here = weights[core[0]]
    there = weights[1 - core[0]]
    real = jnp.zeros((n, n), F32)
    imag = jnp.zeros((n, n), F32)
    for weight, wave in ((here, kept), (there, got)):
        w = wave[...]
        scaled = (w.astype(F32) * weight).astype(BF16)
        real = real + mul_transposed(scaled, w)
        imag = imag + mul_transposed(scaled, turned(w))
    real = real.astype(BF16)
    imag = imag.astype(BF16)
    for i in range(outer):
        for j in range(inner):
            first = (j * outer + i) * rows
            out[i, j, :, :n] = real[first : first + rows]
            out[i, j, :, n:] = imag[first : first + rows]


def call(kernel, out_shapes, *operands, scratch=(), flops=0, smem=0, limit=24):
    whole = pl.BlockSpec(memory_space=pltpu.VMEM)
    scalars = pl.BlockSpec(memory_space=pltpu.SMEM)
    outs = [pltpu.VMEM(s, d) for s, d in out_shapes]
    operands = list(operands[:smem]) + [pltpu.with_memory_space_constraint(o, pltpu.VMEM) for o in operands[smem:]]
    result = pl.pallas_call(
        kernel,
        out_shape=outs,
        in_specs=[scalars] * smem + [whole] * (len(operands) - smem),
        out_specs=[whole] * len(outs),
        scratch_shapes=[pltpu.VMEM(s, d) for s, d in scratch],
        cost_estimate=pl.CostEstimate(flops=flops, transcendentals=0, bytes_accessed=1 << 20),
        compiler_params=pltpu.CompilerParams(vmem_limit_bytes=limit << 20),
    )(*operands)
    return result if len(outs) > 1 else result[0]


def fermi(index_values, scale):
    exponent = (index_values.astype(F32) - 128.0) / 24.0
    return scale / (1.0 + jnp.exp(exponent))


def shards(green_local, coupling, masks, incident, energy_index):
    count = green_local.shape[0]
    n = green_local.shape[3]
    modes = incident.shape[4]
    cols = 2 * modes
    devices = lax.axis_size("energy")
    ny, nx, nz = energy_grid(devices)
    at = lambda y, x, z: (y * nx + x) * nz + z
    along_z = [[at(y, x, z) for z in range(nz)] for y in range(ny) for x in range(nx)]
    along_yx = [[at(y, x, z) for y in range(ny) for x in range(nx)] for z in range(nz)]
    along_x = [[at(y, x, z) for x in range(nx)] for y in range(ny) for z in range(nz)]
    along_yz = [[at(y, x, z) for y in range(ny) for z in range(nz)] for x in range(nx)]
    rows = coupling.shape[1]
    tile = n // masks.shape[1]
    vec = (n, cols)
    mat = (2, n, n)
    unit = 2 * n * n * cols

    some = exchange(jnp.tile(coupling[0], (nz, 1)), along_z)
    by_row = jnp.repeat(masks[0].astype(BF16), tile, axis=0)
    first_row = (lax.axis_index("energy") // nz) * nz * rows
    here = lax.dynamic_slice_in_dim(by_row, first_row, nz * rows, 0)
    some = some * jnp.repeat(here, tile, axis=1)

    core = lax.rem(lax.axis_index("slab"), 2)
    own = green_local[:, 0]
    green = ordered(core, pick(own, core), swap(pick(own, 1 - core)))
    own = incident[:, 0].reshape(count, n, cols)
    source = ordered(core, pick(own, core), swap(pick(own, 1 - core)))
    some, green, source = lax.optimization_barrier((jnp.tile(some, (ny * nx, 1)), green, source))
    whole = exchange(some, along_yx)
    first = jnp.stack([apply(green[s, 0], green[s, 1], source[s]) for s in range(2)]).astype(BF16)
    following = chip_hop(first[0], -1)
    c = ordered(core, whole, swap(whole))
    ct = c.transpose(0, 2, 1)

    hops = lax.axis_size("slab") // 2 - 1
    base, start, send = call(
        begin_kernel, [(vec, F32), (vec, F32), (vec, BF16)], green, c, ct, source, first, following, flops=8 * unit
    )
    flux = chip_hop(send, 1)
    step_a, through = call(
        compose_kernel, [(mat, BF16), (mat, BF16)], green, ct, scratch=[(mat, BF16)], flops=16 * n**3
    )
    for _ in range(hops - 1):
        send = call(hop_kernel, [(vec, BF16)], through, start, flux, flops=2 * unit)
        flux = chip_hop(send, 1)
    back = call(
        compose_back_kernel, [(mat, BF16)], green, c, scratch=[(mat, BF16), (mat, BF16)], flops=16 * n**3
    )
    left, start, send = call(
        turn_kernel, [((2, *vec), F32), (vec, F32), (vec, BF16)], green, c, step_a, source, base, flux, flops=7 * unit
    )
    arrived = chip_hop(send, -1)
    for _ in range(hops - 1):
        send = call(hop_kernel, [(vec, BF16)], back, start, arrived, flops=2 * unit)
        arrived = chip_hop(send, -1)
    which = core.reshape(1)
    kept, send = call(
        finish_kernel, [(vec, BF16), (vec, BF16)], which, green, c, left, arrived, smem=1, flops=6 * unit
    )

    got = swap(send)
    weights = fermi(energy_index, 4.0 / (count * devices * modes))
    partial = call(
        density_kernel, [((nx, ny, nz * rows, 2 * n), BF16)], which, weights, kept, got, smem=2, flops=8 * unit
    )
    parts = exchange(partial, along_x)
    summed = jnp.sum(parts.astype(F32), axis=0).astype(BF16)
    parts = exchange(summed.reshape(ny * nz, rows, 2 * n), along_yz)
    density = jnp.sum(parts.astype(F32), axis=0).reshape(1, rows, 2, n)

    wave = ordered(core, kept, got)
    outflow = jnp.stack([mul(whole.T, wave[e]) for e in range(count)]).astype(BF16)
    shape = (count, 1, n, 2, modes)
    return (wave.reshape(shape), outflow.reshape(shape), density)


def solution(mesh):
    return jax.shard_map(
        shards,
        mesh=mesh,
        in_specs=(
            P("energy", "slab", None, None, None),
            P("slab", "energy", None),
            P("slab", None, None),
            P("energy", "slab", None, None, None),
            P("energy"),
        ),
        out_specs=(
            P("energy", "slab", None, None, None),
            P("energy", "slab", None, None, None),
            P("slab", "energy", None, None),
        ),
        check_vma=False,
    )
```

time: 220 us -> 176 us (0.80)
  the two profiles are of different devices: /device:TPU:14 before, /device:TPU:8 now
where the time goes in v2:
time: 176 us; the launch traced here: 175 us
  waiting for transfers between devices  80.9 us (46%)
  starting transfers between devices  54 us (31%)
  Pallas kernels  15.2 us (9%)
  local copies, waits for them, and re-layouts  12.4 us (7%)
  other arithmetic  8.18 us (5%)
  matrix products  3.48 us (2%)
    all_to_all x4, waiting for transfers between devices, exchange(): lax.all_to_all(block, 'energy', 0, 0, axis_index_groups=groups, tiled=True)  46.4 us
    ppermute x7, waiting for transfers between devices, chip_hop(): return lax.ppermute(block, 'slab', route)  33 us
    all_to_all x4, starting transfers between devices, exchange(): lax.all_to_all(block, 'energy', 0, 0, axis_index_groups=groups, tiled=True)  26 us
    ppermute x7, starting transfers between devices, chip_hop(): return lax.ppermute(block, 'slab', route)  19.6 us
    pallas_call x10, Pallas kernels, call(): pl.pallas_call(kernel, out_shape=outs, in_specs=[scalars] * smem + [whole...  15.2 us
    ppermute x4, starting transfers between devices, swap(): return lax.ppermute(block, 'slab', route)  8.28 us
    unnamed x28, local copies, waits for them, and re-layouts  5.32 us
  transfers between devices with their start and end apart: 15, of which 11 were waited for; matrix products, arithmetic and copies ran while one was open for 8% of the time, Pallas kernels for 3%

profile of v2, /device:TPU:8, one launch (start us, length us, event | category | flops | bytes accessed | tf_op | source)
XLA Modules:
  0.0 175.2 jit_solution(6506443015063770082)
XLA Ops:
  0.7 2.3 %dynamic-slice_bitcast_fusion = bf16[2,512,512]{2,1,0:T(8,128)(2,1)} fusion(bf16[2,1,2,512,512]{4,3,2,1,0:T(8,128)(2,1)} %param.5, s32[]{:T(128)S(6)} %select_n.69), kind=kLoop, calls=%fused_computation.15 | loop fusion | bytes 2097156 | tf_op jit(solution)/shard_map/jit(dynamic_index_in_dim)/squeeze | solution.py:24
  3.0 2.0 %collective-permute-start = (bf16[2,512,512]{2,1,0:T(8,128)(2,1)}, bf16[2,512,512]{2,1,0:T(8,128)(2,1)}, u32[]{:S(2)}, u32[]{:S(2)}) collective-permute-start(bf16[2,512,512]{2,1,0:T(8,128)(2,1)} %dynamic-slice_bitcast_fusion), channel_id=1, source_target_pairs={{0,1},{1,0},{2,3},{3,2},{4,5},{5,4},{6,7},{7,6},{8,9},{9,8},{10,11... | collective-permute-start | bytes 3145736 | tf_op jit(solution)/shard_map/ppermute | solution.py:20
  5.0 0.3 reshape_squeeze.3
  5.4 2.4 %collective-permute-start.1 = (bf16[512,256]{1,0:T(8,128)(2,1)S(1)}, bf16[512,256]{1,0:T(8,128)(2,1)S(1)}, u32[]{:S(2)}, u32[]{:S(2)}) collective-permute-start(bf16[512,256]{1,0:T(8,128)(2,1)S(1)} %dynamic-slice_bitcast_fusion.1), channel_id=1, source_target_pairs={{0,1},{1,0},{2,3},{3,2},{4,5},{5,4},{6,7},{7,6},{8,9},{9,8},{10,11... | collective-permute-start | bytes 786440 | tf_op jit(solution)/shard_map/ppermute | solution.py:20
  7.8 0.6 tile.18
  8.5 10.3 %all-to-all-start = ((bf16[8,8,512]{2,1,0:T(8,128)(2,1)}), bf16[8,8,512]{2,1,0:T(8,128)(2,1)S(1)}, u32[]{:S(2)}, u32[]{:S(2)}) async-start(bf16[8,8,512]{2,1,0:T(8,128)(2,1)} %tile.18), calls=%async_computation | async-start | bytes 131072 | tf_op jit(solution)/shard_map/all_to_all | solution.py:33
  18.9 8.3 %all-to-all-done = bf16[8,8,512]{2,1,0:T(8,128)(2,1)S(1)} async-done(((bf16[8,8,512]{2,1,0:T(8,128)(2,1)}), bf16[8,8,512]{2,1,0:T(8,128)(2,1)S(1)}, u32[]{:S(2)}, u32[]{:S(2)}) %all-to-all-start) | async-done | bytes 65568 | tf_op jit(solution)/shard_map/all_to_all | solution.py:33
  27.2 0.1 broadcast_in_dim.7
  27.5 1.5 fusion.5
  29.0 0.2 pad_maximum_fusion.g
  29.2 0.8 tile.19
  30.1 8.7 %all-to-all-start.1 = ((bf16[8,64,512]{2,1,0:T(8,128)(2,1)}), bf16[8,64,512]{2,1,0:T(8,128)(2,1)S(1)}, u32[]{:S(2)}, u32[]{:S(2)}) async-start(bf16[8,64,512]{2,1,0:T(8,128)(2,1)} %tile.19), calls=%async_computation.1 | async-start | bytes 1048576 | tf_op jit(solution)/shard_map/all_to_all | solution.py:33
  38.8 0.7 slice_negate_fusion
  39.5 0.3 fusion.11
  39.8 1.0 fusion
  40.8 3.2 %collective-permute-start.3 = (bf16[512,256]{1,0:T(8,128)(2,1)}, bf16[512,256]{1,0:T(8,128)(2,1)S(1)}, u32[]{:S(2)}, u32[]{:S(2)}) collective-permute-start(bf16[512,256]{1,0:T(8,128)(2,1)} %fusion), channel_id=1, source_target_pairs={{2,0},{3,1},{4,2},{5,3},{6,4},{7,5},{10,8},{11,9},{12,10},{13,11},... | collective-permute-start | bytes 786440 | tf_op jit(solution)/shard_map/ppermute | solution.py:15
  44.0 11.7 %all-to-all-done.1 = bf16[8,64,512]{2,1,0:T(8,128)(2,1)S(1)} async-done(((bf16[8,64,512]{2,1,0:T(8,128)(2,1)}), bf16[8,64,512]{2,1,0:T(8,128)(2,1)S(1)}, u32[]{:S(2)}, u32[]{:S(2)}) %all-to-all-start.1) | async-done | bytes 524320 | tf_op jit(solution)/shard_map/all_to_all | solution.py:33
  55.8 1.9 %collective-permute-start.2 = (bf16[512,512]{1,0:T(8,128)(2,1)S(1)}, bf16[512,512]{1,0:T(8,128)(2,1)S(1)}, u32[]{:S(2)}, u32[]{:S(2)}) collective-permute-start(bf16[512,512]{1,0:T(8,128)(2,1)S(1)} %bitcast.85), channel_id=1, source_target_pairs={{0,1},{1,0},{2,3},{3,2},{4,5},{5,4},{6,7},{7,6},{8,9},{9,8},{10,11... | collective-permute-start | bytes 1572872 | tf_op jit(solution)/shard_map/ppermute | solution.py:20
  57.7 0.3 fusion.8
  58.0 1.2 fusion.4
  59.2 1.8 %pad_maximum_fusion.3.first = bf16[2,512,256]{2,1,0:T(8,128)(2,1)} fusion(bf16[1,512,256]{2,1,0:T(8,128)(2,1)S(1)} %fusion.4, bf16[1,512,256]{2,1,0:T(8,128)(2,1)} %bitcast.22), kind=kLoop, calls=%fused_computation.17 | loop fusion | flops 262144 | bytes 1048576 | tf_op jit(solution)/shard_map/stack | solution.py:200
  61.0 0.1 select_bitcast_fusion.1
  61.1 1.1 fusion.27
  62.2 2.3 %copy.15.ct = bf16[2,512,512]{2,1,0:T(8,128)(2,1)} copy(bf16[2,512,512]{1,2,0:T(8,128)(2,1)} %get-tuple-element.37) | data formatting | bytes 2097152 | tf_op jit(solution)/shard_map/transpose | solution.py:203
  64.5 1.0 copy-done.1
  65.5 1.2 copy-done.3
  66.8 1.0 copy-done.5
  67.8 2.2 %shard_map.77 = (f32[512,256]{1,0:T(8,128)S(1)}, f32[512,256]{1,0:T(8,128)S(1)}, bf16[512,256]{1,0:T(8,128)(2,1)S(1)}) custom-call(bf16[2,2,512,512]{3,2,1,0:T(8,128)(2,1)S(1)} %pad_maximum_fusion.g, bf16[2,512,512]{2,1,0:T(8,128)(2,1)S(1)} %get-tuple-element.38.c, bf16[2,512,512]{2,1,0:T(8,128)(2,1)S(1)} %copy-done.3, bf16[2,512,256]{2,1,0:T(8,128)(2,1)S(1)} %copy-done.1, ...), custom_call_target="tpu_custom_call" | custom-call | flops 1073741824 | bytes 1048576 | tf_op jit(solution)/shard_map/pallas_call | solution.py:152
  70.1 3.5 %collective-permute-start.4 = (bf16[512,256]{1,0:T(8,128)(2,1)S(1)}, bf16[512,256]{1,0:T(8,128)(2,1)S(1)}, u32[]{:S(2)}, u32[]{:S(2)}) collective-permute-start(bf16[512,256]{1,0:T(8,128)(2,1)S(1)} %get-tuple-element.23), channel_id=1, source_target_pairs={{0,2},{1,3},{2,4},{3,5},{4,6},{5,7},{8,10},{9,11},{10,12},{11,13},... | collective-permute-start | bytes 786440 | tf_op jit(solution)/shard_map/ppermute | solution.py:15
  73.6 2.3 %shard_map.76 = (bf16[2,512,512]{2,1,0:T(8,128)(2,1)S(1)}, bf16[2,512,512]{2,1,0:T(8,128)(2,1)S(1)}) custom-call(bf16[2,2,512,512]{3,2,1,0:T(8,128)(2,1)S(1)} %pad_maximum_fusion.g, bf16[2,512,512]{2,1,0:T(8,128)(2,1)S(1)} %copy-done.4), custom_call_target="tpu_custom_call" | custom-call | flops 2147483648 | bytes 1048576 | tf_op jit(solution)/shard_map/pallas_call | solution.py:152
  76.0 4.7 %collective-permute-done.4.arrived = bf16[512,256]{1,0:T(8,128)(2,1)S(1)} collective-permute-done((bf16[512,256]{1,0:T(8,128)(2,1)S(1)}, bf16[512,256]{1,0:T(8,128)(2,1)S(1)}, u32[]{:S(2)}, u32[]{:S(2)}) %collective-permute-start.4) | collective-permute-done | bytes 262176 | tf_op jit(solution)/shard_map/ppermute | solution.py:15
  80.7 0.4 shard_map.78
  81.1 3.5 %collective-permute-start.5 = (bf16[512,256]{1,0:T(8,128)(2,1)S(1)}, bf16[512,256]{1,0:T(8,128)(2,1)S(1)}, u32[]{:S(2)}, u32[]{:S(2)}) collective-permute-start(bf16[512,256]{1,0:T(8,128)(2,1)S(1)} %shard_map.78), channel_id=1, source_target_pairs={{0,2},{1,3},{2,4},{3,5},{4,6},{5,7},{8,10},{9,11},{10,12},{11,13},... | collective-permute-start | bytes 786440 | tf_op jit(solution)/shard_map/ppermute | solution.py:15
  84.6 6.3 %collective-permute-done.5.arrived = bf16[512,256]{1,0:T(8,128)(2,1)S(1)} collective-permute-done((bf16[512,256]{1,0:T(8,128)(2,1)S(1)}, bf16[512,256]{1,0:T(8,128)(2,1)S(1)}, u32[]{:S(2)}, u32[]{:S(2)}) %collective-permute-start.5) | collective-permute-done | bytes 262176 | tf_op jit(solution)/shard_map/ppermute | solution.py:15
  90.9 0.4 shard_map.79
  91.4 3.5 %collective-permute-start.6 = (bf16[512,256]{1,0:T(8,128)(2,1)S(1)}, bf16[512,256]{1,0:T(8,128)(2,1)S(1)}, u32[]{:S(2)}, u32[]{:S(2)}) collective-permute-start(bf16[512,256]{1,0:T(8,128)(2,1)S(1)} %shard_map.79), channel_id=1, source_target_pairs={{0,2},{1,3},{2,4},{3,5},{4,6},{5,7},{8,10},{9,11},{10,12},{11,13},... | collective-permute-start | bytes 786440 | tf_op jit(solution)/shard_map/ppermute | solution.py:15
  94.9 5.4 %collective-permute-done.6.flux = bf16[512,256]{1,0:T(8,128)(2,1)S(1)} collective-permute-done((bf16[512,256]{1,0:T(8,128)(2,1)S(1)}, bf16[512,256]{1,0:T(8,128)(2,1)S(1)}, u32[]{:S(2)}, u32[]{:S(2)}) %collective-permute-start.6) | collective-permute-done | bytes 262176 | tf_op jit(solution)/shard_map/ppermute | solution.py:15
  100.3 2.1 %shard_map.80 = (f32[2,512,256]{2,1,0:T(8,128)S(1)}, f32[512,256]{1,0:T(8,128)S(1)}, bf16[512,256]{1,0:T(8,128)(2,1)S(1)}) custom-call(bf16[2,2,512,512]{3,2,1,0:T(8,128)(2,1)S(1)} %pad_maximum_fusion.g, bf16[2,512,512]{2,1,0:T(8,128)(2,1)S(1)} %get-tuple-element.38.c, bf16[2,512,512]{2,1,0:T(8,128)(2,1)S(1)} %get-tuple-element.18.step_a, ...), custom_call_target="tpu_custom_call" | custom-call | flops 939524096 | bytes 1048576 | tf_op jit(solution)/shard_map/pallas_call | solution.py:152
  102.4 1.9 %collective-permute-start.7 = (bf16[512,256]{1,0:T(8,128)(2,1)S(1)}, bf16[512,256]{1,0:T(8,128)(2,1)S(1)}, u32[]{:S(2)}, u32[]{:S(2)}) collective-permute-start(bf16[512,256]{1,0:T(8,128)(2,1)S(1)} %get-tuple-element.26), channel_id=1, source_target_pairs={{2,0},{3,1},{4,2},{5,3},{6,4},{7,5},{10,8},{11,9},{12,10},{13,11},... | collective-permute-start | bytes 786440 | tf_op jit(solution)/shard_map/ppermute | solution.py:15
  104.4 2.3 %shard_map.81.matrix = bf16[2,512,512]{2,1,0:T(8,128)(2,1)S(1)} custom-call(bf16[2,2,512,512]{3,2,1,0:T(8,128)(2,1)S(1)} %pad_maximum_fusion.g, bf16[2,512,512]{2,1,0:T(8,128)(2,1)S(1)} %get-tuple-element.38.c), custom_call_target="tpu_custom_call" | custom-call | flops 2147483648 | bytes 1048576 | tf_op jit(solution)/shard_map/pallas_call | solution.py:152
  106.7 4.0 %collective-permute-done.7.arrived = bf16[512,256]{1,0:T(8,128)(2,1)S(1)} collective-permute-done((bf16[512,256]{1,0:T(8,128)(2,1)S(1)}, bf16[512,256]{1,0:T(8,128)(2,1)S(1)}, u32[]{:S(2)}, u32[]{:S(2)}) %collective-permute-start.7) | collective-permute-done | bytes 262176 | tf_op jit(solution)/shard_map/ppermute | solution.py:15
  110.7 0.4 shard_map.82
  111.1 1.9 %collective-permute-start.8 = (bf16[512,256]{1,0:T(8,128)(2,1)S(1)}, bf16[512,256]{1,0:T(8,128)(2,1)S(1)}, u32[]{:S(2)}, u32[]{:S(2)}) collective-permute-start(bf16[512,256]{1,0:T(8,128)(2,1)S(1)} %shard_map.82), channel_id=1, source_target_pairs={{2,0},{3,1},{4,2},{5,3},{6,4},{7,5},{10,8},{11,9},{12,10},{13,11},... | collective-permute-start | bytes 786440 | tf_op jit(solution)/shard_map/ppermute | solution.py:15
  113.1 6.3 %collective-permute-done.8.arrived = bf16[512,256]{1,0:T(8,128)(2,1)S(1)} collective-permute-done((bf16[512,256]{1,0:T(8,128)(2,1)S(1)}, bf16[512,256]{1,0:T(8,128)(2,1)S(1)}, u32[]{:S(2)}, u32[]{:S(2)}) %collective-permute-start.8) | collective-permute-done | bytes 262176 | tf_op jit(solution)/shard_map/ppermute | solution.py:15
  119.4 0.4 shard_map.83
  119.8 1.9 %collective-permute-start.9 = (bf16[512,256]{1,0:T(8,128)(2,1)S(1)}, bf16[512,256]{1,0:T(8,128)(2,1)S(1)}, u32[]{:S(2)}, u32[]{:S(2)}) collective-permute-start(bf16[512,256]{1,0:T(8,128)(2,1)S(1)} %shard_map.83), channel_id=1, source_target_pairs={{2,0},{3,1},{4,2},{5,3},{6,4},{7,5},{10,8},{11,9},{12,10},{13,11},... | collective-permute-start | bytes 786440 | tf_op jit(solution)/shard_map/ppermute | solution.py:15
  121.8 6.3 %collective-permute-done.9.arrived = bf16[512,256]{1,0:T(8,128)(2,1)S(1)} collective-permute-done((bf16[512,256]{1,0:T(8,128)(2,1)S(1)}, bf16[512,256]{1,0:T(8,128)(2,1)S(1)}, u32[]{:S(2)}, u32[]{:S(2)}) %collective-permute-start.9) | collective-permute-done | bytes 262176 | tf_op jit(solution)/shard_map/ppermute | solution.py:15
  128.1 2.1 %shard_map.84 = (bf16[512,256]{1,0:T(8,128)(2,1)S(1)}, bf16[512,256]{1,0:T(8,128)(2,1)S(1)}) custom-call(s32[1]{0:T(128)} %bitcast.core, bf16[2,2,512,512]{3,2,1,0:T(8,128)(2,1)S(1)} %pad_maximum_fusion.g, bf16[2,512,512]{2,1,0:T(8,128)(2,1)S(1)} %get-tuple-element.38.c, f32[2,512,256]{2,1,0:T(8,128)S(1)} %get-tuple-element.24.left, ...), custom_call_target="tpu_custom_call" | custom-call | flops 805306368 | bytes 1048576 | tf_op jit(solution)/shard_map/pallas_call | solution.py:152
  130.3 1.9 %collective-permute-start.10 = (bf16[512,256]{1,0:T(8,128)(2,1)S(1)}, bf16[512,256]{1,0:T(8,128)(2,1)S(1)}, u32[]{:S(2)}, u32[]{:S(2)}) collective-permute-start(bf16[512,256]{1,0:T(8,128)(2,1)S(1)} %get-tuple-element.28), channel_id=1, source_target_pairs={{0,1},{1,0},{2,3},{3,2},{4,5},{5,4},{6,7},{7,6},{8,9},{9,8},{10,11... | collective-permute-start | bytes 786440 | tf_op jit(solution)/shard_map/ppermute | solution.py:20
  132.2 1.5 collective-permute-done.10.got
  133.7 2.3 %shard_map.85 = bf16[4,2,64,1024]{3,2,1,0:T(8,128)(2,1)} custom-call(s32[1]{0:T(128)} %bitcast.core, f32[2]{0:T(128)S(1)} %add_divide_fusion.weights, bf16[512,256]{1,0:T(8,128)(2,1)S(1)} %get-tuple-element.27.kept, bf16[512,256]{1,0:T(8,128)(2,1)S(1)} %collective-permute-done.10.got), custom_call_target="tpu_custom_call" | custom-call | flops 1073741824 | bytes 1048576 | tf_op jit(solution)/shard_map/pallas_call | solution.py:152
  136.0 3.5 %all-to-all-start.2 = ((bf16[4,2,64,1024]{3,2,1,0:T(8,128)(2,1)}), bf16[4,2,64,1024]{3,2,1,0:T(8,128)(2,1)S(1)}, u32[]{:S(2)}, u32[]{:S(2)}) async-start(bf16[4,2,64,1024]{3,2,1,0:T(8,128)(2,1)} %shard_map.85), calls=%async_computation.2 | async-start | bytes 2097152 | tf_op jit(solution)/shard_map/all_to_all | solution.py:33
  139.6 0.1 stack.69
  139.6 0.1 copy.26
  139.8 0.1 copy.28
  140.0 15.1 %all-to-all-done.2 = bf16[4,2,64,1024]{3,2,1,0:T(8,128)(2,1)S(1)} async-done(((bf16[4,2,64,1024]{3,2,1,0:T(8,128)(2,1)}), bf16[4,2,64,1024]{3,2,1,0:T(8,128)(2,1)S(1)}, u32[]{:S(2)}, u32[]{:S(2)}) %all-to-all-start.2) | async-done | bytes 1048608 | tf_op jit(solution)/shard_map/all_to_all | solution.py:33
  155.1 0.9 reduce_sum.21
  156.0 3.5 %all-to-all-start.3 = ((bf16[16,8,1024]{2,1,0:T(8,128)(2,1)}), bf16[16,8,1024]{2,1,0:T(8,128)(2,1)S(1)}, u32[]{:S(2)}, u32[]{:S(2)}) async-start(bf16[16,8,1024]{2,1,0:T(8,128)(2,1)} %bitcast.35), calls=%async_computation.3 | async-start | bytes 524288 | tf_op jit(solution)/shard_map/all_to_all | solution.py:33
  159.6 0.3 fusion.2
  160.0 0.3 fusion.3
  160.4 1.3 copy.21
  161.7 1.6 pad_maximum_fusion.4
  163.3 11.2 %all-to-all-done.3 = bf16[16,8,1024]{2,1,0:T(8,128)(2,1)S(1)} async-done(((bf16[16,8,1024]{2,1,0:T(8,128)(2,1)}), bf16[16,8,1024]{2,1,0:T(8,128)(2,1)S(1)}, u32[]{:S(2)}, u32[]{:S(2)}) %all-to-all-start.3) | async-done | bytes 262176 | tf_op jit(solution)/shard_map/all_to_all | solution.py:33
  174.5 0.6 copy.22
  (40 shorter events, 0.5 us)
Async XLA Ops:
  0.6 4.4 %copy-start.9 = (bf16[2,1,512,2,128]{4,3,2,1,0:T(2,128)(2,1)S(1)}, bf16[2,1,512,2,128]{4,3,2,1,0:T(2,128)(2,1)}, u32[]{:S(2)}) copy-start(bf16[2,1,512,2,128]{4,3,2,1,0:T(2,128)(2,1)} %param.8) | copy-start | bytes 1572868
  0.6 7.2 %copy-start.10 = (bf16[1,8,512]{2,1,0:T(8,128)(2,1)S(1)}, bf16[1,8,512]{2,1,0:T(8,128)(2,1)}, u32[]{:S(2)}) copy-start(bf16[1,8,512]{2,1,0:T(8,128)(2,1)} %param.6) | copy-start | bytes 24580
  0.7 18.2 %copy-start.11 = (s32[1,4,4]{2,1,0:T(4,128)S(1)}, s32[1,4,4]{2,1,0:T(4,128)}, u32[]{:S(2)}) copy-start(s32[1,4,4]{2,1,0:T(4,128)} %param.7) | copy-start | bytes 196
  3.0 24.5 %copy-start.8 = (bf16[2,1,2,512,512]{4,3,2,1,0:T(8,128)(2,1)S(1)}, bf16[2,1,2,512,512]{4,3,2,1,0:T(8,128)(2,1)}, u32[]{:S(2)}) copy-start(bf16[2,1,2,512,512]{4,3,2,1,0:T(8,128)(2,1)} %param.5) | copy-start | bytes 6291460
  3.0 24.5 %collective-permute-start = (bf16[2,512,512]{2,1,0:T(8,128)(2,1)}, bf16[2,512,512]{2,1,0:T(8,128)(2,1)}, u32[]{:S(2)}, u32[]{:S(2)}) collective-permute-start(bf16[2,512,512]{2,1,0:T(8,128)(2,1)} %dynamic-slice_bitcast_fusion), channel_id=1, source_target_pairs={{0,1},{1,0},{2,3},{3,2},{4,5},{5,4},{6,7},{7,6},{8,9},{9,8},{10,11... | collective-permute-start | bytes 3145736 | tf_op jit(solution)/shard_map/ppermute | solution.py:20
  5.4 21.9 %collective-permute-start.1 = (bf16[512,256]{1,0:T(8,128)(2,1)S(1)}, bf16[512,256]{1,0:T(8,128)(2,1)S(1)}, u32[]{:S(2)}, u32[]{:S(2)}) collective-permute-start(bf16[512,256]{1,0:T(8,128)(2,1)S(1)} %dynamic-slice_bitcast_fusion.1), channel_id=1, source_target_pairs={{0,1},{1,0},{2,3},{3,2},{4,5},{5,4},{6,7},{7,6},{8,9},{9,8},{10,11... | collective-permute-start | bytes 786440 | tf_op jit(solution)/shard_map/ppermute | solution.py:20
  8.5 18.7 %all-to-all-start = ((bf16[8,8,512]{2,1,0:T(8,128)(2,1)}), bf16[8,8,512]{2,1,0:T(8,128)(2,1)S(1)}, u32[]{:S(2)}, u32[]{:S(2)}) async-start(bf16[8,8,512]{2,1,0:T(8,128)(2,1)} %tile.18), calls=%async_computation | async-start | bytes 131072 | tf_op jit(solution)/shard_map/all_to_all | solution.py:33
  27.5 30.2 %copy-start = (bf16[2,512,256]{2,1,0:T(8,128)(2,1)}, bf16[2,512,256]{2,1,0:T(8,128)(2,1)S(1)}, u32[]{:S(2)}) copy-start(bf16[2,512,256]{2,1,0:T(8,128)(2,1)S(1)} %pad_maximum_fusion.2.src) | copy-start | bytes 1572868
  30.1 25.7 %all-to-all-start.1 = ((bf16[8,64,512]{2,1,0:T(8,128)(2,1)}), bf16[8,64,512]{2,1,0:T(8,128)(2,1)S(1)}, u32[]{:S(2)}, u32[]{:S(2)}) async-start(bf16[8,64,512]{2,1,0:T(8,128)(2,1)} %tile.19), calls=%async_computation.1 | async-start | bytes 1048576 | tf_op jit(solution)/shard_map/all_to_all | solution.py:33
  40.8 23.7 %collective-permute-start.3 = (bf16[512,256]{1,0:T(8,128)(2,1)}, bf16[512,256]{1,0:T(8,128)(2,1)S(1)}, u32[]{:S(2)}, u32[]{:S(2)}) collective-permute-start(bf16[512,256]{1,0:T(8,128)(2,1)} %fusion), channel_id=1, source_target_pairs={{2,0},{3,1},{4,2},{5,3},{6,4},{7,5},{10,8},{11,9},{12,10},{13,11},... | collective-permute-start | bytes 786440 | tf_op jit(solution)/shard_map/ppermute | solution.py:15
  55.7 5.3 %copy-start.6 = (bf16[8,64,512]{2,1,0:T(8,128)(2,1)}, bf16[8,64,512]{2,1,0:T(8,128)(2,1)S(1)}, u32[]{:S(2)}) copy-start(bf16[8,64,512]{2,1,0:T(8,128)(2,1)S(1)} %all-to-all-done.1) | copy-start | bytes 1572868
  55.8 5.2 %collective-permute-start.2 = (bf16[512,512]{1,0:T(8,128)(2,1)S(1)}, bf16[512,512]{1,0:T(8,128)(2,1)S(1)}, u32[]{:S(2)}, u32[]{:S(2)}) collective-permute-start(bf16[512,512]{1,0:T(8,128)(2,1)S(1)} %bitcast.85), channel_id=1, source_target_pairs={{0,1},{1,0},{2,3},{3,2},{4,5},{5,4},{6,7},{7,6},{8,9},{9,8},{10,11... | collective-permute-start | bytes 1572872 | tf_op jit(solution)/shard_map/ppermute | solution.py:20
  64.5 1.0 copy-start.1
  65.5 1.2 copy-start.3
  66.8 1.0 copy-start.5
  67.8 5.8 %copy-start.4 = (bf16[2,512,512]{2,1,0:T(8,128)(2,1)S(1)}, bf16[2,512,512]{2,1,0:T(8,128)(2,1)}, u32[]{:S(2)}) copy-start(bf16[2,512,512]{2,1,0:T(8,128)(2,1)} %copy.15.ct) | copy-start | bytes 3145732
  70.1 10.6 %collective-permute-start.4 = (bf16[512,256]{1,0:T(8,128)(2,1)S(1)}, bf16[512,256]{1,0:T(8,128)(2,1)S(1)}, u32[]{:S(2)}, u32[]{:S(2)}) collective-permute-start(bf16[512,256]{1,0:T(8,128)(2,1)S(1)} %get-tuple-element.23), channel_id=1, source_target_pairs={{0,2},{1,3},{2,4},{3,5},{4,6},{5,7},{8,10},{9,11},{10,12},{11,13},... | collective-permute-start | bytes 786440 | tf_op jit(solution)/shard_map/ppermute | solution.py:15
  80.7 19.6 %copy-start.2 = (bf16[2,512,256]{2,1,0:T(8,128)(2,1)S(1)}, bf16[2,512,256]{2,1,0:T(8,128)(2,1)}, u32[]{:S(2)}) copy-start(bf16[2,512,256]{2,1,0:T(8,128)(2,1)} %copy-done) | copy-start | bytes 1572868
  81.1 9.8 %collective-permute-start.5 = (bf16[512,256]{1,0:T(8,128)(2,1)S(1)}, bf16[512,256]{1,0:T(8,128)(2,1)S(1)}, u32[]{:S(2)}, u32[]{:S(2)}) collective-permute-start(bf16[512,256]{1,0:T(8,128)(2,1)S(1)} %shard_map.78), channel_id=1, source_target_pairs={{0,2},{1,3},{2,4},{3,5},{4,6},{5,7},{8,10},{9,11},{10,12},{11,13},... | collective-permute-start | bytes 786440 | tf_op jit(solution)/shard_map/ppermute | solution.py:15
  91.4 8.9 %collective-permute-start.6 = (bf16[512,256]{1,0:T(8,128)(2,1)S(1)}, bf16[512,256]{1,0:T(8,128)(2,1)S(1)}, u32[]{:S(2)}, u32[]{:S(2)}) collective-permute-start(bf16[512,256]{1,0:T(8,128)(2,1)S(1)} %shard_map.79), channel_id=1, source_target_pairs={{0,2},{1,3},{2,4},{3,5},{4,6},{5,7},{8,10},{9,11},{10,12},{11,13},... | collective-permute-start | bytes 786440 | tf_op jit(solution)/shard_map/ppermute | solution.py:15
  102.4 8.3 %collective-permute-start.7 = (bf16[512,256]{1,0:T(8,128)(2,1)S(1)}, bf16[512,256]{1,0:T(8,128)(2,1)S(1)}, u32[]{:S(2)}, u32[]{:S(2)}) collective-permute-start(bf16[512,256]{1,0:T(8,128)(2,1)S(1)} %get-tuple-element.26), channel_id=1, source_target_pairs={{2,0},{3,1},{4,2},{5,3},{6,4},{7,5},{10,8},{11,9},{12,10},{13,11},... | collective-permute-start | bytes 786440 | tf_op jit(solution)/shard_map/ppermute | solution.py:15
  111.1 8.3 %collective-permute-start.8 = (bf16[512,256]{1,0:T(8,128)(2,1)S(1)}, bf16[512,256]{1,0:T(8,128)(2,1)S(1)}, u32[]{:S(2)}, u32[]{:S(2)}) collective-permute-start(bf16[512,256]{1,0:T(8,128)(2,1)S(1)} %shard_map.82), channel_id=1, source_target_pairs={{2,0},{3,1},{4,2},{5,3},{6,4},{7,5},{10,8},{11,9},{12,10},{13,11},... | collective-permute-start | bytes 786440 | tf_op jit(solution)/shard_map/ppermute | solution.py:15
  119.8 8.3 %collective-permute-start.9 = (bf16[512,256]{1,0:T(8,128)(2,1)S(1)}, bf16[512,256]{1,0:T(8,128)(2,1)S(1)}, u32[]{:S(2)}, u32[]{:S(2)}) collective-permute-start(bf16[512,256]{1,0:T(8,128)(2,1)S(1)} %shard_map.83), channel_id=1, source_target_pairs={{2,0},{3,1},{4,2},{5,3},{6,4},{7,5},{10,8},{11,9},{12,10},{13,11},... | collective-permute-start | bytes 786440 | tf_op jit(solution)/shard_map/ppermute | solution.py:15
  128.1 4.1 %copy-start.12 = (s32[2]{0:T(128)S(1)}, s32[2]{0:T(128)}, u32[]{:S(2)}) copy-start(s32[2]{0:T(128)} %param.9) | copy-start | bytes 28
  130.3 3.4 %collective-permute-start.10 = (bf16[512,256]{1,0:T(8,128)(2,1)S(1)}, bf16[512,256]{1,0:T(8,128)(2,1)S(1)}, u32[]{:S(2)}, u32[]{:S(2)}) collective-permute-start(bf16[512,256]{1,0:T(8,128)(2,1)S(1)} %get-tuple-element.28), channel_id=1, source_target_pairs={{0,1},{1,0},{2,3},{3,2},{4,5},{5,4},{6,7},{7,6},{8,9},{9,8},{10,11... | collective-permute-start | bytes 786440 | tf_op jit(solution)/shard_map/ppermute | solution.py:20
  136.0 19.2 %all-to-all-start.2 = ((bf16[4,2,64,1024]{3,2,1,0:T(8,128)(2,1)}), bf16[4,2,64,1024]{3,2,1,0:T(8,128)(2,1)S(1)}, u32[]{:S(2)}, u32[]{:S(2)}) async-start(bf16[4,2,64,1024]{3,2,1,0:T(8,128)(2,1)} %shard_map.85), calls=%async_computation.2 | async-start | bytes 2097152 | tf_op jit(solution)/shard_map/all_to_all | solution.py:33
  139.5 20.0 %copy-start.7 = (bf16[8,64,512]{2,1,0:T(8,128)(2,1)S(1)}, bf16[8,64,512]{2,1,0:T(8,128)(2,1)}, u32[]{:S(2)}) copy-start(bf16[8,64,512]{2,1,0:T(8,128)(2,1)} %copy-done.6) | copy-start | bytes 1572868
  156.0 18.4 %all-to-all-start.3 = ((bf16[16,8,1024]{2,1,0:T(8,128)(2,1)}), bf16[16,8,1024]{2,1,0:T(8,128)(2,1)S(1)}, u32[]{:S(2)}, u32[]{:S(2)}) async-start(bf16[16,8,1024]{2,1,0:T(8,128)(2,1)} %bitcast.35), calls=%async_computation.3 | async-start | bytes 524288 | tf_op jit(solution)/shard_map/all_to_all | solution.py:33

commit v3 on v2

--- a/solution.py
+++ b/solution.py
@@ -60,9 +60,33 @@
     out[1] = (mul(lr, ri) + mul(li, rr)).astype(BF16)
 
 
-def begin_kernel(g, c, ct, src, first, following, base, start, send):
-    base_a = src[0].astype(F32) + mul(c[0], first[1])
+def split_kernel(core, own, block):
+    block[...] = own[1 - core[0]]
+
+
+def first_kernel(core, own_g, got_g, own_s, got_s, g, src, first, send):
+    here = core[0]
+    g[here] = own_g[here]
+    g[1 - here] = got_g[...]
+    src[here] = own_s[here]
+    src[1 - here] = got_s[...]
+    field = apply(g[0, 0], g[0, 1], src[0]).astype(BF16)
+    send[...] = field
+    first[...] = apply(g[1, 0], g[1, 1], src[1]).astype(BF16)
+
+
+def begin_kernel(core, own_c, got_c, g, src, first, following, c, ct, base, start, send):
+    outer, inner, rows, _ = own_c.shape
+    here = core[0]
+    for i in range(outer):
+        for j in range(inner):
+            at = (j * outer + i) * rows
+            c[here, at : at + rows] = own_c[i, j]
+            c[1 - here, at : at + rows] = got_c[i, j]
+    base_a = src[0].astype(F32) + mul(c[0], first[...])
     base[...] = base_a
+    ct[0] = c[0].T
+    ct[1] = c[1].T
     field = apply(g[0, 0], g[0, 1], base_a.astype(BF16)).astype(BF16)
     summed = src[1].astype(F32) + mul(c[1], following[...]) + mul(ct[0], field)
     field = apply(g[1, 0], g[1, 1], summed.astype(BF16)).astype(BF16)
@@ -79,7 +103,7 @@
     product(step_b, step_a, through)
 
 
-def compose_back_kernel(g, c, back, back_a, back_b):
+def compose_back_kernel(g, c, back_a, back_b, back):
     back_a[0] = mul(g[0, 0], c[0]).astype(BF16)
     back_a[1] = mul(g[0, 1], c[0]).astype(BF16)
     back_b[0] = mul(g[1, 0], c[1]).astype(BF16)
@@ -87,30 +111,36 @@
     product(back_a, back_b, back)
 
 
+def compose_turn_kernel(g, step_a, back_a, src, base, to_b, to_a, field_b, field_a):
+    gbr, gbi = g[1, 0], g[1, 1]
+    sr, si = step_a[0], step_a[1]
+    to_b[0] = (mul(gbr, sr) - mul(gbi, si)).astype(BF16)
+    to_b[1] = (mul(gbr, si) + mul(gbi, sr)).astype(BF16)
+    ar, ai = back_a[0], back_a[1]
+    br, bi = to_b[0], to_b[1]
+    to_a[0] = (g[0, 0].astype(F32) + mul(ar, br) - mul(ai, bi)).astype(BF16)
+    to_a[1] = (g[0, 1].astype(F32) + mul(ar, bi) + mul(ai, br)).astype(BF16)
+    flux_a = apply(sr, si, base[...].astype(BF16))
+    here = apply(gbr, gbi, (src[1].astype(F32) + flux_a).astype(BF16))
+    field_b[...] = here
+    field_a[...] = apply(g[0, 0], g[0, 1], src[0]) + apply(ar, ai, here.astype(BF16))
+
+
 def hop_kernel(matrix, start, arrived, send):
     send[...] = (start[...] + apply(matrix[0], matrix[1], arrived[...])).astype(BF16)
 
 
-def turn_kernel(g, c, step_a, src, base, flux, left, start, send):
-    arrived = flux[...].astype(F32)
-    summed = (base[...] + arrived).astype(BF16)
-    flux_a = apply(step_a[0], step_a[1], summed)
-    left_a = src[0].astype(F32) + arrived
-    left_b = src[1].astype(F32) + flux_a
-    left[0] = left_a
-    left[1] = left_b
-    field = apply(g[1, 0], g[1, 1], left_b.astype(BF16)).astype(BF16)
-    summed = (left_a + mul(c[0], field)).astype(BF16)
-    wave = apply(g[0, 0], g[0, 1], summed)
+def turn_kernel(to_a, to_b, field_a, field_b, flux, start, end, send):
+    arrived = flux[...]
+    wave = field_a[...] + apply(to_a[0], to_a[1], arrived)
     start[...] = wave
     send[...] = wave.astype(BF16)
-
-
-def finish_kernel(core, g, c, left, arrived, keep, send):
-    summed = (left[1] + mul(c[1], arrived[...])).astype(BF16)
-    wave_b = apply(g[1, 0], g[1, 1], summed).astype(BF16)
-    summed = (left[0] + mul(c[0], wave_b)).astype(BF16)
-    wave_a = apply(g[0, 0], g[0, 1], summed).astype(BF16)
+    end[...] = field_b[...] + apply(to_b[0], to_b[1], arrived)
+
+
+def finish_kernel(core, back, back_b, start, end, arrived, keep, send):
+    wave_a = (start[...] + apply(back[0], back[1], arrived[...])).astype(BF16)
+    wave_b = (end[...] + apply(back_b[0], back_b[1], arrived[...])).astype(BF16)
 
     @pl.when(core[0] == 0)
     def _():
@@ -174,8 +204,6 @@
     devices = lax.axis_size("energy")
     ny, nx, nz = energy_grid(devices)
     at = lambda y, x, z: (y * nx + x) * nz + z
-    along_z = [[at(y, x, z) for z in range(nz)] for y in range(ny) for x in range(nx)]
-    along_yx = [[at(y, x, z) for y in range(ny) for x in range(nx)] for z in range(nz)]
     along_x = [[at(y, x, z) for x in range(nx)] for y in range(ny) for z in range(nz)]
     along_yz = [[at(y, x, z) for y in range(ny) for z in range(nz)] for x in range(nx)]
     rows = coupling.shape[1]
@@ -184,27 +212,36 @@
     mat = (2, n, n)
     unit = 2 * n * n * cols
 
-    some = exchange(jnp.tile(coupling[0], (nz, 1)), along_z)
-    by_row = jnp.repeat(masks[0].astype(BF16), tile, axis=0)
-    first_row = (lax.axis_index("energy") // nz) * nz * rows
-    here = lax.dynamic_slice_in_dim(by_row, first_row, nz * rows, 0)
-    some = some * jnp.repeat(here, tile, axis=1)
-
     core = lax.rem(lax.axis_index("slab"), 2)
-    own = green_local[:, 0]
-    green = ordered(core, pick(own, core), swap(pick(own, 1 - core)))
-    own = incident[:, 0].reshape(count, n, cols)
-    source = ordered(core, pick(own, core), swap(pick(own, 1 - core)))
-    some, green, source = lax.optimization_barrier((jnp.tile(some, (ny * nx, 1)), green, source))
-    whole = exchange(some, along_yx)
-    first = jnp.stack([apply(green[s, 0], green[s, 1], source[s]) for s in range(2)]).astype(BF16)
-    following = chip_hop(first[0], -1)
-    c = ordered(core, whole, swap(whole))
-    ct = c.transpose(0, 2, 1)
+    which = core.reshape(1)
+
+    some = jnp.tile(coupling[0], (ny * nz, 1))
+    some, green_local, incident = lax.optimization_barrier((some, green_local, incident))
+    own_g, own_s = green_local[:, 0], incident[:, 0].reshape(count, n, cols)
+    some = exchange(some, along_yz)
+    by_row = jnp.repeat(masks[0].astype(BF16), tile, axis=0).reshape(ny, nx, nz * rows, -1)
+    here = lax.rem(lax.axis_index("energy") // nz, nx)
+    here = lax.dynamic_index_in_dim(by_row, here, 1, keepdims=False)
+    some = some.reshape(ny, nz * rows, n) * jnp.repeat(here, tile, axis=2)
+
+    got_g = swap(call(split_kernel, [(mat, BF16)], which, own_g, smem=1))
+    got_s = swap(call(split_kernel, [(vec, BF16)], which, own_s, smem=1))
+    green, source, first, send = call(
+        first_kernel,
+        [((2, *mat), BF16), ((2, *vec), BF16), (vec, BF16), (vec, BF16)],
+        which, own_g, got_g, own_s, got_s, smem=1, flops=4 * unit,
+    )
+    some = jnp.broadcast_to(some[None], (nx, *some.shape))
+    some, send = lax.optimization_barrier((some, send))
+    own_c = exchange(some, along_x)
+    following = chip_hop(send, -1)
+    got_c = swap(own_c)
 
     hops = lax.axis_size("slab") // 2 - 1
-    base, start, send = call(
-        begin_kernel, [(vec, F32), (vec, F32), (vec, BF16)], green, c, ct, source, first, following, flops=8 * unit
+    c, ct, base, start, send = call(
+        begin_kernel,
+        [(mat, BF16), (mat, BF16), (vec, F32), (vec, F32), (vec, BF16)],
+        which, own_c, got_c, green, source, first, following, smem=1, flops=8 * unit,
     )
     flux = chip_hop(send, 1)
     step_a, through = call(
@@ -213,19 +250,21 @@
     for _ in range(hops - 1):
         send = call(hop_kernel, [(vec, BF16)], through, start, flux, flops=2 * unit)
         flux = chip_hop(send, 1)
-    back = call(
-        compose_back_kernel, [(mat, BF16)], green, c, scratch=[(mat, BF16), (mat, BF16)], flops=16 * n**3
-    )
-    left, start, send = call(
-        turn_kernel, [((2, *vec), F32), (vec, F32), (vec, BF16)], green, c, step_a, source, base, flux, flops=7 * unit
+    back_a, back_b, back = call(compose_back_kernel, [(mat, BF16)] * 3, green, c, flops=16 * n**3)
+    to_b, to_a, field_b, field_a = call(
+        compose_turn_kernel,
+        [(mat, BF16), (mat, BF16), (vec, F32), (vec, F32)],
+        green, step_a, back_a, source, base, flops=16 * n**3 + 8 * unit,
+    )
+    start, end, send = call(
+        turn_kernel, [(vec, F32), (vec, F32), (vec, BF16)], to_a, to_b, field_a, field_b, flux, flops=4 * unit
     )
     arrived = chip_hop(send, -1)
     for _ in range(hops - 1):
         send = call(hop_kernel, [(vec, BF16)], back, start, arrived, flops=2 * unit)
         arrived = chip_hop(send, -1)
-    which = core.reshape(1)
     kept, send = call(
-        finish_kernel, [(vec, BF16), (vec, BF16)], which, green, c, left, arrived, smem=1, flops=6 * unit
+        finish_kernel, [(vec, BF16), (vec, BF16)], which, back, back_b, start, end, arrived, smem=1, flops=4 * unit
     )
 
     got = swap(send)
@@ -239,7 +278,8 @@
     density = jnp.sum(parts.astype(F32), axis=0).reshape(1, rows, 2, n)
 
     wave = ordered(core, kept, got)
-    outflow = jnp.stack([mul(whole.T, wave[e]) for e in range(count)]).astype(BF16)
+    flow = pick(ct, core)
+    outflow = jnp.stack([mul(flow, wave[e]) for e in range(count)]).astype(BF16)
     shape = (count, 1, n, 2, modes)
     return (wave.reshape(shape), outflow.reshape(shape), density)
 

time: 176 us -> 165 us (0.938)
  blocking collectives: 0 us -> 12.7 us
  starting transfers between devices: 54 us -> 44.7 us
  local copies, waits for them, and re-layouts: 12.4 us -> 6.53 us
  other arithmetic: 8.18 us -> 2.65 us
  Pallas kernels: 15.2 us -> 19.7 us
  waiting for transfers between devices: 80.9 us -> 76.7 us
  matrix products: 3.48 us -> 0.66 us
    all_to_all x0 -> x1, blocking collectives: none -> 12.7 us  [exchange(): lax.all_to_all(block, 'energy', 0, 0, axis_index_groups=groups, tiled=True)]
    all_to_all x4 -> x3, waiting for transfers between devices: 46.4 us -> 35.9 us  [exchange(): lax.all_to_all(block, 'energy', 0, 0, axis_index_groups=groups, tiled=True)]
    ppermute x7, waiting for transfers between devices: 33 us -> 39.4 us  [chip_hop(): return lax.ppermute(block, 'slab', route)]
    ppermute x7, starting transfers between devices: 19.6 us -> 14.8 us  [chip_hop(): return lax.ppermute(block, 'slab', route)]
    pallas_call x10 -> x14, Pallas kernels: 15.2 us -> 19.7 us  [call(): pl.pallas_call(kernel, out_shape=outs, in_specs=[scalars] * smem + [whole...]
    all_to_all x4 -> x3, starting transfers between devices: 26 us -> 21.9 us  [exchange(): lax.all_to_all(block, 'energy', 0, 0, axis_index_groups=groups, tiled=True)]
    dot_general x6 -> x2, matrix products: 3.48 us -> 0.66 us  [mul(): lax.dot_general(left, right, (((1,), (0,)), ((), ())), preferred_element_...]
    squeeze x3 -> x0, local copies, waits for them, and re-layouts: 2.38 us -> none  [the longest x2 2.35 us: pick(): return lax.dynamic_index_in_dim(blocks, index, 0, keepdims=False)]
  transfers between devices with their start and end apart: 15 -> 14, of which waited for: 11 -> 11; matrix products, arithmetic and copies ran while one was open for 8% -> 3% of each run, Pallas kernels for 3% -> 5%
where the time goes in v3:
time: 165 us
  waiting for transfers between devices  76.7 us (46%)
  starting transfers between devices  44.7 us (27%)
  Pallas kernels  19.7 us (12%)
  blocking collectives  12.7 us (8%)
  local copies, waits for them, and re-layouts  6.53 us (4%)
  other arithmetic  2.65 us (2%)
    ppermute x7, waiting for transfers between devices, chip_hop(): return lax.ppermute(block, 'slab', route)  39.4 us
    all_to_all x3, waiting for transfers between devices, exchange(): lax.all_to_all(block, 'energy', 0, 0, axis_index_groups=groups, tiled=True)  35.9 us
    all_to_all x3, starting transfers between devices, exchange(): lax.all_to_all(block, 'energy', 0, 0, axis_index_groups=groups, tiled=True)  21.9 us
    pallas_call x14, Pallas kernels, call(): pl.pallas_call(kernel, out_shape=outs, in_specs=[scalars] * smem + [whole...  19.7 us
    ppermute x7, starting transfers between devices, chip_hop(): return lax.ppermute(block, 'slab', route)  14.8 us
    all_to_all x1, blocking collectives, exchange(): lax.all_to_all(block, 'energy', 0, 0, axis_index_groups=groups, tiled=True)  12.7 us
    ppermute x4, starting transfers between devices, swap(): return lax.ppermute(block, 'slab', route)  8 us
    unnamed x19, local copies, waits for them, and re-layouts  4.36 us
  transfers between devices with their start and end apart: 14, of which 11 were waited for; matrix products, arithmetic and copies ran while one was open for 3% of the time, Pallas kernels for 5%

profile of v3, /device:TPU:8, one launch (start us, length us, event | category | flops | bytes accessed | tf_op | source)
XLA Modules:
  0.0 164.7 jit_solution(9101407141122851816)
XLA Ops:
  0.6 0.0 copy-start
  0.6 0.7 copy-done
  1.3 0.7 broadcast_bitcast_fusion
  2.0 1.6 copy-done.1
  3.6 1.1 shard_map.76
  4.7 2.0 %collective-permute-start = (bf16[2,512,512]{2,1,0:T(8,128)(2,1)}, bf16[2,512,512]{2,1,0:T(8,128)(2,1)}, u32[]{:S(2)}, u32[]{:S(2)}) collective-permute-start(bf16[2,512,512]{2,1,0:T(8,128)(2,1)} %shard_map.76), channel_id=1, source_target_pairs={{0,1},{1,0},{2,3},{3,2},{4,5},{5,4},{6,7},{7,6},{8,9},{9,8},{10,11... | collective-permute-start | bytes 3145736 | tf_op jit(solution)/shard_map/ppermute | solution.py:20
  6.7 14.8 %all-to-all-start = ((bf16[16,8,512]{2,1,0:T(8,128)(2,1)}), bf16[16,8,512]{2,1,0:T(8,128)(2,1)S(1)}, u32[]{:S(2)}, u32[]{:S(2)}) async-start(bf16[16,8,512]{2,1,0:T(8,128)(2,1)} %bitcast.4), calls=%async_computation | async-start | bytes 262144 | tf_op jit(solution)/shard_map/all_to_all | solution.py:33
  21.5 0.0 copy-done.4
  21.5 0.3 reshape_squeeze.3.own.own_s
  21.9 2.1 %collective-permute-start.1 = (bf16[512,256]{1,0:T(8,128)(2,1)S(1)}, bf16[512,256]{1,0:T(8,128)(2,1)S(1)}, u32[]{:S(2)}, u32[]{:S(2)}) collective-permute-start(bf16[512,256]{1,0:T(8,128)(2,1)S(1)} %shard_map.77), channel_id=1, source_target_pairs={{0,1},{1,0},{2,3},{3,2},{4,5},{5,4},{6,7},{7,6},{8,9},{9,8},{10,11... | collective-permute-start | bytes 786440 | tf_op jit(solution)/shard_map/ppermute | solution.py:20
  24.1 0.0 copy-done.5
  24.1 0.1 broadcast_bitcast_fusion.1
  24.2 10.9 %all-to-all-done = bf16[16,8,512]{2,1,0:T(8,128)(2,1)S(1)} async-done(((bf16[16,8,512]{2,1,0:T(8,128)(2,1)}), bf16[16,8,512]{2,1,0:T(8,128)(2,1)S(1)}, u32[]{:S(2)}, u32[]{:S(2)}) %all-to-all-start) | async-done | bytes 131104 | tf_op jit(solution)/shard_map/all_to_all | solution.py:33
  35.1 0.0 collective-permute-done.1.got_s
  35.1 0.0 collective-permute-done.got_g
  35.1 0.0 copy-done.2
  35.2 2.1 %shard_map.78 = (bf16[2,2,512,512]{3,2,1,0:T(8,128)(2,1)S(1)}, bf16[2,512,256]{2,1,0:T(8,128)(2,1)S(1)}, bf16[512,256]{1,0:T(8,128)(2,1)S(1)}, bf16[512,256]{1,0:T(8,128)(2,1)S(1)}) custom-call(s32[1]{0:T(128)} %bitcast.core, bf16[2,2,512,512]{3,2,1,0:T(8,128)(2,1)S(1)} %bitcast.40, bf16[2,512,512]{2,1,0:T(8,128)(2,1)} %collective-permute-done.got_g, ...), custom_call_target="tpu_custom_call" | custom-call | flops 536870912 | bytes 1048576 | tf_op jit(solution)/shard_map/pallas_call | solution.py:182
  37.3 12.7 %all_to_all.24.own_c = bf16[4,2,64,512]{3,2,1,0:T(8,128)(2,1)S(1)} all-to-all(bf16[4,2,64,512]{3,2,1,0:T(8,128)(2,1)S(1)} %broadcast_in_dim.23), channel_id=1, replica_groups={{0,64,128,192},{8,72,136,200},{16,80,144,208},{24,88,152,216},{32,96,16..., dimensions={0} | all-to-all | bytes 1048576 | tf_op jit(solution)/shard_map/all_to_all | solution.py:33
  50.0 1.9 %collective-permute-start.2 = (bf16[4,2,64,512]{3,2,1,0:T(8,128)(2,1)S(1)}, bf16[4,2,64,512]{3,2,1,0:T(8,128)(2,1)S(1)}, u32[]{:S(2)}, u32[]{:S(2)}) collective-permute-start(bf16[4,2,64,512]{3,2,1,0:T(8,128)(2,1)S(1)} %all_to_all.24.own_c), channel_id=1, source_target_pairs={{0,1},{1,0},{2,3},{3,2},{4,5},{5,4},{6,7},{7,6},{8,9},{9,8},{10,11... | collective-permute-start | bytes 1572872 | tf_op jit(solution)/shard_map/ppermute | solution.py:20
  52.0 2.2 %collective-permute-start.3 = (bf16[512,256]{1,0:T(8,128)(2,1)S(1)}, bf16[512,256]{1,0:T(8,128)(2,1)S(1)}, u32[]{:S(2)}, u32[]{:S(2)}) collective-permute-start(bf16[512,256]{1,0:T(8,128)(2,1)S(1)} %get-tuple-element.39), channel_id=1, source_target_pairs={{2,0},{3,1},{4,2},{5,3},{6,4},{7,5},{10,8},{11,9},{12,10},{13,11},... | collective-permute-start | bytes 786440 | tf_op jit(solution)/shard_map/ppermute | solution.py:15
  54.2 8.4 %collective-permute-done.3.following = bf16[512,256]{1,0:T(8,128)(2,1)S(1)} collective-permute-done((bf16[512,256]{1,0:T(8,128)(2,1)S(1)}, bf16[512,256]{1,0:T(8,128)(2,1)S(1)}, u32[]{:S(2)}, u32[]{:S(2)}) %collective-permute-start.3) | collective-permute-done | bytes 262176 | tf_op jit(solution)/shard_map/ppermute | solution.py:15
  62.6 0.0 collective-permute-done.2.got_c
  62.6 2.3 %shard_map.79 = (bf16[2,512,512]{2,1,0:T(8,128)(2,1)S(1)}, bf16[2,512,512]{2,1,0:T(8,128)(2,1)S(1)}, f32[512,256]{1,0:T(8,128)S(1)}, f32[512,256]{1,0:T(8,128)S(1)}, bf16[512,256]{1,0:T(8,128)(2,1)S(1)}) custom-call(s32[1]{0:T(128)} %bitcast.core, bf16[4,2,64,512]{3,2,1,0:T(8,128)(2,1)S(1)} %all_to_all.24.own_c, ...), custom_call_target="tpu_custom_call" | custom-call | flops 1073741824 | bytes 1048576 | tf_op jit(solution)/shard_map/pallas_call | solution.py:182
  64.9 1.9 %collective-permute-start.4 = (bf16[512,256]{1,0:T(8,128)(2,1)S(1)}, bf16[512,256]{1,0:T(8,128)(2,1)S(1)}, u32[]{:S(2)}, u32[]{:S(2)}) collective-permute-start(bf16[512,256]{1,0:T(8,128)(2,1)S(1)} %get-tuple-element.53), channel_id=1, source_target_pairs={{0,2},{1,3},{2,4},{3,5},{4,6},{5,7},{8,10},{9,11},{10,12},{11,13},... | collective-permute-start | bytes 786440 | tf_op jit(solution)/shard_map/ppermute | solution.py:15
  66.8 2.3 %shard_map.81 = (bf16[2,512,512]{2,1,0:T(8,128)(2,1)S(1)}, bf16[2,512,512]{2,1,0:T(8,128)(2,1)S(1)}) custom-call(bf16[2,2,512,512]{3,2,1,0:T(8,128)(2,1)S(1)} %get-tuple-element.33.g, bf16[2,512,512]{2,1,0:T(8,128)(2,1)S(1)} %get-tuple-element.43.ct), custom_call_target="tpu_custom_call" | custom-call | flops 2147483648 | bytes 1048576 | tf_op jit(solution)/shard_map/pallas_call | solution.py:182
  69.1 5.5 %collective-permute-done.4.arrived = bf16[512,256]{1,0:T(8,128)(2,1)S(1)} collective-permute-done((bf16[512,256]{1,0:T(8,128)(2,1)S(1)}, bf16[512,256]{1,0:T(8,128)(2,1)S(1)}, u32[]{:S(2)}, u32[]{:S(2)}) %collective-permute-start.4) | collective-permute-done | bytes 262176 | tf_op jit(solution)/shard_map/ppermute | solution.py:15
  74.7 0.4 shard_map.83
  75.1 2.2 %collective-permute-start.5 = (bf16[512,256]{1,0:T(8,128)(2,1)S(1)}, bf16[512,256]{1,0:T(8,128)(2,1)S(1)}, u32[]{:S(2)}, u32[]{:S(2)}) collective-permute-start(bf16[512,256]{1,0:T(8,128)(2,1)S(1)} %shard_map.83), channel_id=1, source_target_pairs={{0,2},{1,3},{2,4},{3,5},{4,6},{5,7},{8,10},{9,11},{10,12},{11,13},... | collective-permute-start | bytes 786440 | tf_op jit(solution)/shard_map/ppermute | solution.py:15
  77.3 2.3 %shard_map.80 = (bf16[2,512,512]{2,1,0:T(8,128)(2,1)S(1)}, bf16[2,512,512]{2,1,0:T(8,128)(2,1)S(1)}, bf16[2,512,512]{2,1,0:T(8,128)(2,1)S(1)}) custom-call(bf16[2,2,512,512]{3,2,1,0:T(8,128)(2,1)S(1)} %get-tuple-element.33.g, bf16[2,512,512]{2,1,0:T(8,128)(2,1)S(1)} %get-tuple-element.40.c), custom_call_target="tpu_custom_call" | custom-call | flops 2147483648 | bytes 1048576 | tf_op jit(solution)/shard_map/pallas_call | solution.py:182
  79.7 4.4 %collective-permute-done.5.arrived = bf16[512,256]{1,0:T(8,128)(2,1)S(1)} collective-permute-done((bf16[512,256]{1,0:T(8,128)(2,1)S(1)}, bf16[512,256]{1,0:T(8,128)(2,1)S(1)}, u32[]{:S(2)}, u32[]{:S(2)}) %collective-permute-start.5) | collective-permute-done | bytes 262176 | tf_op jit(solution)/shard_map/ppermute | solution.py:15
  84.0 0.4 shard_map.84
  84.5 2.5 %collective-permute-start.6 = (bf16[512,256]{1,0:T(8,128)(2,1)S(1)}, bf16[512,256]{1,0:T(8,128)(2,1)S(1)}, u32[]{:S(2)}, u32[]{:S(2)}) collective-permute-start(bf16[512,256]{1,0:T(8,128)(2,1)S(1)} %shard_map.84), channel_id=1, source_target_pairs={{0,2},{1,3},{2,4},{3,5},{4,6},{5,7},{8,10},{9,11},{10,12},{11,13},... | collective-permute-start | bytes 786440 | tf_op jit(solution)/shard_map/ppermute | solution.py:15
  87.0 4.0 %shard_map.82 = (bf16[2,512,512]{2,1,0:T(8,128)(2,1)S(1)}, bf16[2,512,512]{2,1,0:T(8,128)(2,1)S(1)}, f32[512,256]{1,0:T(8,128)S(1)}, f32[512,256]{1,0:T(8,128)S(1)}) custom-call(bf16[2,2,512,512]{3,2,1,0:T(8,128)(2,1)S(1)} %get-tuple-element.33.g, bf16[2,512,512]{2,1,0:T(8,128)(2,1)S(1)} %get-tuple-element.44.step_a, ...), custom_call_target="tpu_custom_call" | custom-call | flops 3221225472 | bytes 1048576 | tf_op jit(solution)/shard_map/pallas_call | solution.py:182
  91.0 1.7 %collective-permute-done.6.flux = bf16[512,256]{1,0:T(8,128)(2,1)S(1)} collective-permute-done((bf16[512,256]{1,0:T(8,128)(2,1)S(1)}, bf16[512,256]{1,0:T(8,128)(2,1)S(1)}, u32[]{:S(2)}, u32[]{:S(2)}) %collective-permute-start.6) | collective-permute-done | bytes 262176 | tf_op jit(solution)/shard_map/ppermute | solution.py:15
  92.8 0.7 shard_map.85
  93.5 1.9 %collective-permute-start.7 = (bf16[512,256]{1,0:T(8,128)(2,1)S(1)}, bf16[512,256]{1,0:T(8,128)(2,1)S(1)}, u32[]{:S(2)}, u32[]{:S(2)}) collective-permute-start(bf16[512,256]{1,0:T(8,128)(2,1)S(1)} %get-tuple-element.56), channel_id=1, source_target_pairs={{2,0},{3,1},{4,2},{5,3},{6,4},{7,5},{10,8},{11,9},{12,10},{13,11},... | collective-permute-start | bytes 786440 | tf_op jit(solution)/shard_map/ppermute | solution.py:15
  95.4 6.3 %collective-permute-done.7.arrived = bf16[512,256]{1,0:T(8,128)(2,1)S(1)} collective-permute-done((bf16[512,256]{1,0:T(8,128)(2,1)S(1)}, bf16[512,256]{1,0:T(8,128)(2,1)S(1)}, u32[]{:S(2)}, u32[]{:S(2)}) %collective-permute-start.7) | collective-permute-done | bytes 262176 | tf_op jit(solution)/shard_map/ppermute | solution.py:15
  101.7 0.4 shard_map.86
  102.2 1.9 %collective-permute-start.8 = (bf16[512,256]{1,0:T(8,128)(2,1)S(1)}, bf16[512,256]{1,0:T(8,128)(2,1)S(1)}, u32[]{:S(2)}, u32[]{:S(2)}) collective-permute-start(bf16[512,256]{1,0:T(8,128)(2,1)S(1)} %shard_map.86), channel_id=1, source_target_pairs={{2,0},{3,1},{4,2},{5,3},{6,4},{7,5},{10,8},{11,9},{12,10},{13,11},... | collective-permute-start | bytes 786440 | tf_op jit(solution)/shard_map/ppermute | solution.py:15
  104.1 6.9 %collective-permute-done.8.arrived = bf16[512,256]{1,0:T(8,128)(2,1)S(1)} collective-permute-done((bf16[512,256]{1,0:T(8,128)(2,1)S(1)}, bf16[512,256]{1,0:T(8,128)(2,1)S(1)}, u32[]{:S(2)}, u32[]{:S(2)}) %collective-permute-start.8) | collective-permute-done | bytes 262176 | tf_op jit(solution)/shard_map/ppermute | solution.py:15
  111.0 0.4 shard_map.87
  111.4 0.0 copy-start.6
  111.4 2.1 %collective-permute-start.9 = (bf16[512,256]{1,0:T(8,128)(2,1)S(1)}, bf16[512,256]{1,0:T(8,128)(2,1)S(1)}, u32[]{:S(2)}, u32[]{:S(2)}) collective-permute-start(bf16[512,256]{1,0:T(8,128)(2,1)S(1)} %shard_map.87), channel_id=1, source_target_pairs={{2,0},{3,1},{4,2},{5,3},{6,4},{7,5},{10,8},{11,9},{12,10},{13,11},... | collective-permute-start | bytes 786440 | tf_op jit(solution)/shard_map/ppermute | solution.py:15
  113.5 6.2 %collective-permute-done.9.arrived = bf16[512,256]{1,0:T(8,128)(2,1)S(1)} collective-permute-done((bf16[512,256]{1,0:T(8,128)(2,1)S(1)}, bf16[512,256]{1,0:T(8,128)(2,1)S(1)}, u32[]{:S(2)}, u32[]{:S(2)}) %collective-permute-start.9) | collective-permute-done | bytes 262176 | tf_op jit(solution)/shard_map/ppermute | solution.py:15
  119.7 0.8 shard_map.88
  120.5 1.9 %collective-permute-start.10 = (bf16[512,256]{1,0:T(8,128)(2,1)S(1)}, bf16[512,256]{1,0:T(8,128)(2,1)S(1)}, u32[]{:S(2)}, u32[]{:S(2)}) collective-permute-start(bf16[512,256]{1,0:T(8,128)(2,1)S(1)} %get-tuple-element.58), channel_id=1, source_target_pairs={{0,1},{1,0},{2,3},{3,2},{4,5},{5,4},{6,7},{7,6},{8,9},{9,8},{10,11... | collective-permute-start | bytes 786440 | tf_op jit(solution)/shard_map/ppermute | solution.py:20
  122.4 1.5 collective-permute-done.10.got
  123.9 2.3 %shard_map.89 = bf16[4,2,64,1024]{3,2,1,0:T(8,128)(2,1)} custom-call(s32[1]{0:T(128)} %bitcast.core, f32[2]{0:T(128)S(1)} %add_divide_fusion.weights, bf16[512,256]{1,0:T(8,128)(2,1)S(1)} %get-tuple-element.57.kept, bf16[512,256]{1,0:T(8,128)(2,1)S(1)} %collective-permute-done.10.got), custom_call_target="tpu_custom_call" | custom-call | flops 1073741824 | bytes 1048576 | tf_op jit(solution)/shard_map/pallas_call | solution.py:182
  126.2 3.5 %all-to-all-start.2 = ((bf16[4,2,64,1024]{3,2,1,0:T(8,128)(2,1)}), bf16[4,2,64,1024]{3,2,1,0:T(8,128)(2,1)S(1)}, u32[]{:S(2)}, u32[]{:S(2)}) async-start(bf16[4,2,64,1024]{3,2,1,0:T(8,128)(2,1)} %shard_map.89), calls=%async_computation.2 | async-start | bytes 2097152 | tf_op jit(solution)/shard_map/all_to_all | solution.py:33
  129.8 0.1 stack.18
  129.9 0.1 copy.18
  130.0 0.1 stack.19
  130.1 0.8 copy.19
  130.9 14.4 %all-to-all-done.2 = bf16[4,2,64,1024]{3,2,1,0:T(8,128)(2,1)S(1)} async-done(((bf16[4,2,64,1024]{3,2,1,0:T(8,128)(2,1)}), bf16[4,2,64,1024]{3,2,1,0:T(8,128)(2,1)S(1)}, u32[]{:S(2)}, u32[]{:S(2)}) %all-to-all-start.2) | async-done | bytes 1048608 | tf_op jit(solution)/shard_map/all_to_all | solution.py:33
  145.4 0.9 reduce_sum.21
  146.3 3.6 %all-to-all-start.3 = ((bf16[16,8,1024]{2,1,0:T(8,128)(2,1)}), bf16[16,8,1024]{2,1,0:T(8,128)(2,1)S(1)}, u32[]{:S(2)}, u32[]{:S(2)}) async-start(bf16[16,8,1024]{2,1,0:T(8,128)(2,1)} %bitcast.16), calls=%async_computation.3 | async-start | bytes 524288 | tf_op jit(solution)/shard_map/all_to_all | solution.py:33
  149.9 0.3 fusion
  150.2 0.0 copy-done.3
  150.2 0.3 fusion.1
  150.6 0.1 pad_maximum_fusion.1
  150.6 1.3 copy.16
  152.0 1.6 pad_maximum_fusion
  153.5 10.5 %all-to-all-done.3 = bf16[16,8,1024]{2,1,0:T(8,128)(2,1)S(1)} async-done(((bf16[16,8,1024]{2,1,0:T(8,128)(2,1)}), bf16[16,8,1024]{2,1,0:T(8,128)(2,1)S(1)}, u32[]{:S(2)}, u32[]{:S(2)}) %all-to-all-start.3) | async-done | bytes 262176 | tf_op jit(solution)/shard_map/all_to_all | solution.py:33
  164.1 0.6 copy.17
  (17 shorter events, 0.2 us)
Async XLA Ops:
  0.6 0.7 copy-start
  2.0 1.6 copy-start.1
  3.6 17.9 %copy-start.4 = (bf16[2,1,512,2,128]{4,3,2,1,0:T(2,128)(2,1)S(1)}, bf16[2,1,512,2,128]{4,3,2,1,0:T(2,128)(2,1)}, u32[]{:S(2)}) copy-start(bf16[2,1,512,2,128]{4,3,2,1,0:T(2,128)(2,1)} %param.8) | copy-start | bytes 1572868
  3.6 20.5 %copy-start.5 = (s32[1,4,4]{2,1,0:T(4,128)S(1)}, s32[1,4,4]{2,1,0:T(4,128)}, u32[]{:S(2)}) copy-start(s32[1,4,4]{2,1,0:T(4,128)} %param.7) | copy-start | bytes 196
  3.6 31.6 %copy-start.2 = (bf16[2,1,2,512,512]{4,3,2,1,0:T(8,128)(2,1)S(1)}, bf16[2,1,2,512,512]{4,3,2,1,0:T(8,128)(2,1)}, u32[]{:S(2)}) copy-start(bf16[2,1,2,512,512]{4,3,2,1,0:T(8,128)(2,1)} %param.5) | copy-start | bytes 6291460
  4.7 30.5 %collective-permute-start = (bf16[2,512,512]{2,1,0:T(8,128)(2,1)}, bf16[2,512,512]{2,1,0:T(8,128)(2,1)}, u32[]{:S(2)}, u32[]{:S(2)}) collective-permute-start(bf16[2,512,512]{2,1,0:T(8,128)(2,1)} %shard_map.76), channel_id=1, source_target_pairs={{0,1},{1,0},{2,3},{3,2},{4,5},{5,4},{6,7},{7,6},{8,9},{9,8},{10,11... | collective-permute-start | bytes 3145736 | tf_op jit(solution)/shard_map/ppermute | solution.py:20
  6.7 28.4 %all-to-all-start = ((bf16[16,8,512]{2,1,0:T(8,128)(2,1)}), bf16[16,8,512]{2,1,0:T(8,128)(2,1)S(1)}, u32[]{:S(2)}, u32[]{:S(2)}) async-start(bf16[16,8,512]{2,1,0:T(8,128)(2,1)} %bitcast.4), calls=%async_computation | async-start | bytes 262144 | tf_op jit(solution)/shard_map/all_to_all | solution.py:33
  21.9 13.2 %collective-permute-start.1 = (bf16[512,256]{1,0:T(8,128)(2,1)S(1)}, bf16[512,256]{1,0:T(8,128)(2,1)S(1)}, u32[]{:S(2)}, u32[]{:S(2)}) collective-permute-start(bf16[512,256]{1,0:T(8,128)(2,1)S(1)} %shard_map.77), channel_id=1, source_target_pairs={{0,1},{1,0},{2,3},{3,2},{4,5},{5,4},{6,7},{7,6},{8,9},{9,8},{10,11... | collective-permute-start | bytes 786440 | tf_op jit(solution)/shard_map/ppermute | solution.py:20
  50.0 12.5 %collective-permute-start.2 = (bf16[4,2,64,512]{3,2,1,0:T(8,128)(2,1)S(1)}, bf16[4,2,64,512]{3,2,1,0:T(8,128)(2,1)S(1)}, u32[]{:S(2)}, u32[]{:S(2)}) collective-permute-start(bf16[4,2,64,512]{3,2,1,0:T(8,128)(2,1)S(1)} %all_to_all.24.own_c), channel_id=1, source_target_pairs={{0,1},{1,0},{2,3},{3,2},{4,5},{5,4},{6,7},{7,6},{8,9},{9,8},{10,11... | collective-permute-start | bytes 1572872 | tf_op jit(solution)/shard_map/ppermute | solution.py:20
  52.0 10.6 %collective-permute-start.3 = (bf16[512,256]{1,0:T(8,128)(2,1)S(1)}, bf16[512,256]{1,0:T(8,128)(2,1)S(1)}, u32[]{:S(2)}, u32[]{:S(2)}) collective-permute-start(bf16[512,256]{1,0:T(8,128)(2,1)S(1)} %get-tuple-element.39), channel_id=1, source_target_pairs={{2,0},{3,1},{4,2},{5,3},{6,4},{7,5},{10,8},{11,9},{12,10},{13,11},... | collective-permute-start | bytes 786440 | tf_op jit(solution)/shard_map/ppermute | solution.py:15
  64.9 9.8 %collective-permute-start.4 = (bf16[512,256]{1,0:T(8,128)(2,1)S(1)}, bf16[512,256]{1,0:T(8,128)(2,1)S(1)}, u32[]{:S(2)}, u32[]{:S(2)}) collective-permute-start(bf16[512,256]{1,0:T(8,128)(2,1)S(1)} %get-tuple-element.53), channel_id=1, source_target_pairs={{0,2},{1,3},{2,4},{3,5},{4,6},{5,7},{8,10},{9,11},{10,12},{11,13},... | collective-permute-start | bytes 786440 | tf_op jit(solution)/shard_map/ppermute | solution.py:15
  75.1 8.9 %collective-permute-start.5 = (bf16[512,256]{1,0:T(8,128)(2,1)S(1)}, bf16[512,256]{1,0:T(8,128)(2,1)S(1)}, u32[]{:S(2)}, u32[]{:S(2)}) collective-permute-start(bf16[512,256]{1,0:T(8,128)(2,1)S(1)} %shard_map.83), channel_id=1, source_target_pairs={{0,2},{1,3},{2,4},{3,5},{4,6},{5,7},{8,10},{9,11},{10,12},{11,13},... | collective-permute-start | bytes 786440 | tf_op jit(solution)/shard_map/ppermute | solution.py:15
  84.5 8.3 %collective-permute-start.6 = (bf16[512,256]{1,0:T(8,128)(2,1)S(1)}, bf16[512,256]{1,0:T(8,128)(2,1)S(1)}, u32[]{:S(2)}, u32[]{:S(2)}) collective-permute-start(bf16[512,256]{1,0:T(8,128)(2,1)S(1)} %shard_map.84), channel_id=1, source_target_pairs={{0,2},{1,3},{2,4},{3,5},{4,6},{5,7},{8,10},{9,11},{10,12},{11,13},... | collective-permute-start | bytes 786440 | tf_op jit(solution)/shard_map/ppermute | solution.py:15
  93.5 8.3 %collective-permute-start.7 = (bf16[512,256]{1,0:T(8,128)(2,1)S(1)}, bf16[512,256]{1,0:T(8,128)(2,1)S(1)}, u32[]{:S(2)}, u32[]{:S(2)}) collective-permute-start(bf16[512,256]{1,0:T(8,128)(2,1)S(1)} %get-tuple-element.56), channel_id=1, source_target_pairs={{2,0},{3,1},{4,2},{5,3},{6,4},{7,5},{10,8},{11,9},{12,10},{13,11},... | collective-permute-start | bytes 786440 | tf_op jit(solution)/shard_map/ppermute | solution.py:15
  102.2 8.8 %collective-permute-start.8 = (bf16[512,256]{1,0:T(8,128)(2,1)S(1)}, bf16[512,256]{1,0:T(8,128)(2,1)S(1)}, u32[]{:S(2)}, u32[]{:S(2)}) collective-permute-start(bf16[512,256]{1,0:T(8,128)(2,1)S(1)} %shard_map.86), channel_id=1, source_target_pairs={{2,0},{3,1},{4,2},{5,3},{6,4},{7,5},{10,8},{11,9},{12,10},{13,11},... | collective-permute-start | bytes 786440 | tf_op jit(solution)/shard_map/ppermute | solution.py:15
  111.4 11.0 %copy-start.6 = (s32[2]{0:T(128)S(1)}, s32[2]{0:T(128)}, u32[]{:S(2)}) copy-start(s32[2]{0:T(128)} %param.9) | copy-start | bytes 28
  111.4 8.3 %collective-permute-start.9 = (bf16[512,256]{1,0:T(8,128)(2,1)S(1)}, bf16[512,256]{1,0:T(8,128)(2,1)S(1)}, u32[]{:S(2)}, u32[]{:S(2)}) collective-permute-start(bf16[512,256]{1,0:T(8,128)(2,1)S(1)} %shard_map.87), channel_id=1, source_target_pairs={{2,0},{3,1},{4,2},{5,3},{6,4},{7,5},{10,8},{11,9},{12,10},{13,11},... | collective-permute-start | bytes 786440 | tf_op jit(solution)/shard_map/ppermute | solution.py:15
  120.5 3.4 %collective-permute-start.10 = (bf16[512,256]{1,0:T(8,128)(2,1)S(1)}, bf16[512,256]{1,0:T(8,128)(2,1)S(1)}, u32[]{:S(2)}, u32[]{:S(2)}) collective-permute-start(bf16[512,256]{1,0:T(8,128)(2,1)S(1)} %get-tuple-element.58), channel_id=1, source_target_pairs={{0,1},{1,0},{2,3},{3,2},{4,5},{5,4},{6,7},{7,6},{8,9},{9,8},{10,11... | collective-permute-start | bytes 786440 | tf_op jit(solution)/shard_map/ppermute | solution.py:20
  126.2 19.2 %all-to-all-start.2 = ((bf16[4,2,64,1024]{3,2,1,0:T(8,128)(2,1)}), bf16[4,2,64,1024]{3,2,1,0:T(8,128)(2,1)S(1)}, u32[]{:S(2)}, u32[]{:S(2)}) async-start(bf16[4,2,64,1024]{3,2,1,0:T(8,128)(2,1)} %shard_map.89), calls=%async_computation.2 | async-start | bytes 2097152 | tf_op jit(solution)/shard_map/all_to_all | solution.py:33
  130.9 19.3 %copy-start.3 = (bf16[256,512]{1,0:T(8,128)(2,1)S(1)}, bf16[256,512]{1,0:T(8,128)(2,1)}, u32[]{:S(2)}) copy-start(bf16[256,512]{1,0:T(8,128)(2,1)} %copy.19) | copy-start | bytes 786436
  146.3 17.7 %all-to-all-start.3 = ((bf16[16,8,1024]{2,1,0:T(8,128)(2,1)}), bf16[16,8,1024]{2,1,0:T(8,128)(2,1)S(1)}, u32[]{:S(2)}, u32[]{:S(2)}) async-start(bf16[16,8,1024]{2,1,0:T(8,128)(2,1)} %bitcast.16), calls=%async_computation.3 | async-start | bytes 524288 | tf_op jit(solution)/shard_map/all_to_all | solution.py:33

commit v4 on v3

--- a/solution.py
+++ b/solution.py
@@ -58,6 +58,19 @@
     lr, li, rr, ri = left[0], left[1], right[0], right[1]
     out[0] = (mul(lr, rr) - mul(li, ri)).astype(BF16)
     out[1] = (mul(lr, ri) + mul(li, rr)).astype(BF16)
+
+
+def rows_kernel(place, masks, rows, out):
+    copies, count, n = out.shape
+    blocks = masks.shape[1]
+    tile = n // blocks
+    here = (place[0] * count) // tile
+    for j in range(blocks):
+        at = slice(j * tile, (j + 1) * tile)
+        present = masks[here, j].astype(F32)
+        masked = (rows[:, at].astype(F32) * present).astype(BF16)
+        for i in range(copies):
+            out[i, :, at] = masked
 
 
 def split_kernel(core, own, block):
@@ -76,13 +89,9 @@
 
 
 def begin_kernel(core, own_c, got_c, g, src, first, following, c, ct, base, start, send):
-    outer, inner, rows, _ = own_c.shape
     here = core[0]
-    for i in range(outer):
-        for j in range(inner):
-            at = (j * outer + i) * rows
-            c[here, at : at + rows] = own_c[i, j]
-            c[1 - here, at : at + rows] = got_c[i, j]
+    c[here] = own_c[...]
+    c[1 - here] = got_c[...]
     base_a = src[0].astype(F32) + mul(c[0], first[...])
     base[...] = base_a
     ct[0] = c[0].T
@@ -155,7 +164,7 @@
 
 def density_kernel(core, weights, kept, got, out):
     n, _ = kept.shape
-    outer, inner, rows, _ = out.shape
+    nx, near, ny, far, rows, _ = out.shape
     here = weights[core[0]]
     there = weights[1 - core[0]]
     real = jnp.zeros((n, n), F32)
@@ -167,17 +176,19 @@
         imag = imag + mul_transposed(scaled, turned(w))
     real = real.astype(BF16)
     imag = imag.astype(BF16)
-    for i in range(outer):
-        for j in range(inner):
-            first = (j * outer + i) * rows
-            out[i, j, :, :n] = real[first : first + rows]
-            out[i, j, :, n:] = imag[first : first + rows]
-
-
-def call(kernel, out_shapes, *operands, scratch=(), flops=0, smem=0, limit=24):
+    for y in range(ny):
+        for x in range(nx):
+            for h in range(far):
+                for l in range(near):
+                    at = (((y * nx + x) * far + h) * near + l) * rows
+                    out[x, l, y, h, :, :n] = real[at : at + rows]
+                    out[x, l, y, h, :, n:] = imag[at : at + rows]
+
+
+def call(kernel, out_shapes, *operands, scratch=(), flops=0, smem=0, limit=24, placed=True):
     whole = pl.BlockSpec(memory_space=pltpu.VMEM)
     scalars = pl.BlockSpec(memory_space=pltpu.SMEM)
-    outs = [pltpu.VMEM(s, d) for s, d in out_shapes]
+    outs = [pltpu.VMEM(s, d) if placed else jax.ShapeDtypeStruct(s, d) for s, d in out_shapes]
     operands = list(operands[:smem]) + [pltpu.with_memory_space_constraint(o, pltpu.VMEM) for o in operands[smem:]]
     result = pl.pallas_call(
         kernel,
@@ -203,9 +214,10 @@
     cols = 2 * modes
     devices = lax.axis_size("energy")
     ny, nx, nz = energy_grid(devices)
-    at = lambda y, x, z: (y * nx + x) * nz + z
-    along_x = [[at(y, x, z) for x in range(nx)] for y in range(ny) for z in range(nz)]
-    along_yz = [[at(y, x, z) for y in range(ny) for z in range(nz)] for x in range(nx)]
+    near, far = 2, nz // 2
+    at = lambda y, x, h, l: ((y * nx + x) * far + h) * near + l
+    along_xl = [[at(y, x, h, l) for x in range(nx) for l in range(near)] for y in range(ny) for h in range(far)]
+    along_yh = [[at(y, x, h, l) for y in range(ny) for h in range(far)] for x in range(nx) for l in range(near)]
     rows = coupling.shape[1]
     tile = n // masks.shape[1]
     vec = (n, cols)
@@ -215,14 +227,12 @@
     core = lax.rem(lax.axis_index("slab"), 2)
     which = core.reshape(1)
 
-    some = jnp.tile(coupling[0], (ny * nz, 1))
-    some, green_local, incident = lax.optimization_barrier((some, green_local, incident))
+    place = lax.axis_index("energy").reshape(1)
+    mine = call(
+        rows_kernel, [((devices, rows, n), BF16)], place, masks[0], coupling[0], smem=2, placed=False
+    )
+    own_c = exchange(mine, None).reshape(n, n)
     own_g, own_s = green_local[:, 0], incident[:, 0].reshape(count, n, cols)
-    some = exchange(some, along_yz)
-    by_row = jnp.repeat(masks[0].astype(BF16), tile, axis=0).reshape(ny, nx, nz * rows, -1)
-    here = lax.rem(lax.axis_index("energy") // nz, nx)
-    here = lax.dynamic_index_in_dim(by_row, here, 1, keepdims=False)
-    some = some.reshape(ny, nz * rows, n) * jnp.repeat(here, tile, axis=2)
 
     got_g = swap(call(split_kernel, [(mat, BF16)], which, own_g, smem=1))
     got_s = swap(call(split_kernel, [(vec, BF16)], which, own_s, smem=1))
@@ -231,10 +241,8 @@
         [((2, *mat), BF16), ((2, *vec), BF16), (vec, BF16), (vec, BF16)],
         which, own_g, got_g, own_s, got_s, smem=1, flops=4 * unit,
     )
-    some = jnp.broadcast_to(some[None], (nx, *some.shape))
-    some, send = lax.optimization_barrier((some, send))
-    own_c = exchange(some, along_x)
     following = chip_hop(send, -1)
+    own_c, following = lax.optimization_barrier((own_c, following))
     got_c = swap(own_c)
 
     hops = lax.axis_size("slab") // 2 - 1
@@ -270,11 +278,13 @@
     got = swap(send)
     weights = fermi(energy_index, 4.0 / (count * devices * modes))
     partial = call(
-        density_kernel, [((nx, ny, nz * rows, 2 * n), BF16)], which, weights, kept, got, smem=2, flops=8 * unit
-    )
-    parts = exchange(partial, along_x)
+        density_kernel,
+        [((nx, near, ny, far, rows, 2 * n), BF16)],
+        which, weights, kept, got, smem=2, flops=8 * unit,
+    )
+    parts = exchange(partial.reshape(nx * near, ny * far, rows, 2 * n), along_xl)
     summed = jnp.sum(parts.astype(F32), axis=0).astype(BF16)
-    parts = exchange(summed.reshape(ny * nz, rows, 2 * n), along_yz)
+    parts = exchange(summed, along_yh)
     density = jnp.sum(parts.astype(F32), axis=0).reshape(1, rows, 2, n)
 
     wave = ordered(core, kept, got)

time: 165 us -> 163 us (0.988)
  blocking collectives: 12.7 us -> 0 us
  starting transfers between devices: 44.7 us -> 55 us
  waiting for transfers between devices: 76.7 us -> 71.3 us
  local copies, waits for them, and re-layouts: 6.53 us -> 10.2 us
  Pallas kernels: 19.7 us -> 21.8 us
    all_to_all x1 -> x0, blocking collectives: 12.7 us -> none  [exchange(): lax.all_to_all(block, 'energy', 0, 0, axis_index_groups=groups, tiled=True)]
    all_to_all x3, starting transfers between devices: 21.9 us -> 30.5 us  [exchange(): lax.all_to_all(block, 'energy', 0, 0, axis_index_groups=groups, tiled=True)]
    ppermute x7, waiting for transfers between devices: 39.4 us -> 30.8 us  [chip_hop(): return lax.ppermute(block, 'slab', route)]
    unnamed x19 -> x24, local copies, waits for them, and re-layouts: 4.36 us -> 8.37 us
    ppermute x4, waiting for transfers between devices: 1.48 us -> 4.65 us  [swap(): return lax.ppermute(block, 'slab', route)]
    pallas_call x14 -> x15, Pallas kernels: 19.7 us -> 21.8 us  [call(): pl.pallas_call(kernel, out_shape=outs, in_specs=[scalars] * smem + [whole...]
    ppermute x7, starting transfers between devices: 14.8 us -> 16.6 us  [chip_hop(): return lax.ppermute(block, 'slab', route)]
  transfers between devices with their start and end apart: 14 -> 14, of which waited for: 11 -> 12; matrix products, arithmetic and copies ran while one was open for 3% -> 3% of each run, Pallas kernels for 5% -> 8%
where the time goes in v4:
time: 163 us; the launch traced here: 162 us
  waiting for transfers between devices  71.3 us (44%)
  starting transfers between devices  55 us (34%)
  Pallas kernels  21.8 us (13%)
  local copies, waits for them, and re-layouts  10.2 us (6%)
  other arithmetic  2.51 us (2%)
    all_to_all x3, waiting for transfers between devices, exchange(): lax.all_to_all(block, 'energy', 0, 0, axis_index_groups=groups, tiled=True)  35.9 us
    ppermute x7, waiting for transfers between devices, chip_hop(): return lax.ppermute(block, 'slab', route)  30.8 us
    all_to_all x3, starting transfers between devices, exchange(): lax.all_to_all(block, 'energy', 0, 0, axis_index_groups=groups, tiled=True)  30.5 us
    pallas_call x15, Pallas kernels, call(): pl.pallas_call(kernel, out_shape=outs, in_specs=[scalars] * smem + [whole...  21.8 us
    ppermute x7, starting transfers between devices, chip_hop(): return lax.ppermute(block, 'slab', route)  16.6 us
    unnamed x24, local copies, waits for them, and re-layouts  8.37 us
    ppermute x4, starting transfers between devices, swap(): return lax.ppermute(block, 'slab', route)  8 us
    ppermute x4, waiting for transfers between devices, swap(): return lax.ppermute(block, 'slab', route)  4.65 us
  transfers between devices with their start and end apart: 14, of which 12 were waited for; matrix products, arithmetic and copies ran while one was open for 3% of the time, Pallas kernels for 8%

profile of v4, /device:TPU:8, one launch (start us, length us, event | category | flops | bytes accessed | tf_op | source)
XLA Modules:
  0.0 162.4 jit_solution(15650759049646236328)
XLA Ops:
  0.6 0.0 copy-start.9
  0.7 0.0 copy-start
  0.7 1.6 copy-done
  2.3 1.0 shard_map.76
  3.3 2.0 %collective-permute-start = (bf16[2,512,512]{2,1,0:T(8,128)(2,1)}, bf16[2,512,512]{2,1,0:T(8,128)(2,1)}, u32[]{:S(2)}, u32[]{:S(2)}) collective-permute-start(bf16[2,512,512]{2,1,0:T(8,128)(2,1)} %shard_map.76), channel_id=1, source_target_pairs={{0,1},{1,0},{2,3},{3,2},{4,5},{5,4},{6,7},{7,6},{8,9},{9,8},{10,11... | collective-permute-start | bytes 3145736 | tf_op jit(solution)/shard_map/ppermute | solution.py:20
  5.4 1.4 shard_map.79
  6.8 18.1 %all-to-all-start = ((bf16[64,8,512]{2,1,0:T(8,128)(2,1)}), bf16[64,8,512]{2,1,0:T(8,128)(2,1)S(1)}, u32[]{:S(2)}, u32[]{:S(2)}) async-start(bf16[64,8,512]{2,1,0:T(8,128)(2,1)} %shard_map.79), calls=%async_computation | async-start | bytes 1048576 | tf_op jit(solution)/shard_map/all_to_all | solution.py:33
  25.0 1.4 reshape_squeeze.3.own.own_s
  26.4 2.1 %collective-permute-start.1 = (bf16[512,256]{1,0:T(8,128)(2,1)S(1)}, bf16[512,256]{1,0:T(8,128)(2,1)S(1)}, u32[]{:S(2)}, u32[]{:S(2)}) collective-permute-start(bf16[512,256]{1,0:T(8,128)(2,1)S(1)} %shard_map.77), channel_id=1, source_target_pairs={{0,1},{1,0},{2,3},{3,2},{4,5},{5,4},{6,7},{7,6},{8,9},{9,8},{10,11... | collective-permute-start | bytes 786440 | tf_op jit(solution)/shard_map/ppermute | solution.py:20
  28.5 1.3 collective-permute-done.1.got_s
  29.8 0.0 collective-permute-done.got_g
  29.8 2.8 %shard_map.78 = (bf16[2,2,512,512]{3,2,1,0:T(8,128)(2,1)S(1)}, bf16[2,512,256]{2,1,0:T(8,128)(2,1)S(1)}, bf16[512,256]{1,0:T(8,128)(2,1)S(1)}, bf16[512,256]{1,0:T(8,128)(2,1)}) custom-call(s32[1]{0:T(128)} %bitcast.core, bf16[2,2,512,512]{3,2,1,0:T(8,128)(2,1)S(1)} %bitcast.25, bf16[2,512,512]{2,1,0:T(8,128)(2,1)} %collective-permute-done.got_g, ...), custom_call_target="tpu_custom_call" | custom-call | flops 536870912 | bytes 1048576 | tf_op jit(solution)/shard_map/pallas_call | solution.py:193
  32.6 1.4 copy-done.2
  34.0 0.8 copy-done.5
  34.8 3.2 %collective-permute-start.2 = (bf16[512,256]{1,0:T(8,128)(2,1)}, bf16[512,256]{1,0:T(8,128)(2,1)S(1)}, u32[]{:S(2)}, u32[]{:S(2)}) collective-permute-start(bf16[512,256]{1,0:T(8,128)(2,1)} %get-tuple-element.29), channel_id=1, source_target_pairs={{2,0},{3,1},{4,2},{5,3},{6,4},{7,5},{10,8},{11,9},{12,10},{13,11},... | collective-permute-start | bytes 786440 | tf_op jit(solution)/shard_map/ppermute | solution.py:15
  38.0 10.9 %all-to-all-done = bf16[64,8,512]{2,1,0:T(8,128)(2,1)S(1)} async-done(((bf16[64,8,512]{2,1,0:T(8,128)(2,1)}), bf16[64,8,512]{2,1,0:T(8,128)(2,1)S(1)}, u32[]{:S(2)}, u32[]{:S(2)}) %all-to-all-start) | async-done | bytes 524320 | tf_op jit(solution)/shard_map/all_to_all | solution.py:33
  49.0 0.0 collective-permute-done.2.following
  49.0 1.9 %collective-permute-start.3 = (bf16[512,512]{1,0:T(8,128)(2,1)S(1)}, bf16[512,512]{1,0:T(8,128)(2,1)S(1)}, u32[]{:S(2)}, u32[]{:S(2)}) collective-permute-start(bf16[512,512]{1,0:T(8,128)(2,1)S(1)} %bitcast.26), channel_id=1, source_target_pairs={{0,1},{1,0},{2,3},{3,2},{4,5},{5,4},{6,7},{7,6},{8,9},{9,8},{10,11... | collective-permute-start | bytes 1572872 | tf_op jit(solution)/shard_map/ppermute | solution.py:20
  50.9 1.9 %collective-permute-done.3.got_c = bf16[512,512]{1,0:T(8,128)(2,1)S(1)} collective-permute-done((bf16[512,512]{1,0:T(8,128)(2,1)S(1)}, bf16[512,512]{1,0:T(8,128)(2,1)S(1)}, u32[]{:S(2)}, u32[]{:S(2)}) %collective-permute-start.3) | collective-permute-done | bytes 524320 | tf_op jit(solution)/shard_map/ppermute | solution.py:20
  52.8 1.6 copy-done.3
  54.4 1.0 copy-done.6
  55.4 2.3 %shard_map.80 = (bf16[2,512,512]{2,1,0:T(8,128)(2,1)S(1)}, bf16[2,512,512]{2,1,0:T(8,128)(2,1)S(1)}, f32[512,256]{1,0:T(8,128)S(1)}, f32[512,256]{1,0:T(8,128)S(1)}, bf16[512,256]{1,0:T(8,128)(2,1)S(1)}) custom-call(s32[1]{0:T(128)} %bitcast.core, bf16[512,512]{1,0:T(8,128)(2,1)S(1)} %bitcast.27, bf16[512,512]{1,0:T(8,128)(2,1)S(1)} %collective-permute-done.3.got_c, ...), custom_call_target="tpu_custom_call" | custom-call | flops 1073741824 | bytes 1048576 | tf_op jit(solution)/shard_map/pallas_call | solution.py:193
  57.7 2.5 %collective-permute-start.4 = (bf16[512,256]{1,0:T(8,128)(2,1)S(1)}, bf16[512,256]{1,0:T(8,128)(2,1)S(1)}, u32[]{:S(2)}, u32[]{:S(2)}) collective-permute-start(bf16[512,256]{1,0:T(8,128)(2,1)S(1)} %get-tuple-element.47), channel_id=1, source_target_pairs={{0,2},{1,3},{2,4},{3,5},{4,6},{5,7},{8,10},{9,11},{10,12},{11,13},... | collective-permute-start | bytes 786440 | tf_op jit(solution)/shard_map/ppermute | solution.py:15
  60.1 0.0 copy-done.4
  60.2 2.3 %shard_map.82 = (bf16[2,512,512]{2,1,0:T(8,128)(2,1)S(1)}, bf16[2,512,512]{2,1,0:T(8,128)(2,1)S(1)}) custom-call(bf16[2,2,512,512]{3,2,1,0:T(8,128)(2,1)S(1)} %copy-done.4, bf16[2,512,512]{2,1,0:T(8,128)(2,1)S(1)} %get-tuple-element.37.ct), custom_call_target="tpu_custom_call" | custom-call | flops 2147483648 | bytes 1048576 | tf_op jit(solution)/shard_map/pallas_call | solution.py:193
  62.5 5.4 %collective-permute-done.4.arrived = bf16[512,256]{1,0:T(8,128)(2,1)S(1)} collective-permute-done((bf16[512,256]{1,0:T(8,128)(2,1)S(1)}, bf16[512,256]{1,0:T(8,128)(2,1)S(1)}, u32[]{:S(2)}, u32[]{:S(2)}) %collective-permute-start.4) | collective-permute-done | bytes 262176 | tf_op jit(solution)/shard_map/ppermute | solution.py:15
  67.9 0.4 shard_map.84
  68.4 2.5 %collective-permute-start.5 = (bf16[512,256]{1,0:T(8,128)(2,1)S(1)}, bf16[512,256]{1,0:T(8,128)(2,1)S(1)}, u32[]{:S(2)}, u32[]{:S(2)}) collective-permute-start(bf16[512,256]{1,0:T(8,128)(2,1)S(1)} %shard_map.84), channel_id=1, source_target_pairs={{0,2},{1,3},{2,4},{3,5},{4,6},{5,7},{8,10},{9,11},{10,12},{11,13},... | collective-permute-start | bytes 786440 | tf_op jit(solution)/shard_map/ppermute | solution.py:15
  70.8 2.3 %shard_map.81 = (bf16[2,512,512]{2,1,0:T(8,128)(2,1)S(1)}, bf16[2,512,512]{2,1,0:T(8,128)(2,1)S(1)}, bf16[2,512,512]{2,1,0:T(8,128)(2,1)S(1)}) custom-call(bf16[2,2,512,512]{3,2,1,0:T(8,128)(2,1)S(1)} %copy-done.4, bf16[2,512,512]{2,1,0:T(8,128)(2,1)S(1)} %get-tuple-element.34.c), custom_call_target="tpu_custom_call" | custom-call | flops 2147483648 | bytes 1048576 | tf_op jit(solution)/shard_map/pallas_call | solution.py:193
  73.2 0.0 copy-start.7
  73.2 4.6 %collective-permute-done.5.arrived = bf16[512,256]{1,0:T(8,128)(2,1)S(1)} collective-permute-done((bf16[512,256]{1,0:T(8,128)(2,1)S(1)}, bf16[512,256]{1,0:T(8,128)(2,1)S(1)}, u32[]{:S(2)}, u32[]{:S(2)}) %collective-permute-start.5) | collective-permute-done | bytes 262176 | tf_op jit(solution)/shard_map/ppermute | solution.py:15
  77.8 0.4 shard_map.85
  78.2 2.5 %collective-permute-start.6 = (bf16[512,256]{1,0:T(8,128)(2,1)S(1)}, bf16[512,256]{1,0:T(8,128)(2,1)S(1)}, u32[]{:S(2)}, u32[]{:S(2)}) collective-permute-start(bf16[512,256]{1,0:T(8,128)(2,1)S(1)} %shard_map.85), channel_id=1, source_target_pairs={{0,2},{1,3},{2,4},{3,5},{4,6},{5,7},{8,10},{9,11},{10,12},{11,13},... | collective-permute-start | bytes 786440 | tf_op jit(solution)/shard_map/ppermute | solution.py:15
  80.7 4.0 %shard_map.83 = (bf16[2,512,512]{2,1,0:T(8,128)(2,1)S(1)}, bf16[2,512,512]{2,1,0:T(8,128)(2,1)S(1)}, f32[512,256]{1,0:T(8,128)S(1)}, f32[512,256]{1,0:T(8,128)S(1)}) custom-call(bf16[2,2,512,512]{3,2,1,0:T(8,128)(2,1)S(1)} %copy-done.4, bf16[2,512,512]{2,1,0:T(8,128)(2,1)S(1)} %get-tuple-element.38.step_a, ...), custom_call_target="tpu_custom_call" | custom-call | flops 3221225472 | bytes 1048576 | tf_op jit(solution)/shard_map/pallas_call | solution.py:193
  84.7 2.0 %collective-permute-done.6.flux = bf16[512,256]{1,0:T(8,128)(2,1)S(1)} collective-permute-done((bf16[512,256]{1,0:T(8,128)(2,1)S(1)}, bf16[512,256]{1,0:T(8,128)(2,1)S(1)}, u32[]{:S(2)}, u32[]{:S(2)}) %collective-permute-start.6) | collective-permute-done | bytes 262176 | tf_op jit(solution)/shard_map/ppermute | solution.py:15
  86.7 0.7 shard_map.86
  87.4 1.9 %collective-permute-start.7 = (bf16[512,256]{1,0:T(8,128)(2,1)S(1)}, bf16[512,256]{1,0:T(8,128)(2,1)S(1)}, u32[]{:S(2)}, u32[]{:S(2)}) collective-permute-start(bf16[512,256]{1,0:T(8,128)(2,1)S(1)} %get-tuple-element.50), channel_id=1, source_target_pairs={{2,0},{3,1},{4,2},{5,3},{6,4},{7,5},{10,8},{11,9},{12,10},{13,11},... | collective-permute-start | bytes 786440 | tf_op jit(solution)/shard_map/ppermute | solution.py:15
  89.3 6.3 %collective-permute-done.7.arrived = bf16[512,256]{1,0:T(8,128)(2,1)S(1)} collective-permute-done((bf16[512,256]{1,0:T(8,128)(2,1)S(1)}, bf16[512,256]{1,0:T(8,128)(2,1)S(1)}, u32[]{:S(2)}, u32[]{:S(2)}) %collective-permute-start.7) | collective-permute-done | bytes 262176 | tf_op jit(solution)/shard_map/ppermute | solution.py:15
  95.7 0.4 shard_map.87
  96.1 2.1 %collective-permute-start.8 = (bf16[512,256]{1,0:T(8,128)(2,1)S(1)}, bf16[512,256]{1,0:T(8,128)(2,1)S(1)}, u32[]{:S(2)}, u32[]{:S(2)}) collective-permute-start(bf16[512,256]{1,0:T(8,128)(2,1)S(1)} %shard_map.87), channel_id=1, source_target_pairs={{2,0},{3,1},{4,2},{5,3},{6,4},{7,5},{10,8},{11,9},{12,10},{13,11},... | collective-permute-start | bytes 786440 | tf_op jit(solution)/shard_map/ppermute | solution.py:15
  98.2 6.2 %collective-permute-done.8.arrived = bf16[512,256]{1,0:T(8,128)(2,1)S(1)} collective-permute-done((bf16[512,256]{1,0:T(8,128)(2,1)S(1)}, bf16[512,256]{1,0:T(8,128)(2,1)S(1)}, u32[]{:S(2)}, u32[]{:S(2)}) %collective-permute-start.8) | collective-permute-done | bytes 262176 | tf_op jit(solution)/shard_map/ppermute | solution.py:15
  104.4 0.4 shard_map.88
  104.8 0.0 copy-start.10
  104.8 1.9 %collective-permute-start.9 = (bf16[512,256]{1,0:T(8,128)(2,1)S(1)}, bf16[512,256]{1,0:T(8,128)(2,1)S(1)}, u32[]{:S(2)}, u32[]{:S(2)}) collective-permute-start(bf16[512,256]{1,0:T(8,128)(2,1)S(1)} %shard_map.88), channel_id=1, source_target_pairs={{2,0},{3,1},{4,2},{5,3},{6,4},{7,5},{10,8},{11,9},{12,10},{13,11},... | collective-permute-start | bytes 786440 | tf_op jit(solution)/shard_map/ppermute | solution.py:15
  106.8 6.3 %collective-permute-done.9.arrived = bf16[512,256]{1,0:T(8,128)(2,1)S(1)} collective-permute-done((bf16[512,256]{1,0:T(8,128)(2,1)S(1)}, bf16[512,256]{1,0:T(8,128)(2,1)S(1)}, u32[]{:S(2)}, u32[]{:S(2)}) %collective-permute-start.9) | collective-permute-done | bytes 262176 | tf_op jit(solution)/shard_map/ppermute | solution.py:15
  113.1 0.8 shard_map.89
  113.9 1.9 %collective-permute-start.10 = (bf16[512,256]{1,0:T(8,128)(2,1)S(1)}, bf16[512,256]{1,0:T(8,128)(2,1)S(1)}, u32[]{:S(2)}, u32[]{:S(2)}) collective-permute-start(bf16[512,256]{1,0:T(8,128)(2,1)S(1)} %get-tuple-element.52), channel_id=1, source_target_pairs={{0,1},{1,0},{2,3},{3,2},{4,5},{5,4},{6,7},{7,6},{8,9},{9,8},{10,11... | collective-permute-start | bytes 786440 | tf_op jit(solution)/shard_map/ppermute | solution.py:20
  115.8 1.5 collective-permute-done.10.got
  117.3 2.3 %shard_map.90 = bf16[4,2,2,4,8,1024]{5,4,3,2,1,0:T(8,128)(2,1)} custom-call(s32[1]{0:T(128)} %bitcast.core, f32[2]{0:T(128)S(1)} %add_divide_fusion.weights, bf16[512,256]{1,0:T(8,128)(2,1)S(1)} %get-tuple-element.51.kept, bf16[512,256]{1,0:T(8,128)(2,1)S(1)} %collective-permute-done.10.got), custom_call_target="tpu_custom_call" | custom-call | flops 1073741824 | bytes 1048576 | tf_op jit(solution)/shard_map/pallas_call | solution.py:193
  119.6 4.3 %all-to-all-start.1 = ((bf16[8,8,8,1024]{3,2,1,0:T(8,128)(2,1)}), bf16[8,8,8,1024]{3,2,1,0:T(8,128)(2,1)S(1)}, u32[]{:S(2)}, u32[]{:S(2)}) async-start(bf16[8,8,8,1024]{3,2,1,0:T(8,128)(2,1)} %bitcast.14), calls=%async_computation.1 | async-start | bytes 2097152 | tf_op jit(solution)/shard_map/all_to_all | solution.py:33
  124.0 0.1 stack.18
  124.0 0.1 copy.15
  124.2 0.1 stack.19
  124.3 0.1 copy.16
  124.4 0.3 fusion
  124.7 0.3 fusion.1
  125.1 14.9 %all-to-all-done.1 = bf16[8,8,8,1024]{3,2,1,0:T(8,128)(2,1)S(1)} async-done(((bf16[8,8,8,1024]{3,2,1,0:T(8,128)(2,1)}), bf16[8,8,8,1024]{3,2,1,0:T(8,128)(2,1)S(1)}, u32[]{:S(2)}, u32[]{:S(2)}) %all-to-all-start.1) | async-done | bytes 1048608 | tf_op jit(solution)/shard_map/all_to_all | solution.py:33
  140.0 0.8 reduce_sum.21
  140.8 8.0 %all-to-all-start.2 = ((bf16[8,8,1024]{2,1,0:T(8,128)(2,1)}), bf16[8,8,1024]{2,1,0:T(8,128)(2,1)S(1)}, u32[]{:S(2)}, u32[]{:S(2)}) async-start(bf16[8,8,1024]{2,1,0:T(8,128)(2,1)} %reduce_sum.21), calls=%async_computation.2 | async-start | bytes 262144 | tf_op jit(solution)/shard_map/all_to_all | solution.py:33
  148.8 0.1 pad_maximum_fusion.1
  148.8 1.3 copy.13
  150.2 1.6 pad_maximum_fusion
  151.7 10.0 %all-to-all-done.2 = bf16[8,8,1024]{2,1,0:T(8,128)(2,1)S(1)} async-done(((bf16[8,8,1024]{2,1,0:T(8,128)(2,1)}), bf16[8,8,1024]{2,1,0:T(8,128)(2,1)S(1)}, u32[]{:S(2)}, u32[]{:S(2)}) %all-to-all-start.2) | async-done | bytes 131104 | tf_op jit(solution)/shard_map/all_to_all | solution.py:33
  161.8 0.6 copy.14
  (16 shorter events, 0.1 us)
Async XLA Ops:
  0.6 4.7 %copy-start.9 = (s32[1,4,4]{2,1,0:T(4,128)S(1)}, s32[1,4,4]{2,1,0:T(4,128)}, u32[]{:S(2)}) copy-start(s32[1,4,4]{2,1,0:T(4,128)} %param.7) | copy-start | bytes 196
  0.6 4.7 %copy-start.8 = (bf16[1,8,512]{2,1,0:T(8,128)(2,1)S(1)}, bf16[1,8,512]{2,1,0:T(8,128)(2,1)}, u32[]{:S(2)}) copy-start(bf16[1,8,512]{2,1,0:T(8,128)(2,1)} %param.6) | copy-start | bytes 24580
  0.7 1.6 copy-start
  3.3 26.5 %copy-start.1 = (bf16[2,1,2,512,512]{4,3,2,1,0:T(8,128)(2,1)S(1)}, bf16[2,1,2,512,512]{4,3,2,1,0:T(8,128)(2,1)}, u32[]{:S(2)}) copy-start(bf16[2,1,2,512,512]{4,3,2,1,0:T(8,128)(2,1)} %param.5) | copy-start | bytes 6291460
  3.3 26.5 %collective-permute-start = (bf16[2,512,512]{2,1,0:T(8,128)(2,1)}, bf16[2,512,512]{2,1,0:T(8,128)(2,1)}, u32[]{:S(2)}, u32[]{:S(2)}) collective-permute-start(bf16[2,512,512]{2,1,0:T(8,128)(2,1)} %shard_map.76), channel_id=1, source_target_pairs={{0,1},{1,0},{2,3},{3,2},{4,5},{5,4},{6,7},{7,6},{8,9},{9,8},{10,11... | collective-permute-start | bytes 3145736 | tf_op jit(solution)/shard_map/ppermute | solution.py:20
  6.8 42.2 %all-to-all-start = ((bf16[64,8,512]{2,1,0:T(8,128)(2,1)}), bf16[64,8,512]{2,1,0:T(8,128)(2,1)S(1)}, u32[]{:S(2)}, u32[]{:S(2)}) async-start(bf16[64,8,512]{2,1,0:T(8,128)(2,1)} %shard_map.79), calls=%async_computation | async-start | bytes 1048576 | tf_op jit(solution)/shard_map/all_to_all | solution.py:33
  26.4 3.4 %collective-permute-start.1 = (bf16[512,256]{1,0:T(8,128)(2,1)S(1)}, bf16[512,256]{1,0:T(8,128)(2,1)S(1)}, u32[]{:S(2)}, u32[]{:S(2)}) collective-permute-start(bf16[512,256]{1,0:T(8,128)(2,1)S(1)} %shard_map.77), channel_id=1, source_target_pairs={{0,1},{1,0},{2,3},{3,2},{4,5},{5,4},{6,7},{7,6},{8,9},{9,8},{10,11... | collective-permute-start | bytes 786440 | tf_op jit(solution)/shard_map/ppermute | solution.py:20
  32.6 1.4 copy-start.2
  34.0 0.8 copy-start.5
  34.8 14.2 %collective-permute-start.2 = (bf16[512,256]{1,0:T(8,128)(2,1)}, bf16[512,256]{1,0:T(8,128)(2,1)S(1)}, u32[]{:S(2)}, u32[]{:S(2)}) collective-permute-start(bf16[512,256]{1,0:T(8,128)(2,1)} %get-tuple-element.29), channel_id=1, source_target_pairs={{2,0},{3,1},{4,2},{5,3},{6,4},{7,5},{10,8},{11,9},{12,10},{13,11},... | collective-permute-start | bytes 786440 | tf_op jit(solution)/shard_map/ppermute | solution.py:15
  49.0 3.8 %collective-permute-start.3 = (bf16[512,512]{1,0:T(8,128)(2,1)S(1)}, bf16[512,512]{1,0:T(8,128)(2,1)S(1)}, u32[]{:S(2)}, u32[]{:S(2)}) collective-permute-start(bf16[512,512]{1,0:T(8,128)(2,1)S(1)} %bitcast.26), channel_id=1, source_target_pairs={{0,1},{1,0},{2,3},{3,2},{4,5},{5,4},{6,7},{7,6},{8,9},{9,8},{10,11... | collective-permute-start | bytes 1572872 | tf_op jit(solution)/shard_map/ppermute | solution.py:20
  52.8 1.6 copy-start.3
  54.3 1.0 copy-start.6
  55.4 4.8 %copy-start.4 = (bf16[2,2,512,512]{3,2,1,0:T(8,128)(2,1)S(1)}, bf16[2,2,512,512]{3,2,1,0:T(8,128)(2,1)}, u32[]{:S(2)}) copy-start(bf16[2,2,512,512]{3,2,1,0:T(8,128)(2,1)} %copy-done.2) | copy-start | bytes 6291460
  57.7 10.2 %collective-permute-start.4 = (bf16[512,256]{1,0:T(8,128)(2,1)S(1)}, bf16[512,256]{1,0:T(8,128)(2,1)S(1)}, u32[]{:S(2)}, u32[]{:S(2)}) collective-permute-start(bf16[512,256]{1,0:T(8,128)(2,1)S(1)} %get-tuple-element.47), channel_id=1, source_target_pairs={{0,2},{1,3},{2,4},{3,5},{4,6},{5,7},{8,10},{9,11},{10,12},{11,13},... | collective-permute-start | bytes 786440 | tf_op jit(solution)/shard_map/ppermute | solution.py:15
  68.4 9.4 %collective-permute-start.5 = (bf16[512,256]{1,0:T(8,128)(2,1)S(1)}, bf16[512,256]{1,0:T(8,128)(2,1)S(1)}, u32[]{:S(2)}, u32[]{:S(2)}) collective-permute-start(bf16[512,256]{1,0:T(8,128)(2,1)S(1)} %shard_map.84), channel_id=1, source_target_pairs={{0,2},{1,3},{2,4},{3,5},{4,6},{5,7},{8,10},{9,11},{10,12},{11,13},... | collective-permute-start | bytes 786440 | tf_op jit(solution)/shard_map/ppermute | solution.py:15
  73.2 7.5 %copy-start.7 = (bf16[2,512,256]{2,1,0:T(8,128)(2,1)S(1)}, bf16[2,512,256]{2,1,0:T(8,128)(2,1)}, u32[]{:S(2)}) copy-start(bf16[2,512,256]{2,1,0:T(8,128)(2,1)} %copy-done.5) | copy-start | bytes 1572868
  78.2 8.5 %collective-permute-start.6 = (bf16[512,256]{1,0:T(8,128)(2,1)S(1)}, bf16[512,256]{1,0:T(8,128)(2,1)S(1)}, u32[]{:S(2)}, u32[]{:S(2)}) collective-permute-start(bf16[512,256]{1,0:T(8,128)(2,1)S(1)} %shard_map.85), channel_id=1, source_target_pairs={{0,2},{1,3},{2,4},{3,5},{4,6},{5,7},{8,10},{9,11},{10,12},{11,13},... | collective-permute-start | bytes 786440 | tf_op jit(solution)/shard_map/ppermute | solution.py:15
  87.4 8.3 %collective-permute-start.7 = (bf16[512,256]{1,0:T(8,128)(2,1)S(1)}, bf16[512,256]{1,0:T(8,128)(2,1)S(1)}, u32[]{:S(2)}, u32[]{:S(2)}) collective-permute-start(bf16[512,256]{1,0:T(8,128)(2,1)S(1)} %get-tuple-element.50), channel_id=1, source_target_pairs={{2,0},{3,1},{4,2},{5,3},{6,4},{7,5},{10,8},{11,9},{12,10},{13,11},... | collective-permute-start | bytes 786440 | tf_op jit(solution)/shard_map/ppermute | solution.py:15
  96.1 8.3 %collective-permute-start.8 = (bf16[512,256]{1,0:T(8,128)(2,1)S(1)}, bf16[512,256]{1,0:T(8,128)(2,1)S(1)}, u32[]{:S(2)}, u32[]{:S(2)}) collective-permute-start(bf16[512,256]{1,0:T(8,128)(2,1)S(1)} %shard_map.87), channel_id=1, source_target_pairs={{2,0},{3,1},{4,2},{5,3},{6,4},{7,5},{10,8},{11,9},{12,10},{13,11},... | collective-permute-start | bytes 786440 | tf_op jit(solution)/shard_map/ppermute | solution.py:15
  104.8 11.0 %copy-start.10 = (s32[2]{0:T(128)S(1)}, s32[2]{0:T(128)}, u32[]{:S(2)}) copy-start(s32[2]{0:T(128)} %param.9) | copy-start | bytes 28
  104.8 8.3 %collective-permute-start.9 = (bf16[512,256]{1,0:T(8,128)(2,1)S(1)}, bf16[512,256]{1,0:T(8,128)(2,1)S(1)}, u32[]{:S(2)}, u32[]{:S(2)}) collective-permute-start(bf16[512,256]{1,0:T(8,128)(2,1)S(1)} %shard_map.88), channel_id=1, source_target_pairs={{2,0},{3,1},{4,2},{5,3},{6,4},{7,5},{10,8},{11,9},{12,10},{13,11},... | collective-permute-start | bytes 786440 | tf_op jit(solution)/shard_map/ppermute | solution.py:15
  113.9 3.4 %collective-permute-start.10 = (bf16[512,256]{1,0:T(8,128)(2,1)S(1)}, bf16[512,256]{1,0:T(8,128)(2,1)S(1)}, u32[]{:S(2)}, u32[]{:S(2)}) collective-permute-start(bf16[512,256]{1,0:T(8,128)(2,1)S(1)} %get-tuple-element.52), channel_id=1, source_target_pairs={{0,1},{1,0},{2,3},{3,2},{4,5},{5,4},{6,7},{7,6},{8,9},{9,8},{10,11... | collective-permute-start | bytes 786440 | tf_op jit(solution)/shard_map/ppermute | solution.py:20
  119.6 20.4 %all-to-all-start.1 = ((bf16[8,8,8,1024]{3,2,1,0:T(8,128)(2,1)}), bf16[8,8,8,1024]{3,2,1,0:T(8,128)(2,1)S(1)}, u32[]{:S(2)}, u32[]{:S(2)}) async-start(bf16[8,8,8,1024]{3,2,1,0:T(8,128)(2,1)} %bitcast.14), calls=%async_computation.1 | async-start | bytes 2097152 | tf_op jit(solution)/shard_map/all_to_all | solution.py:33
  140.8 20.9 %all-to-all-start.2 = ((bf16[8,8,1024]{2,1,0:T(8,128)(2,1)}), bf16[8,8,1024]{2,1,0:T(8,128)(2,1)S(1)}, u32[]{:S(2)}, u32[]{:S(2)}) async-start(bf16[8,8,1024]{2,1,0:T(8,128)(2,1)} %reduce_sum.21), calls=%async_computation.2 | async-start | bytes 262144 | tf_op jit(solution)/shard_map/all_to_all | solution.py:33

commit v5 on v4

--- a/solution.py
+++ b/solution.py
@@ -88,14 +88,31 @@
     first[...] = apply(g[1, 0], g[1, 1], src[1]).astype(BF16)
 
 
-def begin_kernel(core, own_c, got_c, g, src, first, following, c, ct, base, start, send):
+def compose(g, ct, step_a, through, step_b):
+    step_a[0] = mul(ct[0], g[0, 0]).astype(BF16)
+    step_a[1] = mul(ct[0], g[0, 1]).astype(BF16)
+    step_b[0] = mul(ct[1], g[1, 0]).astype(BF16)
+    step_b[1] = mul(ct[1], g[1, 1]).astype(BF16)
+    product(step_b, step_a, through)
+
+
+def begin_kernel(
+    core, g_far, src_far, own_c, got_c, first, following,
+    g, src, c, ct, base, start, send, step_a, through, step_b, g_sem, src_sem,
+):
+    src_copy = pltpu.make_async_copy(src_far, src, src_sem)
+    g_copy = pltpu.make_async_copy(g_far, g, g_sem)
+    src_copy.start()
+    g_copy.start()
     here = core[0]
     c[here] = own_c[...]
     c[1 - here] = got_c[...]
+    ct[0] = c[0].T
+    ct[1] = c[1].T
+    src_copy.wait()
     base_a = src[0].astype(F32) + mul(c[0], first[...])
     base[...] = base_a
-    ct[0] = c[0].T
-    ct[1] = c[1].T
+    g_copy.wait()
     field = apply(g[0, 0], g[0, 1], base_a.astype(BF16)).astype(BF16)
     summed = src[1].astype(F32) + mul(c[1], following[...]) + mul(ct[0], field)
     field = apply(g[1, 0], g[1, 1], summed.astype(BF16)).astype(BF16)
@@ -103,13 +120,15 @@
     start[...] = flux
     send[...] = flux.astype(BF16)
 
-
-def compose_kernel(g, ct, step_a, through, step_b):
-    step_a[0] = mul(ct[0], g[0, 0]).astype(BF16)
-    step_a[1] = mul(ct[0], g[0, 1]).astype(BF16)
-    step_b[0] = mul(ct[1], g[1, 0]).astype(BF16)
-    step_b[1] = mul(ct[1], g[1, 1]).astype(BF16)
-    product(step_b, step_a, through)
+    @pl.when(here == 1)
+    def _():
+        compose(g, ct, step_a, through, step_b)
+
+
+def compose_kernel(core, g, ct, step_a_in, through_in, step_a, through, step_b):
+    @pl.when(core[0] == 0)
+    def _():
+        compose(g, ct, step_a, through, step_b)
 
 
 def compose_back_kernel(g, c, back_a, back_b, back):
@@ -164,7 +183,7 @@
 
 def density_kernel(core, weights, kept, got, out):
     n, _ = kept.shape
-    nx, near, ny, far, rows, _ = out.shape
+    outer, inner, rows, _ = out.shape
     here = weights[core[0]]
     there = weights[1 - core[0]]
     real = jnp.zeros((n, n), F32)
@@ -176,28 +195,31 @@
         imag = imag + mul_transposed(scaled, turned(w))
     real = real.astype(BF16)
     imag = imag.astype(BF16)
-    for y in range(ny):
-        for x in range(nx):
-            for h in range(far):
-                for l in range(near):
-                    at = (((y * nx + x) * far + h) * near + l) * rows
-                    out[x, l, y, h, :, :n] = real[at : at + rows]
-                    out[x, l, y, h, :, n:] = imag[at : at + rows]
-
-
-def call(kernel, out_shapes, *operands, scratch=(), flops=0, smem=0, limit=24, placed=True):
+    for i in range(outer):
+        for j in range(inner):
+            first = (j * outer + i) * rows
+            out[i, j, :, :n] = real[first : first + rows]
+            out[i, j, :, n:] = imag[first : first + rows]
+
+
+def call(kernel, out_shapes, *operands, scratch=(), flops=0, smem=0, far=0, plain=0, aliases=None):
     whole = pl.BlockSpec(memory_space=pltpu.VMEM)
-    scalars = pl.BlockSpec(memory_space=pltpu.SMEM)
-    outs = [pltpu.VMEM(s, d) if placed else jax.ShapeDtypeStruct(s, d) for s, d in out_shapes]
-    operands = list(operands[:smem]) + [pltpu.with_memory_space_constraint(o, pltpu.VMEM) for o in operands[smem:]]
+    specs = [pl.BlockSpec(memory_space=pltpu.SMEM)] * smem + [pl.BlockSpec(memory_space=pltpu.HBM)] * far
+    outs = [pltpu.VMEM(s, d) if i >= plain else jax.ShapeDtypeStruct(s, d) for i, (s, d) in enumerate(out_shapes)]
+    first = smem + far
+    space = lambda i: pltpu.HBM if i < first else pltpu.VMEM
+    operands = [
+        o if i < smem else pltpu.with_memory_space_constraint(o, space(i)) for i, o in enumerate(operands)
+    ]
     result = pl.pallas_call(
         kernel,
         out_shape=outs,
-        in_specs=[scalars] * smem + [whole] * (len(operands) - smem),
+        in_specs=specs + [whole] * (len(operands) - first),
         out_specs=[whole] * len(outs),
-        scratch_shapes=[pltpu.VMEM(s, d) for s, d in scratch],
+        scratch_shapes=list(scratch),
         cost_estimate=pl.CostEstimate(flops=flops, transcendentals=0, bytes_accessed=1 << 20),
-        compiler_params=pltpu.CompilerParams(vmem_limit_bytes=limit << 20),
+        compiler_params=pltpu.CompilerParams(vmem_limit_bytes=24 << 20),
+        input_output_aliases=aliases or {},
     )(*operands)
     return result if len(outs) > 1 else result[0]
 
@@ -214,10 +236,9 @@
     cols = 2 * modes
     devices = lax.axis_size("energy")
     ny, nx, nz = energy_grid(devices)
-    near, far = 2, nz // 2
-    at = lambda y, x, h, l: ((y * nx + x) * far + h) * near + l
-    along_xl = [[at(y, x, h, l) for x in range(nx) for l in range(near)] for y in range(ny) for h in range(far)]
-    along_yh = [[at(y, x, h, l) for y in range(ny) for h in range(far)] for x in range(nx) for l in range(near)]
+    at = lambda y, x, z: (y * nx + x) * nz + z
+    along_x = [[at(y, x, z) for x in range(nx)] for y in range(ny) for z in range(nz)]
+    along_yz = [[at(y, x, z) for y in range(ny) for z in range(nz)] for x in range(nx)]
     rows = coupling.shape[1]
     tile = n // masks.shape[1]
     vec = (n, cols)
@@ -229,7 +250,7 @@
 
     place = lax.axis_index("energy").reshape(1)
     mine = call(
-        rows_kernel, [((devices, rows, n), BF16)], place, masks[0], coupling[0], smem=2, placed=False
+        rows_kernel, [((devices, rows, n), BF16)], place, masks[0], coupling[0], smem=2, plain=1
     )
     own_c = exchange(mine, None).reshape(n, n)
     own_g, own_s = green_local[:, 0], incident[:, 0].reshape(count, n, cols)
@@ -239,21 +260,24 @@
     green, source, first, send = call(
         first_kernel,
         [((2, *mat), BF16), ((2, *vec), BF16), (vec, BF16), (vec, BF16)],
-        which, own_g, got_g, own_s, got_s, smem=1, flops=4 * unit,
+        which, own_g, got_g, own_s, got_s, smem=1, plain=2, flops=4 * unit,
     )
     following = chip_hop(send, -1)
     own_c, following = lax.optimization_barrier((own_c, following))
     got_c = swap(own_c)
 
     hops = lax.axis_size("slab") // 2 - 1
-    c, ct, base, start, send = call(
+    green, source, c, ct, base, start, send, step_a, through = call(
         begin_kernel,
-        [(mat, BF16), (mat, BF16), (vec, F32), (vec, F32), (vec, BF16)],
-        which, own_c, got_c, green, source, first, following, smem=1, flops=8 * unit,
+        [((2, *mat), BF16), ((2, *vec), BF16), (mat, BF16), (mat, BF16), (vec, F32), (vec, F32), (vec, BF16)]
+        + [(mat, BF16)] * 2,
+        which, green, source, own_c, got_c, first, following,
+        smem=1, far=2, scratch=[pltpu.VMEM(mat, BF16)] + [pltpu.SemaphoreType.DMA(())] * 2, flops=8 * unit,
     )
     flux = chip_hop(send, 1)
     step_a, through = call(
-        compose_kernel, [(mat, BF16), (mat, BF16)], green, ct, scratch=[(mat, BF16)], flops=16 * n**3
+        compose_kernel, [(mat, BF16), (mat, BF16)], which, green, ct, step_a, through,
+        smem=1, scratch=[pltpu.VMEM(mat, BF16)], flops=16 * n**3, aliases={3: 0, 4: 1},
     )
     for _ in range(hops - 1):
         send = call(hop_kernel, [(vec, BF16)], through, start, flux, flops=2 * unit)
@@ -278,13 +302,11 @@
     got = swap(send)
     weights = fermi(energy_index, 4.0 / (count * devices * modes))
     partial = call(
-        density_kernel,
-        [((nx, near, ny, far, rows, 2 * n), BF16)],
-        which, weights, kept, got, smem=2, flops=8 * unit,
-    )
-    parts = exchange(partial.reshape(nx * near, ny * far, rows, 2 * n), along_xl)
+        density_kernel, [((nx, ny, nz * rows, 2 * n), BF16)], which, weights, kept, got, smem=2, flops=8 * unit
+    )
+    parts = exchange(partial, along_x)
     summed = jnp.sum(parts.astype(F32), axis=0).astype(BF16)
-    parts = exchange(summed, along_yh)
+    parts = exchange(summed.reshape(ny * nz, rows, 2 * n), along_yz)
     density = jnp.sum(parts.astype(F32), axis=0).reshape(1, rows, 2, n)
 
     wave = ordered(core, kept, got)

time: 163 us -> 166 us (1.018)
  waiting for transfers between devices: 71.3 us -> 73.5 us
  local copies, waits for them, and re-layouts: 10.2 us -> 8.2 us
    ppermute x7, waiting for transfers between devices: 30.8 us -> 33.7 us  [chip_hop(): return lax.ppermute(block, 'slab', route)]
    unnamed x24 -> x18, local copies, waits for them, and re-layouts: 8.37 us -> 5.71 us
  transfers between devices with their start and end apart: 14 -> 14, of which waited for: 12 -> 12; matrix products, arithmetic and copies ran while one was open for 3% -> 4% of each run, Pallas kernels for 8% -> 8%
where the time goes in v5:
time: 166 us; the launch traced here: 165 us
  waiting for transfers between devices  73.5 us (44%)
  starting transfers between devices  55.8 us (34%)
  Pallas kernels  23.3 us (14%)
  local copies, waits for them, and re-layouts  8.2 us (5%)
  other arithmetic  2.62 us (2%)
    all_to_all x3, waiting for transfers between devices, exchange(): lax.all_to_all(block, 'energy', 0, 0, axis_index_groups=groups, tiled=True)  35.2 us
    ppermute x7, waiting for transfers between devices, chip_hop(): return lax.ppermute(block, 'slab', route)  33.7 us
    all_to_all x3, starting transfers between devices, exchange(): lax.all_to_all(block, 'energy', 0, 0, axis_index_groups=groups, tiled=True)  30.4 us
    pallas_call x15, Pallas kernels, call(): pl.pallas_call(kernel, out_shape=outs, in_specs=specs + [whole] * (len(op...  23.3 us
    ppermute x7, starting transfers between devices, chip_hop(): return lax.ppermute(block, 'slab', route)  17.4 us
    ppermute x4, starting transfers between devices, swap(): return lax.ppermute(block, 'slab', route)  8 us
    unnamed x18, local copies, waits for them, and re-layouts  5.71 us
    ppermute x4, waiting for transfers between devices, swap(): return lax.ppermute(block, 'slab', route)  4.65 us
  transfers between devices with their start and end apart: 14, of which 12 were waited for; matrix products, arithmetic and copies ran while one was open for 4% of the time, Pallas kernels for 8%

profile of v5, /device:TPU:8, one launch (start us, length us, event | category | flops | bytes accessed | tf_op | source)
XLA Modules:
  0.0 165.1 jit_solution(13404514638209957238)
XLA Ops:
  0.6 0.0 copy-start.5
  0.6 0.0 copy-start.4
  0.7 0.0 copy-start
  0.7 1.6 copy-done
  2.3 1.0 shard_map.76
  3.3 2.0 %collective-permute-start = (bf16[2,512,512]{2,1,0:T(8,128)(2,1)}, bf16[2,512,512]{2,1,0:T(8,128)(2,1)}, u32[]{:S(2)}, u32[]{:S(2)}) collective-permute-start(bf16[2,512,512]{2,1,0:T(8,128)(2,1)} %shard_map.76), channel_id=1, source_target_pairs={{0,1},{1,0},{2,3},{3,2},{4,5},{5,4},{6,7},{7,6},{8,9},{9,8},{10,11... | collective-permute-start | bytes 3145736 | tf_op jit(solution)/shard_map/ppermute | solution.py:20
  5.3 0.0 copy-done.5
  5.3 0.0 copy-done.4
  5.3 1.4 shard_map.79
  6.8 18.1 %all-to-all-start = ((bf16[64,8,512]{2,1,0:T(8,128)(2,1)}), bf16[64,8,512]{2,1,0:T(8,128)(2,1)S(1)}, u32[]{:S(2)}, u32[]{:S(2)}) async-start(bf16[64,8,512]{2,1,0:T(8,128)(2,1)} %shard_map.79), calls=%async_computation | async-start | bytes 1048576 | tf_op jit(solution)/shard_map/all_to_all | solution.py:33
  24.9 1.4 reshape_squeeze.3.own.own_s
  26.4 2.1 %collective-permute-start.1 = (bf16[512,256]{1,0:T(8,128)(2,1)S(1)}, bf16[512,256]{1,0:T(8,128)(2,1)S(1)}, u32[]{:S(2)}, u32[]{:S(2)}) collective-permute-start(bf16[512,256]{1,0:T(8,128)(2,1)S(1)} %shard_map.77), channel_id=1, source_target_pairs={{0,1},{1,0},{2,3},{3,2},{4,5},{5,4},{6,7},{7,6},{8,9},{9,8},{10,11... | collective-permute-start | bytes 786440 | tf_op jit(solution)/shard_map/ppermute | solution.py:20
  28.5 1.3 collective-permute-done.1.got_s
  29.8 0.0 collective-permute-done.got_g
  29.8 0.0 copy-done.1
  29.8 2.8 %shard_map.78 = (bf16[2,2,512,512]{3,2,1,0:T(8,128)(2,1)S(1)}, bf16[2,512,256]{2,1,0:T(8,128)(2,1)S(1)}, bf16[512,256]{1,0:T(8,128)(2,1)S(1)}, bf16[512,256]{1,0:T(8,128)(2,1)}) custom-call(s32[1]{0:T(128)} %bitcast.core, bf16[2,2,512,512]{3,2,1,0:T(8,128)(2,1)S(1)} %bitcast.25, bf16[2,512,512]{2,1,0:T(8,128)(2,1)} %collective-permute-done.got_g, ...), custom_call_target="tpu_custom_call" | custom-call | flops 536870912 | bytes 1048576 | tf_op jit(solution)/shard_map/pallas_call | solution.py:214
  32.6 1.3 copy-done.2
  33.9 0.8 copy-done.3
  34.7 3.2 %collective-permute-start.2 = (bf16[512,256]{1,0:T(8,128)(2,1)}, bf16[512,256]{1,0:T(8,128)(2,1)S(1)}, u32[]{:S(2)}, u32[]{:S(2)}) collective-permute-start(bf16[512,256]{1,0:T(8,128)(2,1)} %get-tuple-element.34), channel_id=1, source_target_pairs={{2,0},{3,1},{4,2},{5,3},{6,4},{7,5},{10,8},{11,9},{12,10},{13,11},... | collective-permute-start | bytes 786440 | tf_op jit(solution)/shard_map/ppermute | solution.py:15
  38.0 11.0 %all-to-all-done = bf16[64,8,512]{2,1,0:T(8,128)(2,1)S(1)} async-done(((bf16[64,8,512]{2,1,0:T(8,128)(2,1)}), bf16[64,8,512]{2,1,0:T(8,128)(2,1)S(1)}, u32[]{:S(2)}, u32[]{:S(2)}) %all-to-all-start) | async-done | bytes 524320 | tf_op jit(solution)/shard_map/all_to_all | solution.py:33
  48.9 0.0 collective-permute-done.2.following
  48.9 1.9 %collective-permute-start.3 = (bf16[512,512]{1,0:T(8,128)(2,1)S(1)}, bf16[512,512]{1,0:T(8,128)(2,1)S(1)}, u32[]{:S(2)}, u32[]{:S(2)}) collective-permute-start(bf16[512,512]{1,0:T(8,128)(2,1)S(1)} %bitcast.26), channel_id=1, source_target_pairs={{0,1},{1,0},{2,3},{3,2},{4,5},{5,4},{6,7},{7,6},{8,9},{9,8},{10,11... | collective-permute-start | bytes 1572872 | tf_op jit(solution)/shard_map/ppermute | solution.py:20
  50.9 1.9 %collective-permute-done.3.got_c = bf16[512,512]{1,0:T(8,128)(2,1)S(1)} collective-permute-done((bf16[512,512]{1,0:T(8,128)(2,1)S(1)}, bf16[512,512]{1,0:T(8,128)(2,1)S(1)}, u32[]{:S(2)}, u32[]{:S(2)}) %collective-permute-start.3) | collective-permute-done | bytes 524320 | tf_op jit(solution)/shard_map/ppermute | solution.py:20
  52.7 3.7 %shard_map.80 = (bf16[2,2,512,512]{3,2,1,0:T(8,128)(2,1)S(1)}, bf16[2,512,256]{2,1,0:T(8,128)(2,1)S(1)}, bf16[2,512,512]{2,1,0:T(8,128)(2,1)S(1)}, bf16[2,512,51...) custom-call(s32[1]{0:T(128)} %bitcast.core, ...), custom_call_target="tpu_custom_call" | custom-call | flops 1073741824 | bytes 1048576 | tf_op jit(solution)/shard_map/pallas_call | solution.py:214
  56.5 2.5 %collective-permute-start.4 = (bf16[512,256]{1,0:T(8,128)(2,1)S(1)}, bf16[512,256]{1,0:T(8,128)(2,1)S(1)}, u32[]{:S(2)}, u32[]{:S(2)}) collective-permute-start(bf16[512,256]{1,0:T(8,128)(2,1)S(1)} %get-tuple-element.55), channel_id=1, source_target_pairs={{0,2},{1,3},{2,4},{3,5},{4,6},{5,7},{8,10},{9,11},{10,12},{11,13},... | collective-permute-start | bytes 786440 | tf_op jit(solution)/shard_map/ppermute | solution.py:15
  58.9 2.3 %shard_map.82 = (bf16[2,512,512]{2,1,0:T(8,128)(2,1)S(1)}, bf16[2,512,512]{2,1,0:T(8,128)(2,1)S(1)}) custom-call(s32[1]{0:T(128)} %bitcast.core, bf16[2,2,512,512]{3,2,1,0:T(8,128)(2,1)S(1)} %get-tuple-element.38.g, bf16[2,512,512]{2,1,0:T(8,128)(2,1)S(1)} %get-tuple-element.42.ct, ...), custom_call_target="tpu_custom_call", output_to_operand_aliasing={{0}: (3, {}), {1}: (4, {})} | custom-call | flops 2147483648 | bytes 1048576 | tf_op jit(solution)/shard_map/pallas_call | solution.py:214
  61.3 4.7 %collective-permute-done.4.arrived = bf16[512,256]{1,0:T(8,128)(2,1)S(1)} collective-permute-done((bf16[512,256]{1,0:T(8,128)(2,1)S(1)}, bf16[512,256]{1,0:T(8,128)(2,1)S(1)}, u32[]{:S(2)}, u32[]{:S(2)}) %collective-permute-start.4) | collective-permute-done | bytes 262176 | tf_op jit(solution)/shard_map/ppermute | solution.py:15
  66.0 0.4 shard_map.84
  66.4 2.5 %collective-permute-start.5 = (bf16[512,256]{1,0:T(8,128)(2,1)S(1)}, bf16[512,256]{1,0:T(8,128)(2,1)S(1)}, u32[]{:S(2)}, u32[]{:S(2)}) collective-permute-start(bf16[512,256]{1,0:T(8,128)(2,1)S(1)} %shard_map.84), channel_id=1, source_target_pairs={{0,2},{1,3},{2,4},{3,5},{4,6},{5,7},{8,10},{9,11},{10,12},{11,13},... | collective-permute-start | bytes 786440 | tf_op jit(solution)/shard_map/ppermute | solution.py:15
  68.9 2.4 %shard_map.81 = (bf16[2,512,512]{2,1,0:T(8,128)(2,1)S(1)}, bf16[2,512,512]{2,1,0:T(8,128)(2,1)S(1)}, bf16[2,512,512]{2,1,0:T(8,128)(2,1)S(1)}) custom-call(bf16[2,2,512,512]{3,2,1,0:T(8,128)(2,1)S(1)} %get-tuple-element.38.g, bf16[2,512,512]{2,1,0:T(8,128)(2,1)S(1)} %get-tuple-element.39.c), custom_call_target="tpu_custom_call" | custom-call | flops 2147483648 | bytes 1048576 | tf_op jit(solution)/shard_map/pallas_call | solution.py:214
  71.2 5.9 %collective-permute-done.5.arrived = bf16[512,256]{1,0:T(8,128)(2,1)S(1)} collective-permute-done((bf16[512,256]{1,0:T(8,128)(2,1)S(1)}, bf16[512,256]{1,0:T(8,128)(2,1)S(1)}, u32[]{:S(2)}, u32[]{:S(2)}) %collective-permute-start.5) | collective-permute-done | bytes 262176 | tf_op jit(solution)/shard_map/ppermute | solution.py:15
  77.1 0.4 shard_map.85
  77.6 2.6 %collective-permute-start.6 = (bf16[512,256]{1,0:T(8,128)(2,1)S(1)}, bf16[512,256]{1,0:T(8,128)(2,1)S(1)}, u32[]{:S(2)}, u32[]{:S(2)}) collective-permute-start(bf16[512,256]{1,0:T(8,128)(2,1)S(1)} %shard_map.85), channel_id=1, source_target_pairs={{0,2},{1,3},{2,4},{3,5},{4,6},{5,7},{8,10},{9,11},{10,12},{11,13},... | collective-permute-start | bytes 786440 | tf_op jit(solution)/shard_map/ppermute | solution.py:15
  80.2 4.1 %shard_map.83 = (bf16[2,512,512]{2,1,0:T(8,128)(2,1)S(1)}, bf16[2,512,512]{2,1,0:T(8,128)(2,1)S(1)}, f32[512,256]{1,0:T(8,128)S(1)}, f32[512,256]{1,0:T(8,128)S(1)}) custom-call(bf16[2,2,512,512]{3,2,1,0:T(8,128)(2,1)S(1)} %get-tuple-element.38.g, bf16[2,512,512]{2,1,0:T(8,128)(2,1)S(1)} %get-tuple-element.45.step_a, ...), custom_call_target="tpu_custom_call" | custom-call | flops 3221225472 | bytes 1048576 | tf_op jit(solution)/shard_map/pallas_call | solution.py:214
  84.3 3.5 %collective-permute-done.6.flux = bf16[512,256]{1,0:T(8,128)(2,1)S(1)} collective-permute-done((bf16[512,256]{1,0:T(8,128)(2,1)S(1)}, bf16[512,256]{1,0:T(8,128)(2,1)S(1)}, u32[]{:S(2)}, u32[]{:S(2)}) %collective-permute-start.6) | collective-permute-done | bytes 262176 | tf_op jit(solution)/shard_map/ppermute | solution.py:15
  87.9 0.7 shard_map.86
  88.6 1.9 %collective-permute-start.7 = (bf16[512,256]{1,0:T(8,128)(2,1)S(1)}, bf16[512,256]{1,0:T(8,128)(2,1)S(1)}, u32[]{:S(2)}, u32[]{:S(2)}) collective-permute-start(bf16[512,256]{1,0:T(8,128)(2,1)S(1)} %get-tuple-element.58), channel_id=1, source_target_pairs={{2,0},{3,1},{4,2},{5,3},{6,4},{7,5},{10,8},{11,9},{12,10},{13,11},... | collective-permute-start | bytes 786440 | tf_op jit(solution)/shard_map/ppermute | solution.py:15
  90.5 7.5 %collective-permute-done.7.arrived = bf16[512,256]{1,0:T(8,128)(2,1)S(1)} collective-permute-done((bf16[512,256]{1,0:T(8,128)(2,1)S(1)}, bf16[512,256]{1,0:T(8,128)(2,1)S(1)}, u32[]{:S(2)}, u32[]{:S(2)}) %collective-permute-start.7) | collective-permute-done | bytes 262176 | tf_op jit(solution)/shard_map/ppermute | solution.py:15
  98.0 0.4 shard_map.87
  98.5 2.2 %collective-permute-start.8 = (bf16[512,256]{1,0:T(8,128)(2,1)S(1)}, bf16[512,256]{1,0:T(8,128)(2,1)S(1)}, u32[]{:S(2)}, u32[]{:S(2)}) collective-permute-start(bf16[512,256]{1,0:T(8,128)(2,1)S(1)} %shard_map.87), channel_id=1, source_target_pairs={{2,0},{3,1},{4,2},{5,3},{6,4},{7,5},{10,8},{11,9},{12,10},{13,11},... | collective-permute-start | bytes 786440 | tf_op jit(solution)/shard_map/ppermute | solution.py:15
  100.7 6.3 %collective-permute-done.8.arrived = bf16[512,256]{1,0:T(8,128)(2,1)S(1)} collective-permute-done((bf16[512,256]{1,0:T(8,128)(2,1)S(1)}, bf16[512,256]{1,0:T(8,128)(2,1)S(1)}, u32[]{:S(2)}, u32[]{:S(2)}) %collective-permute-start.8) | collective-permute-done | bytes 262176 | tf_op jit(solution)/shard_map/ppermute | solution.py:15
  107.0 0.4 shard_map.88
  107.4 0.0 copy-start.7
  107.4 2.5 %collective-permute-start.9 = (bf16[512,256]{1,0:T(8,128)(2,1)S(1)}, bf16[512,256]{1,0:T(8,128)(2,1)S(1)}, u32[]{:S(2)}, u32[]{:S(2)}) collective-permute-start(bf16[512,256]{1,0:T(8,128)(2,1)S(1)} %shard_map.88), channel_id=1, source_target_pairs={{2,0},{3,1},{4,2},{5,3},{6,4},{7,5},{10,8},{11,9},{12,10},{13,11},... | collective-permute-start | bytes 786440 | tf_op jit(solution)/shard_map/ppermute | solution.py:15
  109.9 5.8 %collective-permute-done.9.arrived = bf16[512,256]{1,0:T(8,128)(2,1)S(1)} collective-permute-done((bf16[512,256]{1,0:T(8,128)(2,1)S(1)}, bf16[512,256]{1,0:T(8,128)(2,1)S(1)}, u32[]{:S(2)}, u32[]{:S(2)}) %collective-permute-start.9) | collective-permute-done | bytes 262176 | tf_op jit(solution)/shard_map/ppermute | solution.py:15
  115.7 0.8 shard_map.89
  116.5 1.9 %collective-permute-start.10 = (bf16[512,256]{1,0:T(8,128)(2,1)S(1)}, bf16[512,256]{1,0:T(8,128)(2,1)S(1)}, u32[]{:S(2)}, u32[]{:S(2)}) collective-permute-start(bf16[512,256]{1,0:T(8,128)(2,1)S(1)} %get-tuple-element.60), channel_id=1, source_target_pairs={{0,1},{1,0},{2,3},{3,2},{4,5},{5,4},{6,7},{7,6},{8,9},{9,8},{10,11... | collective-permute-start | bytes 786440 | tf_op jit(solution)/shard_map/ppermute | solution.py:20
  118.4 1.5 collective-permute-done.10.got
  119.9 2.3 %shard_map.90 = bf16[4,2,64,1024]{3,2,1,0:T(8,128)(2,1)} custom-call(s32[1]{0:T(128)} %bitcast.core, f32[2]{0:T(128)S(1)} %add_divide_fusion.weights, bf16[512,256]{1,0:T(8,128)(2,1)S(1)} %get-tuple-element.59.kept, bf16[512,256]{1,0:T(8,128)(2,1)S(1)} %collective-permute-done.10.got), custom_call_target="tpu_custom_call" | custom-call | flops 1073741824 | bytes 1048576 | tf_op jit(solution)/shard_map/pallas_call | solution.py:214
  122.2 3.7 %all-to-all-start.1 = ((bf16[4,2,64,1024]{3,2,1,0:T(8,128)(2,1)}), bf16[4,2,64,1024]{3,2,1,0:T(8,128)(2,1)S(1)}, u32[]{:S(2)}, u32[]{:S(2)}) async-start(bf16[4,2,64,1024]{3,2,1,0:T(8,128)(2,1)} %shard_map.90), calls=%async_computation.1 | async-start | bytes 2097152 | tf_op jit(solution)/shard_map/all_to_all | solution.py:33
  125.9 0.1 stack.18
  126.0 0.1 copy.17
  126.1 0.1 stack.19
  126.2 0.8 copy.18
  127.0 14.3 %all-to-all-done.1 = bf16[4,2,64,1024]{3,2,1,0:T(8,128)(2,1)S(1)} async-done(((bf16[4,2,64,1024]{3,2,1,0:T(8,128)(2,1)}), bf16[4,2,64,1024]{3,2,1,0:T(8,128)(2,1)S(1)}, u32[]{:S(2)}, u32[]{:S(2)}) %all-to-all-start.1) | async-done | bytes 1048608 | tf_op jit(solution)/shard_map/all_to_all | solution.py:33
  141.4 0.9 reduce_sum.21
  142.3 8.6 %all-to-all-start.2 = ((bf16[16,8,1024]{2,1,0:T(8,128)(2,1)}), bf16[16,8,1024]{2,1,0:T(8,128)(2,1)S(1)}, u32[]{:S(2)}, u32[]{:S(2)}) async-start(bf16[16,8,1024]{2,1,0:T(8,128)(2,1)} %bitcast.14), calls=%async_computation.2 | async-start | bytes 524288 | tf_op jit(solution)/shard_map/all_to_all | solution.py:33
  150.9 0.3 fusion
  151.3 0.3 fusion.1
  151.6 0.1 pad_maximum_fusion.1
  151.7 1.3 copy.15
  153.0 1.6 pad_maximum_fusion
  154.6 9.9 %all-to-all-done.2 = bf16[16,8,1024]{2,1,0:T(8,128)(2,1)S(1)} async-done(((bf16[16,8,1024]{2,1,0:T(8,128)(2,1)}), bf16[16,8,1024]{2,1,0:T(8,128)(2,1)S(1)}, u32[]{:S(2)}, u32[]{:S(2)}) %all-to-all-start.2) | async-done | bytes 262176 | tf_op jit(solution)/shard_map/all_to_all | solution.py:33
  164.5 0.6 copy.16
  (10 shorter events, 0.1 us)
Async XLA Ops:
  0.6 4.7 %copy-start.5 = (s32[1,4,4]{2,1,0:T(4,128)S(1)}, s32[1,4,4]{2,1,0:T(4,128)}, u32[]{:S(2)}) copy-start(s32[1,4,4]{2,1,0:T(4,128)} %param.7) | copy-start | bytes 196
  0.6 4.7 %copy-start.4 = (bf16[1,8,512]{2,1,0:T(8,128)(2,1)S(1)}, bf16[1,8,512]{2,1,0:T(8,128)(2,1)}, u32[]{:S(2)}) copy-start(bf16[1,8,512]{2,1,0:T(8,128)(2,1)} %param.6) | copy-start | bytes 24580
  0.7 1.6 copy-start
  3.3 26.5 %copy-start.1 = (bf16[2,1,2,512,512]{4,3,2,1,0:T(8,128)(2,1)S(1)}, bf16[2,1,2,512,512]{4,3,2,1,0:T(8,128)(2,1)}, u32[]{:S(2)}) copy-start(bf16[2,1,2,512,512]{4,3,2,1,0:T(8,128)(2,1)} %param.5) | copy-start | bytes 6291460
  3.3 26.5 %collective-permute-start = (bf16[2,512,512]{2,1,0:T(8,128)(2,1)}, bf16[2,512,512]{2,1,0:T(8,128)(2,1)}, u32[]{:S(2)}, u32[]{:S(2)}) collective-permute-start(bf16[2,512,512]{2,1,0:T(8,128)(2,1)} %shard_map.76), channel_id=1, source_target_pairs={{0,1},{1,0},{2,3},{3,2},{4,5},{5,4},{6,7},{7,6},{8,9},{9,8},{10,11... | collective-permute-start | bytes 3145736 | tf_op jit(solution)/shard_map/ppermute | solution.py:20
  6.8 42.2 %all-to-all-start = ((bf16[64,8,512]{2,1,0:T(8,128)(2,1)}), bf16[64,8,512]{2,1,0:T(8,128)(2,1)S(1)}, u32[]{:S(2)}, u32[]{:S(2)}) async-start(bf16[64,8,512]{2,1,0:T(8,128)(2,1)} %shard_map.79), calls=%async_computation | async-start | bytes 1048576 | tf_op jit(solution)/shard_map/all_to_all | solution.py:33
  26.4 3.4 %collective-permute-start.1 = (bf16[512,256]{1,0:T(8,128)(2,1)S(1)}, bf16[512,256]{1,0:T(8,128)(2,1)S(1)}, u32[]{:S(2)}, u32[]{:S(2)}) collective-permute-start(bf16[512,256]{1,0:T(8,128)(2,1)S(1)} %shard_map.77), channel_id=1, source_target_pairs={{0,1},{1,0},{2,3},{3,2},{4,5},{5,4},{6,7},{7,6},{8,9},{9,8},{10,11... | collective-permute-start | bytes 786440 | tf_op jit(solution)/shard_map/ppermute | solution.py:20
  32.6 1.3 copy-start.2
  33.9 0.8 copy-start.3
  34.7 14.2 %collective-permute-start.2 = (bf16[512,256]{1,0:T(8,128)(2,1)}, bf16[512,256]{1,0:T(8,128)(2,1)S(1)}, u32[]{:S(2)}, u32[]{:S(2)}) collective-permute-start(bf16[512,256]{1,0:T(8,128)(2,1)} %get-tuple-element.34), channel_id=1, source_target_pairs={{2,0},{3,1},{4,2},{5,3},{6,4},{7,5},{10,8},{11,9},{12,10},{13,11},... | collective-permute-start | bytes 786440 | tf_op jit(solution)/shard_map/ppermute | solution.py:15
  48.9 3.8 %collective-permute-start.3 = (bf16[512,512]{1,0:T(8,128)(2,1)S(1)}, bf16[512,512]{1,0:T(8,128)(2,1)S(1)}, u32[]{:S(2)}, u32[]{:S(2)}) collective-permute-start(bf16[512,512]{1,0:T(8,128)(2,1)S(1)} %bitcast.26), channel_id=1, source_target_pairs={{0,1},{1,0},{2,3},{3,2},{4,5},{5,4},{6,7},{7,6},{8,9},{9,8},{10,11... | collective-permute-start | bytes 1572872 | tf_op jit(solution)/shard_map/ppermute | solution.py:20
  56.5 9.5 %collective-permute-start.4 = (bf16[512,256]{1,0:T(8,128)(2,1)S(1)}, bf16[512,256]{1,0:T(8,128)(2,1)S(1)}, u32[]{:S(2)}, u32[]{:S(2)}) collective-permute-start(bf16[512,256]{1,0:T(8,128)(2,1)S(1)} %get-tuple-element.55), channel_id=1, source_target_pairs={{0,2},{1,3},{2,4},{3,5},{4,6},{5,7},{8,10},{9,11},{10,12},{11,13},... | collective-permute-start | bytes 786440 | tf_op jit(solution)/shard_map/ppermute | solution.py:15
  66.4 10.7 %collective-permute-start.5 = (bf16[512,256]{1,0:T(8,128)(2,1)S(1)}, bf16[512,256]{1,0:T(8,128)(2,1)S(1)}, u32[]{:S(2)}, u32[]{:S(2)}) collective-permute-start(bf16[512,256]{1,0:T(8,128)(2,1)S(1)} %shard_map.84), channel_id=1, source_target_pairs={{0,2},{1,3},{2,4},{3,5},{4,6},{5,7},{8,10},{9,11},{10,12},{11,13},... | collective-permute-start | bytes 786440 | tf_op jit(solution)/shard_map/ppermute | solution.py:15
  77.6 10.3 %collective-permute-start.6 = (bf16[512,256]{1,0:T(8,128)(2,1)S(1)}, bf16[512,256]{1,0:T(8,128)(2,1)S(1)}, u32[]{:S(2)}, u32[]{:S(2)}) collective-permute-start(bf16[512,256]{1,0:T(8,128)(2,1)S(1)} %shard_map.85), channel_id=1, source_target_pairs={{0,2},{1,3},{2,4},{3,5},{4,6},{5,7},{8,10},{9,11},{10,12},{11,13},... | collective-permute-start | bytes 786440 | tf_op jit(solution)/shard_map/ppermute | solution.py:15
  88.6 9.4 %collective-permute-start.7 = (bf16[512,256]{1,0:T(8,128)(2,1)S(1)}, bf16[512,256]{1,0:T(8,128)(2,1)S(1)}, u32[]{:S(2)}, u32[]{:S(2)}) collective-permute-start(bf16[512,256]{1,0:T(8,128)(2,1)S(1)} %get-tuple-element.58), channel_id=1, source_target_pairs={{2,0},{3,1},{4,2},{5,3},{6,4},{7,5},{10,8},{11,9},{12,10},{13,11},... | collective-permute-start | bytes 786440 | tf_op jit(solution)/shard_map/ppermute | solution.py:15
  98.5 8.5 %collective-permute-start.8 = (bf16[512,256]{1,0:T(8,128)(2,1)S(1)}, bf16[512,256]{1,0:T(8,128)(2,1)S(1)}, u32[]{:S(2)}, u32[]{:S(2)}) collective-permute-start(bf16[512,256]{1,0:T(8,128)(2,1)S(1)} %shard_map.87), channel_id=1, source_target_pairs={{2,0},{3,1},{4,2},{5,3},{6,4},{7,5},{10,8},{11,9},{12,10},{13,11},... | collective-permute-start | bytes 786440 | tf_op jit(solution)/shard_map/ppermute | solution.py:15
  107.4 11.0 %copy-start.7 = (s32[2]{0:T(128)S(1)}, s32[2]{0:T(128)}, u32[]{:S(2)}) copy-start(s32[2]{0:T(128)} %param.9) | copy-start | bytes 28
  107.4 8.3 %collective-permute-start.9 = (bf16[512,256]{1,0:T(8,128)(2,1)S(1)}, bf16[512,256]{1,0:T(8,128)(2,1)S(1)}, u32[]{:S(2)}, u32[]{:S(2)}) collective-permute-start(bf16[512,256]{1,0:T(8,128)(2,1)S(1)} %shard_map.88), channel_id=1, source_target_pairs={{2,0},{3,1},{4,2},{5,3},{6,4},{7,5},{10,8},{11,9},{12,10},{13,11},... | collective-permute-start | bytes 786440 | tf_op jit(solution)/shard_map/ppermute | solution.py:15
  116.5 3.4 %collective-permute-start.10 = (bf16[512,256]{1,0:T(8,128)(2,1)S(1)}, bf16[512,256]{1,0:T(8,128)(2,1)S(1)}, u32[]{:S(2)}, u32[]{:S(2)}) collective-permute-start(bf16[512,256]{1,0:T(8,128)(2,1)S(1)} %get-tuple-element.60), channel_id=1, source_target_pairs={{0,1},{1,0},{2,3},{3,2},{4,5},{5,4},{6,7},{7,6},{8,9},{9,8},{10,11... | collective-permute-start | bytes 786440 | tf_op jit(solution)/shard_map/ppermute | solution.py:20
  122.2 19.2 %all-to-all-start.1 = ((bf16[4,2,64,1024]{3,2,1,0:T(8,128)(2,1)}), bf16[4,2,64,1024]{3,2,1,0:T(8,128)(2,1)S(1)}, u32[]{:S(2)}, u32[]{:S(2)}) async-start(bf16[4,2,64,1024]{3,2,1,0:T(8,128)(2,1)} %shard_map.90), calls=%async_computation.1 | async-start | bytes 2097152 | tf_op jit(solution)/shard_map/all_to_all | solution.py:33
  127.0 24.2 %copy-start.6 = (bf16[256,512]{1,0:T(8,128)(2,1)S(1)}, bf16[256,512]{1,0:T(8,128)(2,1)}, u32[]{:S(2)}) copy-start(bf16[256,512]{1,0:T(8,128)(2,1)} %copy.18) | copy-start | bytes 786436
  142.3 22.1 %all-to-all-start.2 = ((bf16[16,8,1024]{2,1,0:T(8,128)(2,1)}), bf16[16,8,1024]{2,1,0:T(8,128)(2,1)S(1)}, u32[]{:S(2)}, u32[]{:S(2)}) async-start(bf16[16,8,1024]{2,1,0:T(8,128)(2,1)} %bitcast.14), calls=%async_computation.2 | async-start | bytes 524288 | tf_op jit(solution)/shard_map/all_to_all | solution.py:33

commit v6 on v5

--- a/solution.py
+++ b/solution.py
@@ -77,58 +77,50 @@
     block[...] = own[1 - core[0]]
 
 
-def first_kernel(core, own_g, got_g, own_s, got_s, g, src, first, send):
+def first_kernel(g, src, here, there):
+    here[...] = apply(g[0, 0], g[0, 1], src[0]).astype(BF16)
+    there[...] = apply(g[1, 0], g[1, 1], src[1]).astype(BF16)
+
+
+def begin_kernel(
+    core, own_g, got_g, own_s, got_s, own_c, got_c, own_first, got_first, next_0, next_1,
+    g, src, c, ct, base, start, send, sems,
+):
     here = core[0]
-    g[here] = own_g[here]
-    g[1 - here] = got_g[...]
-    src[here] = own_s[here]
-    src[1 - here] = got_s[...]
-    field = apply(g[0, 0], g[0, 1], src[0]).astype(BF16)
-    send[...] = field
-    first[...] = apply(g[1, 0], g[1, 1], src[1]).astype(BF16)
-
-
-def compose(g, ct, step_a, through, step_b):
+    copies = [
+        pltpu.make_async_copy(own_s.at[here], src.at[here], sems.at[0]),
+        pltpu.make_async_copy(got_s, src.at[1 - here], sems.at[1]),
+        pltpu.make_async_copy(own_g.at[here], g.at[here], sems.at[2]),
+        pltpu.make_async_copy(got_g, g.at[1 - here], sems.at[3]),
+    ]
+    for copy in copies:
+        copy.start()
+    c[here] = own_c[...]
+    c[1 - here] = got_c[...]
+    ct[0] = c[0].T
+    ct[1] = c[1].T
+    first = jnp.where(here == 0, got_first[...], own_first[...])
+    following = next_0[...] + next_1[...]
+    copies[0].wait()
+    copies[1].wait()
+    base_a = src[0].astype(F32) + mul(c[0], first)
+    base[...] = base_a
+    copies[2].wait()
+    copies[3].wait()
+    field = apply(g[0, 0], g[0, 1], base_a.astype(BF16)).astype(BF16)
+    summed = src[1].astype(F32) + mul(c[1], following) + mul(ct[0], field)
+    field = apply(g[1, 0], g[1, 1], summed.astype(BF16)).astype(BF16)
+    flux = mul(ct[1], field)
+    start[...] = flux
+    send[...] = flux.astype(BF16)
+
+
+def compose_kernel(g, ct, step_a, through, step_b):
     step_a[0] = mul(ct[0], g[0, 0]).astype(BF16)
     step_a[1] = mul(ct[0], g[0, 1]).astype(BF16)
     step_b[0] = mul(ct[1], g[1, 0]).astype(BF16)
     step_b[1] = mul(ct[1], g[1, 1]).astype(BF16)
     product(step_b, step_a, through)
-
-
-def begin_kernel(
-    core, g_far, src_far, own_c, got_c, first, following,
-    g, src, c, ct, base, start, send, step_a, through, step_b, g_sem, src_sem,
-):
-    src_copy = pltpu.make_async_copy(src_far, src, src_sem)
-    g_copy = pltpu.make_async_copy(g_far, g, g_sem)
-    src_copy.start()
-    g_copy.start()
-    here = core[0]
-    c[here] = own_c[...]
-    c[1 - here] = got_c[...]
-    ct[0] = c[0].T
-    ct[1] = c[1].T
-    src_copy.wait()
-    base_a = src[0].astype(F32) + mul(c[0], first[...])
-    base[...] = base_a
-    g_copy.wait()
-    field = apply(g[0, 0], g[0, 1], base_a.astype(BF16)).astype(BF16)
-    summed = src[1].astype(F32) + mul(c[1], following[...]) + mul(ct[0], field)
-    field = apply(g[1, 0], g[1, 1], summed.astype(BF16)).astype(BF16)
-    flux = mul(ct[1], field)
-    start[...] = flux
-    send[...] = flux.astype(BF16)
-
-    @pl.when(here == 1)
-    def _():
-        compose(g, ct, step_a, through, step_b)
-
-
-def compose_kernel(core, g, ct, step_a_in, through_in, step_a, through, step_b):
-    @pl.when(core[0] == 0)
-    def _():
-        compose(g, ct, step_a, through, step_b)
 
 
 def compose_back_kernel(g, c, back_a, back_b, back):
@@ -202,7 +194,7 @@
             out[i, j, :, n:] = imag[first : first + rows]
 
 
-def call(kernel, out_shapes, *operands, scratch=(), flops=0, smem=0, far=0, plain=0, aliases=None):
+def call(kernel, out_shapes, *operands, scratch=(), flops=0, smem=0, far=0, plain=0):
     whole = pl.BlockSpec(memory_space=pltpu.VMEM)
     specs = [pl.BlockSpec(memory_space=pltpu.SMEM)] * smem + [pl.BlockSpec(memory_space=pltpu.HBM)] * far
     outs = [pltpu.VMEM(s, d) if i >= plain else jax.ShapeDtypeStruct(s, d) for i, (s, d) in enumerate(out_shapes)]
@@ -219,7 +211,6 @@
         scratch_shapes=list(scratch),
         cost_estimate=pl.CostEstimate(flops=flops, transcendentals=0, bytes_accessed=1 << 20),
         compiler_params=pltpu.CompilerParams(vmem_limit_bytes=24 << 20),
-        input_output_aliases=aliases or {},
     )(*operands)
     return result if len(outs) > 1 else result[0]
 
@@ -255,29 +246,27 @@
     own_c = exchange(mine, None).reshape(n, n)
     own_g, own_s = green_local[:, 0], incident[:, 0].reshape(count, n, cols)
 
+    size = lax.axis_size("slab")
+    first_0, first_1 = call(first_kernel, [(vec, BF16), (vec, BF16)], own_g, own_s, flops=4 * unit)
+    next_0 = lax.ppermute(first_0, "slab", [(i, i - 2) for i in range(2, size, 2)])
+    next_1 = lax.ppermute(first_1, "slab", [(i, i - 1) for i in range(2, size, 2)])
+    got_first = lax.ppermute(first_0, "slab", [(i + 1, i) for i in range(0, size, 2)])
+
     got_g = swap(call(split_kernel, [(mat, BF16)], which, own_g, smem=1))
     got_s = swap(call(split_kernel, [(vec, BF16)], which, own_s, smem=1))
-    green, source, first, send = call(
-        first_kernel,
-        [((2, *mat), BF16), ((2, *vec), BF16), (vec, BF16), (vec, BF16)],
-        which, own_g, got_g, own_s, got_s, smem=1, plain=2, flops=4 * unit,
-    )
-    following = chip_hop(send, -1)
-    own_c, following = lax.optimization_barrier((own_c, following))
+    own_c, next_0, next_1, got_first, got_s = lax.optimization_barrier((own_c, next_0, next_1, got_first, got_s))
     got_c = swap(own_c)
 
     hops = lax.axis_size("slab") // 2 - 1
-    green, source, c, ct, base, start, send, step_a, through = call(
+    green, source, c, ct, base, start, send = call(
         begin_kernel,
-        [((2, *mat), BF16), ((2, *vec), BF16), (mat, BF16), (mat, BF16), (vec, F32), (vec, F32), (vec, BF16)]
-        + [(mat, BF16)] * 2,
-        which, green, source, own_c, got_c, first, following,
-        smem=1, far=2, scratch=[pltpu.VMEM(mat, BF16)] + [pltpu.SemaphoreType.DMA(())] * 2, flops=8 * unit,
+        [((2, *mat), BF16), ((2, *vec), BF16), (mat, BF16), (mat, BF16), (vec, F32), (vec, F32), (vec, BF16)],
+        which, own_g, got_g, own_s, got_s, own_c, got_c, first_1, got_first, next_0, next_1,
+        smem=1, far=4, scratch=[pltpu.SemaphoreType.DMA((4,))], flops=8 * unit,
     )
     flux = chip_hop(send, 1)
     step_a, through = call(
-        compose_kernel, [(mat, BF16), (mat, BF16)], which, green, ct, step_a, through,
-        smem=1, scratch=[pltpu.VMEM(mat, BF16)], flops=16 * n**3, aliases={3: 0, 4: 1},
+        compose_kernel, [(mat, BF16), (mat, BF16)], green, ct, scratch=[pltpu.VMEM(mat, BF16)], flops=16 * n**3
     )
     for _ in range(hops - 1):
         send = call(hop_kernel, [(vec, BF16)], through, start, flux, flops=2 * unit)

time: 166 us -> 159 us (0.958)
  waiting for transfers between devices: 73.5 us -> 66.5 us
  starting transfers between devices: 55.8 us -> 58.8 us
  Pallas kernels: 23.3 us -> 21.3 us
    all_to_all x3, waiting for transfers between devices: 35.2 us -> 28 us  [exchange(): lax.all_to_all(block, 'energy', 0, 0, axis_index_groups=groups, tiled=True)]
    ppermute x0 -> x3, starting transfers between devices: none -> 5.85 us  [the longest x1 3.26 us: shards(): lax.ppermute(first_0, 'slab', [(i, i - 2) for i in range(2, size, 2)])]
    ppermute x0 -> x3, waiting for transfers between devices: none -> 4.56 us  [the longest x1 4.55 us: shards(): lax.ppermute(first_0, 'slab', [(i, i - 2) for i in range(2, size, 2)])]
    ppermute x7 -> x6, starting transfers between devices: 17.4 us -> 13.5 us  [chip_hop(): return lax.ppermute(block, 'slab', route)]
    ppermute x7 -> x6, waiting for transfers between devices: 33.7 us -> 30.6 us  [chip_hop(): return lax.ppermute(block, 'slab', route)]
    pallas_call x15, Pallas kernels: 23.3 us -> 21.3 us  [call(): pl.pallas_call(kernel, out_shape=outs, in_specs=specs + [whole] * (len(op...]
  transfers between devices with their start and end apart: 14 -> 16, of which waited for: 12 -> 12; matrix products, arithmetic and copies ran while one was open for 4% -> 4% of each run, Pallas kernels for 8% -> 7%
where the time goes in v6:
time: 159 us; the launch traced here: 158 us
  waiting for transfers between devices  66.5 us (42%)
  starting transfers between devices  58.8 us (37%)
  Pallas kernels  21.3 us (13%)
  local copies, waits for them, and re-layouts  7.45 us (5%)
  other arithmetic  2.63 us (2%)
    all_to_all x3, starting transfers between devices, exchange(): lax.all_to_all(block, 'energy', 0, 0, axis_index_groups=groups, tiled=True)  31.3 us
    ppermute x6, waiting for transfers between devices, chip_hop(): return lax.ppermute(block, 'slab', route)  30.6 us
    all_to_all x3, waiting for transfers between devices, exchange(): lax.all_to_all(block, 'energy', 0, 0, axis_index_groups=groups, tiled=True)  28 us
    pallas_call x15, Pallas kernels, call(): pl.pallas_call(kernel, out_shape=outs, in_specs=specs + [whole] * (len(op...  21.3 us
    ppermute x6, starting transfers between devices, chip_hop(): return lax.ppermute(block, 'slab', route)  13.5 us
    ppermute x4, starting transfers between devices, swap(): return lax.ppermute(block, 'slab', route)  8.15 us
    unnamed x18, local copies, waits for them, and re-layouts  4.96 us
    ppermute x1, waiting for transfers between devices, shards(): lax.ppermute(first_0, 'slab', [(i, i - 2) for i in range(2, size, 2)])  4.55 us
  transfers between devices with their start and end apart: 16, of which 12 were waited for; matrix products, arithmetic and copies ran while one was open for 4% of the time, Pallas kernels for 7%

profile of v6, /device:TPU:8, one launch (start us, length us, event | category | flops | bytes accessed | tf_op | source)
XLA Modules:
  0.0 158.2 jit_solution(13588685467869029186)
XLA Ops:
  0.6 0.7 copy-done.3
  1.3 0.7 copy-done.4
  2.0 1.4 shard_map.77
  3.5 18.1 %all-to-all-start = ((bf16[64,8,512]{2,1,0:T(8,128)(2,1)}), bf16[64,8,512]{2,1,0:T(8,128)(2,1)S(1)}, u32[]{:S(2)}, u32[]{:S(2)}) async-start(bf16[64,8,512]{2,1,0:T(8,128)(2,1)} %shard_map.77), calls=%async_computation | async-start | bytes 1048576 | tf_op jit(solution)/shard_map/all_to_all | solution.py:33
  21.6 0.0 copy-start
  21.6 1.6 copy-done
  23.2 1.1 shard_map.76
  24.3 1.9 %collective-permute-start = (bf16[2,512,512]{2,1,0:T(8,128)(2,1)}, bf16[2,512,512]{2,1,0:T(8,128)(2,1)}, u32[]{:S(2)}, u32[]{:S(2)}) collective-permute-start(bf16[2,512,512]{2,1,0:T(8,128)(2,1)} %shard_map.76), channel_id=1, source_target_pairs={{0,1},{1,0},{2,3},{3,2},{4,5},{5,4},{6,7},{7,6},{8,9},{9,8},{10,11... | collective-permute-start | bytes 3145736 | tf_op jit(solution)/shard_map/ppermute | solution.py:20
  26.2 1.4 reshape_squeeze.3.src.own.own_s
  27.6 0.0 copy-start.2
  27.6 2.4 %collective-permute-start.4 = (bf16[512,256]{1,0:T(8,128)(2,1)S(1)}, bf16[512,256]{1,0:T(8,128)(2,1)S(1)}, u32[]{:S(2)}, u32[]{:S(2)}) collective-permute-start(bf16[512,256]{1,0:T(8,128)(2,1)S(1)} %shard_map.79), channel_id=1, source_target_pairs={{0,1},{1,0},{2,3},{3,2},{4,5},{5,4},{6,7},{7,6},{8,9},{9,8},{10,11... | collective-permute-start | bytes 786440 | tf_op jit(solution)/shard_map/ppermute | solution.py:20
  30.0 0.7 shard_map.78
  30.8 3.3 %collective-permute-start.1 = (bf16[512,256]{1,0:T(8,128)(2,1)S(1)}, bf16[512,256]{1,0:T(8,128)(2,1)S(1)}, u32[]{:S(2)}, u32[]{:S(2)}) collective-permute-start(bf16[512,256]{1,0:T(8,128)(2,1)S(1)} %get-tuple-element.31), channel_id=1, source_target_pairs={{2,0},{4,2},{6,4},{10,8},{12,10},{14,12},{18,16},{20,18},{22,20},{... | collective-permute-start | bytes 786440 | tf_op jit(solution)/shard_map/ppermute | solution.py:251
  34.0 1.3 collective-permute-start.2
  35.3 1.3 collective-permute-start.3
  36.6 0.0 collective-permute-done.4.got_s
  36.6 4.6 %collective-permute-done.1.next_0 = bf16[512,256]{1,0:T(8,128)(2,1)S(1)} collective-permute-done((bf16[512,256]{1,0:T(8,128)(2,1)S(1)}, bf16[512,256]{1,0:T(8,128)(2,1)S(1)}, u32[]{:S(2)}, u32[]{:S(2)}) %collective-permute-start.1) | collective-permute-done | bytes 262176 | tf_op jit(solution)/shard_map/ppermute | solution.py:251
  41.2 0.0 collective-permute-done.2.next_1
  41.2 0.0 collective-permute-done.3.got_first
  41.2 3.7 %all-to-all-done = bf16[64,8,512]{2,1,0:T(8,128)(2,1)S(1)} async-done(((bf16[64,8,512]{2,1,0:T(8,128)(2,1)}), bf16[64,8,512]{2,1,0:T(8,128)(2,1)S(1)}, u32[]{:S(2)}, u32[]{:S(2)}) %all-to-all-start) | async-done | bytes 524320 | tf_op jit(solution)/shard_map/all_to_all | solution.py:33
  44.9 1.9 %collective-permute-start.5 = (bf16[512,512]{1,0:T(8,128)(2,1)S(1)}, bf16[512,512]{1,0:T(8,128)(2,1)S(1)}, u32[]{:S(2)}, u32[]{:S(2)}) collective-permute-start(bf16[512,512]{1,0:T(8,128)(2,1)S(1)} %bitcast.27), channel_id=1, source_target_pairs={{0,1},{1,0},{2,3},{3,2},{4,5},{5,4},{6,7},{7,6},{8,9},{9,8},{10,11... | collective-permute-start | bytes 1572872 | tf_op jit(solution)/shard_map/ppermute | solution.py:20
  46.9 0.0 collective-permute-done.got_g
  46.9 1.9 %collective-permute-done.5.got_c = bf16[512,512]{1,0:T(8,128)(2,1)S(1)} collective-permute-done((bf16[512,512]{1,0:T(8,128)(2,1)S(1)}, bf16[512,512]{1,0:T(8,128)(2,1)S(1)}, u32[]{:S(2)}, u32[]{:S(2)}) %collective-permute-start.5) | collective-permute-done | bytes 524320 | tf_op jit(solution)/shard_map/ppermute | solution.py:20
  48.7 3.7 %shard_map.80 = (bf16[2,2,512,512]{3,2,1,0:T(8,128)(2,1)S(1)}, bf16[2,512,256]{2,1,0:T(8,128)(2,1)S(1)}, bf16[2,512,512]{2,1,0:T(8,128)(2,1)S(1)}, bf16[2,512,51...) custom-call(s32[1]{0:T(128)} %bitcast.core, ...), custom_call_target="tpu_custom_call" | custom-call | flops 1073741824 | bytes 1048576 | tf_op jit(solution)/shard_map/pallas_call | solution.py:206
  52.5 2.5 %collective-permute-start.6 = (bf16[512,256]{1,0:T(8,128)(2,1)S(1)}, bf16[512,256]{1,0:T(8,128)(2,1)S(1)}, u32[]{:S(2)}, u32[]{:S(2)}) collective-permute-start(bf16[512,256]{1,0:T(8,128)(2,1)S(1)} %get-tuple-element.53), channel_id=1, source_target_pairs={{0,2},{1,3},{2,4},{3,5},{4,6},{5,7},{8,10},{9,11},{10,12},{11,13},... | collective-permute-start | bytes 786440 | tf_op jit(solution)/shard_map/ppermute | solution.py:15
  55.0 2.4 %shard_map.82 = (bf16[2,512,512]{2,1,0:T(8,128)(2,1)S(1)}, bf16[2,512,512]{2,1,0:T(8,128)(2,1)S(1)}) custom-call(bf16[2,2,512,512]{3,2,1,0:T(8,128)(2,1)S(1)} %get-tuple-element.38.g, bf16[2,512,512]{2,1,0:T(8,128)(2,1)S(1)} %get-tuple-element.42.ct), custom_call_target="tpu_custom_call" | custom-call | flops 2147483648 | bytes 1048576 | tf_op jit(solution)/shard_map/pallas_call | solution.py:206
  57.3 5.4 %collective-permute-done.6.arrived = bf16[512,256]{1,0:T(8,128)(2,1)S(1)} collective-permute-done((bf16[512,256]{1,0:T(8,128)(2,1)S(1)}, bf16[512,256]{1,0:T(8,128)(2,1)S(1)}, u32[]{:S(2)}, u32[]{:S(2)}) %collective-permute-start.6) | collective-permute-done | bytes 262176 | tf_op jit(solution)/shard_map/ppermute | solution.py:15
  62.7 0.4 shard_map.84
  63.1 2.5 %collective-permute-start.7 = (bf16[512,256]{1,0:T(8,128)(2,1)S(1)}, bf16[512,256]{1,0:T(8,128)(2,1)S(1)}, u32[]{:S(2)}, u32[]{:S(2)}) collective-permute-start(bf16[512,256]{1,0:T(8,128)(2,1)S(1)} %shard_map.84), channel_id=1, source_target_pairs={{0,2},{1,3},{2,4},{3,5},{4,6},{5,7},{8,10},{9,11},{10,12},{11,13},... | collective-permute-start | bytes 786440 | tf_op jit(solution)/shard_map/ppermute | solution.py:15
  65.7 2.4 %shard_map.81 = (bf16[2,512,512]{2,1,0:T(8,128)(2,1)S(1)}, bf16[2,512,512]{2,1,0:T(8,128)(2,1)S(1)}, bf16[2,512,512]{2,1,0:T(8,128)(2,1)S(1)}) custom-call(bf16[2,2,512,512]{3,2,1,0:T(8,128)(2,1)S(1)} %get-tuple-element.38.g, bf16[2,512,512]{2,1,0:T(8,128)(2,1)S(1)} %get-tuple-element.39.c), custom_call_target="tpu_custom_call" | custom-call | flops 2147483648 | bytes 1048576 | tf_op jit(solution)/shard_map/pallas_call | solution.py:206
  68.0 4.5 %collective-permute-done.7.arrived = bf16[512,256]{1,0:T(8,128)(2,1)S(1)} collective-permute-done((bf16[512,256]{1,0:T(8,128)(2,1)S(1)}, bf16[512,256]{1,0:T(8,128)(2,1)S(1)}, u32[]{:S(2)}, u32[]{:S(2)}) %collective-permute-start.7) | collective-permute-done | bytes 262176 | tf_op jit(solution)/shard_map/ppermute | solution.py:15
  72.5 0.4 shard_map.85
  73.0 2.5 %collective-permute-start.8 = (bf16[512,256]{1,0:T(8,128)(2,1)S(1)}, bf16[512,256]{1,0:T(8,128)(2,1)S(1)}, u32[]{:S(2)}, u32[]{:S(2)}) collective-permute-start(bf16[512,256]{1,0:T(8,128)(2,1)S(1)} %shard_map.85), channel_id=1, source_target_pairs={{0,2},{1,3},{2,4},{3,5},{4,6},{5,7},{8,10},{9,11},{10,12},{11,13},... | collective-permute-start | bytes 786440 | tf_op jit(solution)/shard_map/ppermute | solution.py:15
  75.5 4.1 %shard_map.83 = (bf16[2,512,512]{2,1,0:T(8,128)(2,1)S(1)}, bf16[2,512,512]{2,1,0:T(8,128)(2,1)S(1)}, f32[512,256]{1,0:T(8,128)S(1)}, f32[512,256]{1,0:T(8,128)S(1)}) custom-call(bf16[2,2,512,512]{3,2,1,0:T(8,128)(2,1)S(1)} %get-tuple-element.38.g, bf16[2,512,512]{2,1,0:T(8,128)(2,1)S(1)} %get-tuple-element.43.step_a, ...), custom_call_target="tpu_custom_call" | custom-call | flops 3221225472 | bytes 1048576 | tf_op jit(solution)/shard_map/pallas_call | solution.py:206
  79.6 1.9 %collective-permute-done.8.flux = bf16[512,256]{1,0:T(8,128)(2,1)S(1)} collective-permute-done((bf16[512,256]{1,0:T(8,128)(2,1)S(1)}, bf16[512,256]{1,0:T(8,128)(2,1)S(1)}, u32[]{:S(2)}, u32[]{:S(2)}) %collective-permute-start.8) | collective-permute-done | bytes 262176 | tf_op jit(solution)/shard_map/ppermute | solution.py:15
  81.5 0.7 shard_map.86
  82.2 2.1 %collective-permute-start.9 = (bf16[512,256]{1,0:T(8,128)(2,1)S(1)}, bf16[512,256]{1,0:T(8,128)(2,1)S(1)}, u32[]{:S(2)}, u32[]{:S(2)}) collective-permute-start(bf16[512,256]{1,0:T(8,128)(2,1)S(1)} %get-tuple-element.56), channel_id=1, source_target_pairs={{2,0},{3,1},{4,2},{5,3},{6,4},{7,5},{10,8},{11,9},{12,10},{13,11},... | collective-permute-start | bytes 786440 | tf_op jit(solution)/shard_map/ppermute | solution.py:15
  84.3 6.2 %collective-permute-done.9.arrived = bf16[512,256]{1,0:T(8,128)(2,1)S(1)} collective-permute-done((bf16[512,256]{1,0:T(8,128)(2,1)S(1)}, bf16[512,256]{1,0:T(8,128)(2,1)S(1)}, u32[]{:S(2)}, u32[]{:S(2)}) %collective-permute-start.9) | collective-permute-done | bytes 262176 | tf_op jit(solution)/shard_map/ppermute | solution.py:15
  90.5 0.4 shard_map.87
  90.9 1.9 %collective-permute-start.10 = (bf16[512,256]{1,0:T(8,128)(2,1)S(1)}, bf16[512,256]{1,0:T(8,128)(2,1)S(1)}, u32[]{:S(2)}, u32[]{:S(2)}) collective-permute-start(bf16[512,256]{1,0:T(8,128)(2,1)S(1)} %shard_map.87), channel_id=1, source_target_pairs={{2,0},{3,1},{4,2},{5,3},{6,4},{7,5},{10,8},{11,9},{12,10},{13,11},... | collective-permute-start | bytes 786440 | tf_op jit(solution)/shard_map/ppermute | solution.py:15
  92.8 6.3 %collective-permute-done.10.arrived = bf16[512,256]{1,0:T(8,128)(2,1)S(1)} collective-permute-done((bf16[512,256]{1,0:T(8,128)(2,1)S(1)}, bf16[512,256]{1,0:T(8,128)(2,1)S(1)}, u32[]{:S(2)}, u32[]{:S(2)}) %collective-permute-start.10) | collective-permute-done | bytes 262176 | tf_op jit(solution)/shard_map/ppermute | solution.py:15
  99.2 0.4 shard_map.88
  99.6 0.0 copy-start.7
  99.6 1.9 %collective-permute-start.11 = (bf16[512,256]{1,0:T(8,128)(2,1)S(1)}, bf16[512,256]{1,0:T(8,128)(2,1)S(1)}, u32[]{:S(2)}, u32[]{:S(2)}) collective-permute-start(bf16[512,256]{1,0:T(8,128)(2,1)S(1)} %shard_map.88), channel_id=1, source_target_pairs={{2,0},{3,1},{4,2},{5,3},{6,4},{7,5},{10,8},{11,9},{12,10},{13,11},... | collective-permute-start | bytes 786440 | tf_op jit(solution)/shard_map/ppermute | solution.py:15
  101.6 6.3 %collective-permute-done.11.arrived = bf16[512,256]{1,0:T(8,128)(2,1)S(1)} collective-permute-done((bf16[512,256]{1,0:T(8,128)(2,1)S(1)}, bf16[512,256]{1,0:T(8,128)(2,1)S(1)}, u32[]{:S(2)}, u32[]{:S(2)}) %collective-permute-start.11) | collective-permute-done | bytes 262176 | tf_op jit(solution)/shard_map/ppermute | solution.py:15
  107.9 0.8 shard_map.89
  108.7 1.9 %collective-permute-start.12 = (bf16[512,256]{1,0:T(8,128)(2,1)S(1)}, bf16[512,256]{1,0:T(8,128)(2,1)S(1)}, u32[]{:S(2)}, u32[]{:S(2)}) collective-permute-start(bf16[512,256]{1,0:T(8,128)(2,1)S(1)} %get-tuple-element.58), channel_id=1, source_target_pairs={{0,1},{1,0},{2,3},{3,2},{4,5},{5,4},{6,7},{7,6},{8,9},{9,8},{10,11... | collective-permute-start | bytes 786440 | tf_op jit(solution)/shard_map/ppermute | solution.py:20
  110.6 1.5 collective-permute-done.12.got
  112.1 2.3 %shard_map.90 = bf16[4,2,64,1024]{3,2,1,0:T(8,128)(2,1)} custom-call(s32[1]{0:T(128)} %bitcast.core, f32[2]{0:T(128)S(1)} %add_divide_fusion.weights, bf16[512,256]{1,0:T(8,128)(2,1)S(1)} %get-tuple-element.57.kept, bf16[512,256]{1,0:T(8,128)(2,1)S(1)} %collective-permute-done.12.got), custom_call_target="tpu_custom_call" | custom-call | flops 1073741824 | bytes 1048576 | tf_op jit(solution)/shard_map/pallas_call | solution.py:206
  114.4 3.7 %all-to-all-start.1 = ((bf16[4,2,64,1024]{3,2,1,0:T(8,128)(2,1)}), bf16[4,2,64,1024]{3,2,1,0:T(8,128)(2,1)S(1)}, u32[]{:S(2)}, u32[]{:S(2)}) async-start(bf16[4,2,64,1024]{3,2,1,0:T(8,128)(2,1)} %shard_map.90), calls=%async_computation.1 | async-start | bytes 2097152 | tf_op jit(solution)/shard_map/all_to_all | solution.py:33
  118.1 0.1 stack.18
  118.1 0.1 copy.15
  118.3 0.1 stack.19
  118.4 0.8 copy.16
  119.2 14.3 %all-to-all-done.1 = bf16[4,2,64,1024]{3,2,1,0:T(8,128)(2,1)S(1)} async-done(((bf16[4,2,64,1024]{3,2,1,0:T(8,128)(2,1)}), bf16[4,2,64,1024]{3,2,1,0:T(8,128)(2,1)S(1)}, u32[]{:S(2)}, u32[]{:S(2)}) %all-to-all-start.1) | async-done | bytes 1048608 | tf_op jit(solution)/shard_map/all_to_all | solution.py:33
  133.5 0.9 reduce_sum.21
  134.5 9.5 %all-to-all-start.2 = ((bf16[16,8,1024]{2,1,0:T(8,128)(2,1)}), bf16[16,8,1024]{2,1,0:T(8,128)(2,1)S(1)}, u32[]{:S(2)}, u32[]{:S(2)}) async-start(bf16[16,8,1024]{2,1,0:T(8,128)(2,1)} %bitcast.14), calls=%async_computation.2 | async-start | bytes 524288 | tf_op jit(solution)/shard_map/all_to_all | solution.py:33
  144.0 0.3 fusion
  144.3 0.3 fusion.1
  144.7 0.1 pad_maximum_fusion.1
  144.7 1.3 copy.13
  146.1 1.6 pad_maximum_fusion
  147.6 9.9 %all-to-all-done.2 = bf16[16,8,1024]{2,1,0:T(8,128)(2,1)S(1)} async-done(((bf16[16,8,1024]{2,1,0:T(8,128)(2,1)}), bf16[16,8,1024]{2,1,0:T(8,128)(2,1)S(1)}, u32[]{:S(2)}, u32[]{:S(2)}) %all-to-all-start.2) | async-done | bytes 262176 | tf_op jit(solution)/shard_map/all_to_all | solution.py:33
  157.6 0.6 copy.14
  (14 shorter events, 0.1 us)
Async XLA Ops:
  0.6 0.7 copy-start.3
  1.3 0.7 copy-start.4
  3.5 41.5 %all-to-all-start = ((bf16[64,8,512]{2,1,0:T(8,128)(2,1)}), bf16[64,8,512]{2,1,0:T(8,128)(2,1)S(1)}, u32[]{:S(2)}, u32[]{:S(2)}) async-start(bf16[64,8,512]{2,1,0:T(8,128)(2,1)} %shard_map.77), calls=%async_computation | async-start | bytes 1048576 | tf_op jit(solution)/shard_map/all_to_all | solution.py:33
  21.6 1.6 %copy-start = (bf16[2,1,2,512,512]{4,3,2,1,0:T(8,128)(2,1)S(1)}, bf16[2,1,2,512,512]{4,3,2,1,0:T(8,128)(2,1)}, u32[]{:S(2)}) copy-start(bf16[2,1,2,512,512]{4,3,2,1,0:T(8,128)(2,1)} %param.5) | copy-start | bytes 6291460
  23.2 6.8 %copy-start.1 = (bf16[2,1,2,512,512]{4,3,2,1,0:T(8,128)(2,1)S(1)}, bf16[2,1,2,512,512]{4,3,2,1,0:T(8,128)(2,1)}, u32[]{:S(2)}) copy-start(bf16[2,1,2,512,512]{4,3,2,1,0:T(8,128)(2,1)} %param.5) | copy-start | bytes 6291460
  24.3 22.6 %collective-permute-start = (bf16[2,512,512]{2,1,0:T(8,128)(2,1)}, bf16[2,512,512]{2,1,0:T(8,128)(2,1)}, u32[]{:S(2)}, u32[]{:S(2)}) collective-permute-start(bf16[2,512,512]{2,1,0:T(8,128)(2,1)} %shard_map.76), channel_id=1, source_target_pairs={{0,1},{1,0},{2,3},{3,2},{4,5},{5,4},{6,7},{7,6},{8,9},{9,8},{10,11... | collective-permute-start | bytes 3145736 | tf_op jit(solution)/shard_map/ppermute | solution.py:20
  27.6 21.2 %copy-start.2 = (bf16[2,512,256]{2,1,0:T(8,128)(2,1)}, bf16[2,512,256]{2,1,0:T(8,128)(2,1)S(1)}, u32[]{:S(2)}) copy-start(bf16[2,512,256]{2,1,0:T(8,128)(2,1)S(1)} %reshape_squeeze.3.src.own.own_s) | copy-start | bytes 1572868
  27.6 9.0 %collective-permute-start.4 = (bf16[512,256]{1,0:T(8,128)(2,1)S(1)}, bf16[512,256]{1,0:T(8,128)(2,1)S(1)}, u32[]{:S(2)}, u32[]{:S(2)}) collective-permute-start(bf16[512,256]{1,0:T(8,128)(2,1)S(1)} %shard_map.79), channel_id=1, source_target_pairs={{0,1},{1,0},{2,3},{3,2},{4,5},{5,4},{6,7},{7,6},{8,9},{9,8},{10,11... | collective-permute-start | bytes 786440 | tf_op jit(solution)/shard_map/ppermute | solution.py:20
  30.8 10.4 %collective-permute-start.1 = (bf16[512,256]{1,0:T(8,128)(2,1)S(1)}, bf16[512,256]{1,0:T(8,128)(2,1)S(1)}, u32[]{:S(2)}, u32[]{:S(2)}) collective-permute-start(bf16[512,256]{1,0:T(8,128)(2,1)S(1)} %get-tuple-element.31), channel_id=1, source_target_pairs={{2,0},{4,2},{6,4},{10,8},{12,10},{14,12},{18,16},{20,18},{22,20},{... | collective-permute-start | bytes 786440 | tf_op jit(solution)/shard_map/ppermute | solution.py:251
  34.0 7.2 %collective-permute-start.2 = (bf16[512,256]{1,0:T(8,128)(2,1)S(1)}, bf16[512,256]{1,0:T(8,128)(2,1)S(1)}, u32[]{:S(2)}, u32[]{:S(2)}) collective-permute-start(bf16[512,256]{1,0:T(8,128)(2,1)S(1)} %get-tuple-element.32.own_first), channel_id=1, source_target_pairs={{2,1},{4,3},{6,5},{10,9},{12,11},{14,13},{18,17},{20,19},{22,21},{... | collective-permute-start | bytes 786440 | tf_op jit(solution)/shard_map/ppermute | solution.py:252
  35.3 5.9 %collective-permute-start.3 = (bf16[512,256]{1,0:T(8,128)(2,1)S(1)}, bf16[512,256]{1,0:T(8,128)(2,1)S(1)}, u32[]{:S(2)}, u32[]{:S(2)}) collective-permute-start(bf16[512,256]{1,0:T(8,128)(2,1)S(1)} %get-tuple-element.31), channel_id=1, source_target_pairs={{1,0},{3,2},{5,4},{7,6},{9,8},{11,10},{13,12},{15,14},{17,16},{19,... | collective-permute-start | bytes 786440 | tf_op jit(solution)/shard_map/ppermute | solution.py:253
  36.6 4.6 %copy-start.6 = (bf16[512,256]{1,0:T(8,128)(2,1)}, bf16[512,256]{1,0:T(8,128)(2,1)S(1)}, u32[]{:S(2)}) copy-start(bf16[512,256]{1,0:T(8,128)(2,1)S(1)} %collective-permute-done.4.got_s) | copy-start | bytes 786436
  44.9 3.8 %collective-permute-start.5 = (bf16[512,512]{1,0:T(8,128)(2,1)S(1)}, bf16[512,512]{1,0:T(8,128)(2,1)S(1)}, u32[]{:S(2)}, u32[]{:S(2)}) collective-permute-start(bf16[512,512]{1,0:T(8,128)(2,1)S(1)} %bitcast.27), channel_id=1, source_target_pairs={{0,1},{1,0},{2,3},{3,2},{4,5},{5,4},{6,7},{7,6},{8,9},{9,8},{10,11... | collective-permute-start | bytes 1572872 | tf_op jit(solution)/shard_map/ppermute | solution.py:20
  52.5 10.2 %collective-permute-start.6 = (bf16[512,256]{1,0:T(8,128)(2,1)S(1)}, bf16[512,256]{1,0:T(8,128)(2,1)S(1)}, u32[]{:S(2)}, u32[]{:S(2)}) collective-permute-start(bf16[512,256]{1,0:T(8,128)(2,1)S(1)} %get-tuple-element.53), channel_id=1, source_target_pairs={{0,2},{1,3},{2,4},{3,5},{4,6},{5,7},{8,10},{9,11},{10,12},{11,13},... | collective-permute-start | bytes 786440 | tf_op jit(solution)/shard_map/ppermute | solution.py:15
  63.1 9.4 %collective-permute-start.7 = (bf16[512,256]{1,0:T(8,128)(2,1)S(1)}, bf16[512,256]{1,0:T(8,128)(2,1)S(1)}, u32[]{:S(2)}, u32[]{:S(2)}) collective-permute-start(bf16[512,256]{1,0:T(8,128)(2,1)S(1)} %shard_map.84), channel_id=1, source_target_pairs={{0,2},{1,3},{2,4},{3,5},{4,6},{5,7},{8,10},{9,11},{10,12},{11,13},... | collective-permute-start | bytes 786440 | tf_op jit(solution)/shard_map/ppermute | solution.py:15
  73.0 8.5 %collective-permute-start.8 = (bf16[512,256]{1,0:T(8,128)(2,1)S(1)}, bf16[512,256]{1,0:T(8,128)(2,1)S(1)}, u32[]{:S(2)}, u32[]{:S(2)}) collective-permute-start(bf16[512,256]{1,0:T(8,128)(2,1)S(1)} %shard_map.85), channel_id=1, source_target_pairs={{0,2},{1,3},{2,4},{3,5},{4,6},{5,7},{8,10},{9,11},{10,12},{11,13},... | collective-permute-start | bytes 786440 | tf_op jit(solution)/shard_map/ppermute | solution.py:15
  82.2 8.3 %collective-permute-start.9 = (bf16[512,256]{1,0:T(8,128)(2,1)S(1)}, bf16[512,256]{1,0:T(8,128)(2,1)S(1)}, u32[]{:S(2)}, u32[]{:S(2)}) collective-permute-start(bf16[512,256]{1,0:T(8,128)(2,1)S(1)} %get-tuple-element.56), channel_id=1, source_target_pairs={{2,0},{3,1},{4,2},{5,3},{6,4},{7,5},{10,8},{11,9},{12,10},{13,11},... | collective-permute-start | bytes 786440 | tf_op jit(solution)/shard_map/ppermute | solution.py:15
  90.9 8.3 %collective-permute-start.10 = (bf16[512,256]{1,0:T(8,128)(2,1)S(1)}, bf16[512,256]{1,0:T(8,128)(2,1)S(1)}, u32[]{:S(2)}, u32[]{:S(2)}) collective-permute-start(bf16[512,256]{1,0:T(8,128)(2,1)S(1)} %shard_map.87), channel_id=1, source_target_pairs={{2,0},{3,1},{4,2},{5,3},{6,4},{7,5},{10,8},{11,9},{12,10},{13,11},... | collective-permute-start | bytes 786440 | tf_op jit(solution)/shard_map/ppermute | solution.py:15
  99.6 11.0 %copy-start.7 = (s32[2]{0:T(128)S(1)}, s32[2]{0:T(128)}, u32[]{:S(2)}) copy-start(s32[2]{0:T(128)} %param.9) | copy-start | bytes 28
  99.6 8.3 %collective-permute-start.11 = (bf16[512,256]{1,0:T(8,128)(2,1)S(1)}, bf16[512,256]{1,0:T(8,128)(2,1)S(1)}, u32[]{:S(2)}, u32[]{:S(2)}) collective-permute-start(bf16[512,256]{1,0:T(8,128)(2,1)S(1)} %shard_map.88), channel_id=1, source_target_pairs={{2,0},{3,1},{4,2},{5,3},{6,4},{7,5},{10,8},{11,9},{12,10},{13,11},... | collective-permute-start | bytes 786440 | tf_op jit(solution)/shard_map/ppermute | solution.py:15
  108.7 3.4 %collective-permute-start.12 = (bf16[512,256]{1,0:T(8,128)(2,1)S(1)}, bf16[512,256]{1,0:T(8,128)(2,1)S(1)}, u32[]{:S(2)}, u32[]{:S(2)}) collective-permute-start(bf16[512,256]{1,0:T(8,128)(2,1)S(1)} %get-tuple-element.58), channel_id=1, source_target_pairs={{0,1},{1,0},{2,3},{3,2},{4,5},{5,4},{6,7},{7,6},{8,9},{9,8},{10,11... | collective-permute-start | bytes 786440 | tf_op jit(solution)/shard_map/ppermute | solution.py:20
  114.4 19.2 %all-to-all-start.1 = ((bf16[4,2,64,1024]{3,2,1,0:T(8,128)(2,1)}), bf16[4,2,64,1024]{3,2,1,0:T(8,128)(2,1)S(1)}, u32[]{:S(2)}, u32[]{:S(2)}) async-start(bf16[4,2,64,1024]{3,2,1,0:T(8,128)(2,1)} %shard_map.90), calls=%async_computation.1 | async-start | bytes 2097152 | tf_op jit(solution)/shard_map/all_to_all | solution.py:33
  119.2 25.1 %copy-start.5 = (bf16[256,512]{1,0:T(8,128)(2,1)S(1)}, bf16[256,512]{1,0:T(8,128)(2,1)}, u32[]{:S(2)}) copy-start(bf16[256,512]{1,0:T(8,128)(2,1)} %copy.16) | copy-start | bytes 786436
  134.5 23.1 %all-to-all-start.2 = ((bf16[16,8,1024]{2,1,0:T(8,128)(2,1)}), bf16[16,8,1024]{2,1,0:T(8,128)(2,1)S(1)}, u32[]{:S(2)}, u32[]{:S(2)}) async-start(bf16[16,8,1024]{2,1,0:T(8,128)(2,1)} %bitcast.14), calls=%async_computation.2 | async-start | bytes 524288 | tf_op jit(solution)/shard_map/all_to_all | solution.py:33

commit v7 on v6

--- a/solution.py
+++ b/solution.py
@@ -123,27 +123,26 @@
     product(step_b, step_a, through)
 
 
-def compose_back_kernel(g, c, back_a, back_b, back):
+def compose_back_kernel(g, c, step_a, src, base, back_a, back_b, back, to_b, field_b):
     back_a[0] = mul(g[0, 0], c[0]).astype(BF16)
     back_a[1] = mul(g[0, 1], c[0]).astype(BF16)
     back_b[0] = mul(g[1, 0], c[1]).astype(BF16)
     back_b[1] = mul(g[1, 1], c[1]).astype(BF16)
     product(back_a, back_b, back)
-
-
-def compose_turn_kernel(g, step_a, back_a, src, base, to_b, to_a, field_b, field_a):
     gbr, gbi = g[1, 0], g[1, 1]
     sr, si = step_a[0], step_a[1]
     to_b[0] = (mul(gbr, sr) - mul(gbi, si)).astype(BF16)
     to_b[1] = (mul(gbr, si) + mul(gbi, sr)).astype(BF16)
+    flux_a = apply(sr, si, base[...].astype(BF16))
+    field_b[...] = apply(gbr, gbi, (src[1].astype(F32) + flux_a).astype(BF16))
+
+
+def compose_turn_a_kernel(g, back_a, src, to_b, field_b, to_a, field_a):
     ar, ai = back_a[0], back_a[1]
     br, bi = to_b[0], to_b[1]
     to_a[0] = (g[0, 0].astype(F32) + mul(ar, br) - mul(ai, bi)).astype(BF16)
     to_a[1] = (g[0, 1].astype(F32) + mul(ar, bi) + mul(ai, br)).astype(BF16)
-    flux_a = apply(sr, si, base[...].astype(BF16))
-    here = apply(gbr, gbi, (src[1].astype(F32) + flux_a).astype(BF16))
-    field_b[...] = here
-    field_a[...] = apply(g[0, 0], g[0, 1], src[0]) + apply(ar, ai, here.astype(BF16))
+    field_a[...] = apply(g[0, 0], g[0, 1], src[0]) + apply(ar, ai, field_b[...].astype(BF16))
 
 
 def hop_kernel(matrix, start, arrived, send):
@@ -173,25 +172,30 @@
         send[...] = wave_a
 
 
-def density_kernel(core, weights, kept, got, out):
-    n, _ = kept.shape
-    outer, inner, rows, _ = out.shape
-    here = weights[core[0]]
-    there = weights[1 - core[0]]
-    real = jnp.zeros((n, n), F32)
-    imag = jnp.zeros((n, n), F32)
-    for weight, wave in ((here, kept), (there, got)):
-        w = wave[...]
-        scaled = (w.astype(F32) * weight).astype(BF16)
-        real = real + mul_transposed(scaled, w)
-        imag = imag + mul_transposed(scaled, turned(w))
-    real = real.astype(BF16)
-    imag = imag.astype(BF16)
-    for i in range(outer):
-        for j in range(inner):
-            first = (j * outer + i) * rows
-            out[i, j, :, :n] = real[first : first + rows]
-            out[i, j, :, n:] = imag[first : first + rows]
+def density_kernel(place, weights, kept, got, out):
+    n = kept.shape[0]
+    ny, rows, _ = out.shape
+    here = weights[place[0]]
+    there = weights[1 - place[0]]
+    for y in range(ny):
+        at = pl.multiple_of(y * (n // ny) + place[1] * rows, rows)
+        real = jnp.zeros((rows, n), F32)
+        imag = jnp.zeros((rows, n), F32)
+        for weight, wave in ((here, kept), (there, got)):
+            w = wave[...]
+            scaled = (wave[pl.ds(at, rows), :].astype(F32) * weight).astype(BF16)
+            real = real + mul_transposed(scaled, w)
+            imag = imag + mul_transposed(scaled, turned(w))
+        out[y, :, :n] = real.astype(out.dtype)
+        out[y, :, n:] = imag.astype(out.dtype)
+
+
+def sum_kernel(own, *refs):
+    *others, out = refs
+    total = own[...]
+    for other in others:
+        total = total + other[...].astype(F32)
+    out[...] = total.astype(BF16)
 
 
 def call(kernel, out_shapes, *operands, scratch=(), flops=0, smem=0, far=0, plain=0):
@@ -228,7 +232,6 @@
     devices = lax.axis_size("energy")
     ny, nx, nz = energy_grid(devices)
     at = lambda y, x, z: (y * nx + x) * nz + z
-    along_x = [[at(y, x, z) for x in range(nx)] for y in range(ny) for z in range(nz)]
     along_yz = [[at(y, x, z) for y in range(ny) for z in range(nz)] for x in range(nx)]
     rows = coupling.shape[1]
     tile = n // masks.shape[1]
@@ -268,14 +271,20 @@
     step_a, through = call(
         compose_kernel, [(mat, BF16), (mat, BF16)], green, ct, scratch=[pltpu.VMEM(mat, BF16)], flops=16 * n**3
     )
-    for _ in range(hops - 1):
+    for step in range(hops - 1):
+        if step == hops - 2:
+            back_a, back_b, back, to_b, field_b = call(
+                compose_back_kernel,
+                [(mat, BF16)] * 4 + [(vec, F32)],
+                green, c, step_a, source, base, flops=24 * n**3 + 4 * unit,
+            )
+            flux, back_a, to_b = lax.optimization_barrier((flux, back_a, to_b))
         send = call(hop_kernel, [(vec, BF16)], through, start, flux, flops=2 * unit)
         flux = chip_hop(send, 1)
-    back_a, back_b, back = call(compose_back_kernel, [(mat, BF16)] * 3, green, c, flops=16 * n**3)
-    to_b, to_a, field_b, field_a = call(
-        compose_turn_kernel,
-        [(mat, BF16), (mat, BF16), (vec, F32), (vec, F32)],
-        green, step_a, back_a, source, base, flops=16 * n**3 + 8 * unit,
+    to_a, field_a = call(
+        compose_turn_a_kernel,
+        [(mat, BF16), (vec, F32)],
+        green, back_a, source, to_b, field_b, flops=8 * n**3 + 4 * unit,
     )
     start, end, send = call(
         turn_kernel, [(vec, F32), (vec, F32), (vec, BF16)], to_a, to_b, field_a, field_b, flux, flops=4 * unit
@@ -290,11 +299,20 @@
 
     got = swap(send)
     weights = fermi(energy_index, 4.0 / (count * devices * modes))
-    partial = call(
-        density_kernel, [((nx, ny, nz * rows, 2 * n), BF16)], which, weights, kept, got, smem=2, flops=8 * unit
-    )
-    parts = exchange(partial, along_x)
-    summed = jnp.sum(parts.astype(F32), axis=0).astype(BF16)
+    x_here = lax.rem(lax.axis_index("energy") // nz, nx)
+    block = (ny, nz * rows, 2 * n)
+
+    def density_of(step, kind):
+        place = jnp.stack([core, lax.rem(x_here + step, nx)])
+        return call(density_kernel, [(block, kind)], place, weights, kept, got, smem=2, flops=2 * unit)
+
+    arrived = []
+    for step in (nx // 2, *[k for k in range(1, nx) if k != nx // 2]):
+        route = [
+            (at(y, x, z), at(y, (x + step) % nx, z)) for y in range(ny) for x in range(nx) for z in range(nz)
+        ]
+        arrived.append(lax.ppermute(density_of(step, BF16), "energy", route))
+    summed = call(sum_kernel, [(block, BF16)], density_of(0, F32), *arrived)
     parts = exchange(summed.reshape(ny * nz, rows, 2 * n), along_yz)
     density = jnp.sum(parts.astype(F32), axis=0).reshape(1, rows, 2, n)
 

time: 159 us -> 165 us (1.038)
  waiting for transfers between devices: 66.5 us -> 53.4 us
  starting transfers between devices: 58.8 us -> 65.2 us
  Pallas kernels: 21.3 us -> 27.2 us
  local copies, waits for them, and re-layouts: 7.45 us -> 13.2 us
    all_to_all x3 -> x2, waiting for transfers between devices: 28 us -> 12.2 us  [exchange(): lax.all_to_all(block, 'energy', 0, 0, axis_index_groups=groups, tiled=True)]
    ppermute x0 -> x3, starting transfers between devices: none -> 10.1 us  [shards(): arrived.append(lax.ppermute(density_of(step, BF16), 'energy', route))]
    pallas_call x15 -> x19, Pallas kernels: 21.3 us -> 27.2 us  [call(): pl.pallas_call(kernel, out_shape=outs, in_specs=specs + [whole] * (len(op...]
    all_to_all x3 -> x2, starting transfers between devices: 31.3 us -> 27.5 us  [exchange(): lax.all_to_all(block, 'energy', 0, 0, axis_index_groups=groups, tiled=True)]
    another operation x2, local copies, waits for them, and re-layouts: 0.13 us -> 2.56 us  [ordered(): return jnp.stack([jnp.where(even, kept, got), jnp.where(even, got, kept)])]
    ppermute x0 -> x3, waiting for transfers between devices: none -> 2.39 us  [shards(): arrived.append(lax.ppermute(density_of(step, BF16), 'energy', route))]
    unnamed x18 -> x29, local copies, waits for them, and re-layouts: 4.96 us -> 5.98 us
  transfers between devices with their start and end apart: 16 -> 18, of which waited for: 12 -> 12; matrix products, arithmetic and copies ran while one was open for 4% -> 7% of each run, Pallas kernels for 7% -> 9%
where the time goes in v7:
time: 165 us; the launch traced here: 164 us
  starting transfers between devices  65.2 us (40%)
  waiting for transfers between devices  53.4 us (32%)
  Pallas kernels  27.2 us (16%)
  local copies, waits for them, and re-layouts  13.2 us (8%)
  other arithmetic  2.7 us (2%)
  matrix products  1.67 us (1%)
    ppermute x6, waiting for transfers between devices, chip_hop(): return lax.ppermute(block, 'slab', route)  30.7 us
    all_to_all x2, starting transfers between devices, exchange(): lax.all_to_all(block, 'energy', 0, 0, axis_index_groups=groups, tiled=True)  27.5 us
    pallas_call x19, Pallas kernels, call(): pl.pallas_call(kernel, out_shape=outs, in_specs=specs + [whole] * (len(op...  27.2 us
    ppermute x6, starting transfers between devices, chip_hop(): return lax.ppermute(block, 'slab', route)  13.6 us
    all_to_all x2, waiting for transfers between devices, exchange(): lax.all_to_all(block, 'energy', 0, 0, axis_index_groups=groups, tiled=True)  12.2 us
    ppermute x3, starting transfers between devices, shards(): arrived.append(lax.ppermute(density_of(step, BF16), 'energy', route))  10.1 us
    ppermute x4, starting transfers between devices, swap(): return lax.ppermute(block, 'slab', route)  8.13 us
    unnamed x29, local copies, waits for them, and re-layouts  5.98 us
  transfers between devices with their start and end apart: 18, of which 12 were waited for; matrix products, arithmetic and copies ran while one was open for 7% of the time, Pallas kernels for 9%

profile of v7, /device:TPU:8, one launch (start us, length us, event | category | flops | bytes accessed | tf_op | source)
XLA Modules:
  0.0 164.4 jit_solution(9178184710307760220)
XLA Ops:
  0.6 0.7 copy-done.7
  1.3 0.7 copy-done.8
  2.0 1.4 shard_map.77
  3.5 18.1 %all-to-all-start = ((bf16[64,8,512]{2,1,0:T(8,128)(2,1)}), bf16[64,8,512]{2,1,0:T(8,128)(2,1)S(1)}, u32[]{:S(2)}, u32[]{:S(2)}) async-start(bf16[64,8,512]{2,1,0:T(8,128)(2,1)} %shard_map.77), calls=%async_computation | async-start | bytes 1048576 | tf_op jit(solution)/shard_map/all_to_all | solution.py:33
  21.6 1.6 copy-done
  23.2 1.0 shard_map.76
  24.3 1.9 %collective-permute-start = (bf16[2,512,512]{2,1,0:T(8,128)(2,1)}, bf16[2,512,512]{2,1,0:T(8,128)(2,1)}, u32[]{:S(2)}, u32[]{:S(2)}) collective-permute-start(bf16[2,512,512]{2,1,0:T(8,128)(2,1)} %shard_map.76), channel_id=1, source_target_pairs={{0,1},{1,0},{2,3},{3,2},{4,5},{5,4},{6,7},{7,6},{8,9},{9,8},{10,11... | collective-permute-start | bytes 3145736 | tf_op jit(solution)/shard_map/ppermute | solution.py:20
  26.2 1.4 reshape_squeeze.3.src.own.own_s
  27.6 2.4 %collective-permute-start.4 = (bf16[512,256]{1,0:T(8,128)(2,1)S(1)}, bf16[512,256]{1,0:T(8,128)(2,1)S(1)}, u32[]{:S(2)}, u32[]{:S(2)}) collective-permute-start(bf16[512,256]{1,0:T(8,128)(2,1)S(1)} %shard_map.79), channel_id=1, source_target_pairs={{0,1},{1,0},{2,3},{3,2},{4,5},{5,4},{6,7},{7,6},{8,9},{9,8},{10,11... | collective-permute-start | bytes 786440 | tf_op jit(solution)/shard_map/ppermute | solution.py:20
  30.0 0.7 shard_map.78
  30.7 3.3 %collective-permute-start.1 = (bf16[512,256]{1,0:T(8,128)(2,1)S(1)}, bf16[512,256]{1,0:T(8,128)(2,1)S(1)}, u32[]{:S(2)}, u32[]{:S(2)}) collective-permute-start(bf16[512,256]{1,0:T(8,128)(2,1)S(1)} %get-tuple-element.34), channel_id=1, source_target_pairs={{2,0},{4,2},{6,4},{10,8},{12,10},{14,12},{18,16},{20,18},{22,20},{... | collective-permute-start | bytes 786440 | tf_op jit(solution)/shard_map/ppermute | solution.py:254
  34.0 1.3 collective-permute-start.2
  35.3 1.3 collective-permute-start.3
  36.6 4.6 %collective-permute-done.1.next_0 = bf16[512,256]{1,0:T(8,128)(2,1)S(1)} collective-permute-done((bf16[512,256]{1,0:T(8,128)(2,1)S(1)}, bf16[512,256]{1,0:T(8,128)(2,1)S(1)}, u32[]{:S(2)}, u32[]{:S(2)}) %collective-permute-start.1) | collective-permute-done | bytes 262176 | tf_op jit(solution)/shard_map/ppermute | solution.py:254
  41.2 3.7 %all-to-all-done = bf16[64,8,512]{2,1,0:T(8,128)(2,1)S(1)} async-done(((bf16[64,8,512]{2,1,0:T(8,128)(2,1)}), bf16[64,8,512]{2,1,0:T(8,128)(2,1)S(1)}, u32[]{:S(2)}, u32[]{:S(2)}) %all-to-all-start) | async-done | bytes 524320 | tf_op jit(solution)/shard_map/all_to_all | solution.py:33
  44.9 1.9 %collective-permute-start.5 = (bf16[512,512]{1,0:T(8,128)(2,1)S(1)}, bf16[512,512]{1,0:T(8,128)(2,1)S(1)}, u32[]{:S(2)}, u32[]{:S(2)}) collective-permute-start(bf16[512,512]{1,0:T(8,128)(2,1)S(1)} %bitcast.30), channel_id=1, source_target_pairs={{0,1},{1,0},{2,3},{3,2},{4,5},{5,4},{6,7},{7,6},{8,9},{9,8},{10,11... | collective-permute-start | bytes 1572872 | tf_op jit(solution)/shard_map/ppermute | solution.py:20
  46.9 1.9 %collective-permute-done.5.got_c = bf16[512,512]{1,0:T(8,128)(2,1)S(1)} collective-permute-done((bf16[512,512]{1,0:T(8,128)(2,1)S(1)}, bf16[512,512]{1,0:T(8,128)(2,1)S(1)}, u32[]{:S(2)}, u32[]{:S(2)}) %collective-permute-start.5) | collective-permute-done | bytes 524320 | tf_op jit(solution)/shard_map/ppermute | solution.py:20
  48.7 3.7 %shard_map.80 = (bf16[2,2,512,512]{3,2,1,0:T(8,128)(2,1)S(1)}, bf16[2,512,256]{2,1,0:T(8,128)(2,1)S(1)}, bf16[2,512,512]{2,1,0:T(8,128)(2,1)S(1)}, bf16[2,512,51...) custom-call(s32[1]{0:T(128)} %bitcast.core, ...), custom_call_target="tpu_custom_call" | custom-call | flops 1073741824 | bytes 1048576 | tf_op jit(solution)/shard_map/pallas_call | solution.py:210
  52.5 2.5 %collective-permute-start.6 = (bf16[512,256]{1,0:T(8,128)(2,1)S(1)}, bf16[512,256]{1,0:T(8,128)(2,1)S(1)}, u32[]{:S(2)}, u32[]{:S(2)}) collective-permute-start(bf16[512,256]{1,0:T(8,128)(2,1)S(1)} %get-tuple-element.51), channel_id=1, source_target_pairs={{0,2},{1,3},{2,4},{3,5},{4,6},{5,7},{8,10},{9,11},{10,12},{11,13},... | collective-permute-start | bytes 786440 | tf_op jit(solution)/shard_map/ppermute | solution.py:15
  55.0 2.3 %shard_map.81 = (bf16[2,512,512]{2,1,0:T(8,128)(2,1)S(1)}, bf16[2,512,512]{2,1,0:T(8,128)(2,1)S(1)}) custom-call(bf16[2,2,512,512]{3,2,1,0:T(8,128)(2,1)S(1)} %get-tuple-element.41.g, bf16[2,512,512]{2,1,0:T(8,128)(2,1)S(1)} %get-tuple-element.43.ct), custom_call_target="tpu_custom_call" | custom-call | flops 2147483648 | bytes 1048576 | tf_op jit(solution)/shard_map/pallas_call | solution.py:210
  57.3 5.4 %collective-permute-done.6.arrived = bf16[512,256]{1,0:T(8,128)(2,1)S(1)} collective-permute-done((bf16[512,256]{1,0:T(8,128)(2,1)S(1)}, bf16[512,256]{1,0:T(8,128)(2,1)S(1)}, u32[]{:S(2)}, u32[]{:S(2)}) %collective-permute-start.6) | collective-permute-done | bytes 262176 | tf_op jit(solution)/shard_map/ppermute | solution.py:15
  62.7 0.4 shard_map.83
  63.1 2.5 %collective-permute-start.7 = (bf16[512,256]{1,0:T(8,128)(2,1)S(1)}, bf16[512,256]{1,0:T(8,128)(2,1)S(1)}, u32[]{:S(2)}, u32[]{:S(2)}) collective-permute-start(bf16[512,256]{1,0:T(8,128)(2,1)S(1)} %shard_map.83), channel_id=1, source_target_pairs={{0,2},{1,3},{2,4},{3,5},{4,6},{5,7},{8,10},{9,11},{10,12},{11,13},... | collective-permute-start | bytes 786440 | tf_op jit(solution)/shard_map/ppermute | solution.py:15
  65.7 4.6 %shard_map.82 = (bf16[2,512,512]{2,1,0:T(8,128)(2,1)S(1)}, bf16[2,512,512]{2,1,0:T(8,128)(2,1)S(1)}, bf16[2,512,512]{2,1,0:T(8,128)(2,1)S(1)}, bf16[2,512,512]{2,1,0:T(8,128)(2,1)S(1)}, f32[512,256]{1,0:T(8,128)S(1)}) custom-call(bf16[2,2,512,512]{3,2,1,0:T(8,128)(2,1)S(1)} %get-tuple-element.41.g, bf16[2,512,512]{2,1,0:T(8,128)(2,1)S(1)} %get-tuple-element.42.c, ...), custom_call_target="tpu_custom_call" | custom-call | flops 3758096384 | bytes 1048576 | tf_op jit(solution)/shard_map/pallas_call | solution.py:210
  70.2 2.3 %collective-permute-done.7.arrived = bf16[512,256]{1,0:T(8,128)(2,1)S(1)} collective-permute-done((bf16[512,256]{1,0:T(8,128)(2,1)S(1)}, bf16[512,256]{1,0:T(8,128)(2,1)S(1)}, u32[]{:S(2)}, u32[]{:S(2)}) %collective-permute-start.7) | collective-permute-done | bytes 262176 | tf_op jit(solution)/shard_map/ppermute | solution.py:15
  72.6 0.4 shard_map.85
  73.0 2.5 %collective-permute-start.8 = (bf16[512,256]{1,0:T(8,128)(2,1)S(1)}, bf16[512,256]{1,0:T(8,128)(2,1)S(1)}, u32[]{:S(2)}, u32[]{:S(2)}) collective-permute-start(bf16[512,256]{1,0:T(8,128)(2,1)S(1)} %shard_map.85), channel_id=1, source_target_pairs={{0,2},{1,3},{2,4},{3,5},{4,6},{5,7},{8,10},{9,11},{10,12},{11,13},... | collective-permute-start | bytes 786440 | tf_op jit(solution)/shard_map/ppermute | solution.py:15
  75.5 1.8 %shard_map.84 = (bf16[2,512,512]{2,1,0:T(8,128)(2,1)S(1)}, f32[512,256]{1,0:T(8,128)S(1)}) custom-call(bf16[2,2,512,512]{3,2,1,0:T(8,128)(2,1)S(1)} %get-tuple-element.41.g, bf16[2,512,512]{2,1,0:T(8,128)(2,1)S(1)} %get-tuple-element.54.back_a, bf16[2,512,256]{2,1,0:T(8,128)(2,1)S(1)} %get-tuple-element.45.src, ...), custom_call_target="tpu_custom_call" | custom-call | flops 1610612736 | bytes 1048576 | tf_op jit(solution)/shard_map/pallas_call | solution.py:210
  77.3 4.2 %collective-permute-done.8.flux = bf16[512,256]{1,0:T(8,128)(2,1)S(1)} collective-permute-done((bf16[512,256]{1,0:T(8,128)(2,1)S(1)}, bf16[512,256]{1,0:T(8,128)(2,1)S(1)}, u32[]{:S(2)}, u32[]{:S(2)}) %collective-permute-start.8) | collective-permute-done | bytes 262176 | tf_op jit(solution)/shard_map/ppermute | solution.py:15
  81.5 0.7 shard_map.86
  82.2 2.1 %collective-permute-start.9 = (bf16[512,256]{1,0:T(8,128)(2,1)S(1)}, bf16[512,256]{1,0:T(8,128)(2,1)S(1)}, u32[]{:S(2)}, u32[]{:S(2)}) collective-permute-start(bf16[512,256]{1,0:T(8,128)(2,1)S(1)} %get-tuple-element.62), channel_id=1, source_target_pairs={{2,0},{3,1},{4,2},{5,3},{6,4},{7,5},{10,8},{11,9},{12,10},{13,11},... | collective-permute-start | bytes 786440 | tf_op jit(solution)/shard_map/ppermute | solution.py:15
  84.3 6.2 %collective-permute-done.9.arrived = bf16[512,256]{1,0:T(8,128)(2,1)S(1)} collective-permute-done((bf16[512,256]{1,0:T(8,128)(2,1)S(1)}, bf16[512,256]{1,0:T(8,128)(2,1)S(1)}, u32[]{:S(2)}, u32[]{:S(2)}) %collective-permute-start.9) | collective-permute-done | bytes 262176 | tf_op jit(solution)/shard_map/ppermute | solution.py:15
  90.5 0.4 shard_map.87
  90.9 1.9 %collective-permute-start.10 = (bf16[512,256]{1,0:T(8,128)(2,1)S(1)}, bf16[512,256]{1,0:T(8,128)(2,1)}, u32[]{:S(2)}, u32[]{:S(2)}) collective-permute-start(bf16[512,256]{1,0:T(8,128)(2,1)S(1)} %shard_map.87), channel_id=1, source_target_pairs={{2,0},{3,1},{4,2},{5,3},{6,4},{7,5},{10,8},{11,9},{12,10},{13,11},... | collective-permute-start | bytes 786440 | tf_op jit(solution)/shard_map/ppermute | solution.py:15
  92.9 6.4 %collective-permute-done.10.arrived = bf16[512,256]{1,0:T(8,128)(2,1)} collective-permute-done((bf16[512,256]{1,0:T(8,128)(2,1)S(1)}, bf16[512,256]{1,0:T(8,128)(2,1)}, u32[]{:S(2)}, u32[]{:S(2)}) %collective-permute-start.10) | collective-permute-done | bytes 262176 | tf_op jit(solution)/shard_map/ppermute | solution.py:15
  99.3 2.1 %shard_map.88 = bf16[512,256]{1,0:T(8,128)(2,1)} custom-call(bf16[2,512,512]{2,1,0:T(8,128)(2,1)S(1)} %get-tuple-element.47.matrix.back, f32[512,256]{1,0:T(8,128)S(1)} %get-tuple-element.60.start, bf16[512,256]{1,0:T(8,128)(2,1)} %collective-permute-done.10.arrived), custom_call_target="tpu_custom_call" | custom-call | flops 268435456 | bytes 1048576 | tf_op jit(solution)/shard_map/pallas_call | solution.py:210
  101.4 2.0 %collective-permute-start.11 = (bf16[512,256]{1,0:T(8,128)(2,1)}, bf16[512,256]{1,0:T(8,128)(2,1)S(1)}, u32[]{:S(2)}, u32[]{:S(2)}) collective-permute-start(bf16[512,256]{1,0:T(8,128)(2,1)} %shard_map.88), channel_id=1, source_target_pairs={{2,0},{3,1},{4,2},{5,3},{6,4},{7,5},{10,8},{11,9},{12,10},{13,11},... | collective-permute-start | bytes 786440 | tf_op jit(solution)/shard_map/ppermute | solution.py:15
  103.7 6.3 %collective-permute-done.11.arrived = bf16[512,256]{1,0:T(8,128)(2,1)S(1)} collective-permute-done((bf16[512,256]{1,0:T(8,128)(2,1)}, bf16[512,256]{1,0:T(8,128)(2,1)S(1)}, u32[]{:S(2)}, u32[]{:S(2)}) %collective-permute-start.11) | collective-permute-done | bytes 262176 | tf_op jit(solution)/shard_map/ppermute | solution.py:15
  110.0 0.7 copy-done.5
  110.7 0.9 copy-done.6
  111.6 1.5 shard_map.89
  113.1 1.9 %collective-permute-start.12 = (bf16[512,256]{1,0:T(8,128)(2,1)}, bf16[512,256]{1,0:T(8,128)(2,1)S(1)}, u32[]{:S(2)}, u32[]{:S(2)}) collective-permute-start(bf16[512,256]{1,0:T(8,128)(2,1)} %get-tuple-element.64), channel_id=1, source_target_pairs={{0,1},{1,0},{2,3},{3,2},{4,5},{5,4},{6,7},{7,6},{8,9},{9,8},{10,11... | collective-permute-start | bytes 786440 | tf_op jit(solution)/shard_map/ppermute | solution.py:20
  115.1 1.6 collective-permute-done.12.got
  116.7 1.3 shard_map.93
  118.0 4.3 %collective-permute-start.15 = (bf16[2,64,1024]{2,1,0:T(8,128)(2,1)S(1)}, bf16[2,64,1024]{2,1,0:T(8,128)(2,1)S(1)}, u32[]{:S(2)}, u32[]{:S(2)}) collective-permute-start(bf16[2,64,1024]{2,1,0:T(8,128)(2,1)S(1)} %shard_map.93), channel_id=1, source_target_pairs={{0,192},{8,200},{16,208},{24,216},{32,224},{40,232},{48,240},{56,2... | collective-permute-start | bytes 786440 | tf_op jit(solution)/shard_map/ppermute | solution.py:314
  122.3 1.3 shard_map.92
  123.6 1.9 %collective-permute-start.14 = (bf16[2,64,1024]{2,1,0:T(8,128)(2,1)S(1)}, bf16[2,64,1024]{2,1,0:T(8,128)(2,1)S(1)}, u32[]{:S(2)}, u32[]{:S(2)}) collective-permute-start(bf16[2,64,1024]{2,1,0:T(8,128)(2,1)S(1)} %shard_map.92), channel_id=1, source_target_pairs={{0,64},{8,72},{16,80},{24,88},{32,96},{40,104},{48,112},{56,120},{... | collective-permute-start | bytes 786440 | tf_op jit(solution)/shard_map/ppermute | solution.py:314
  125.5 1.3 shard_map.91
  126.8 3.9 %collective-permute-start.13 = (bf16[2,64,1024]{2,1,0:T(8,128)(2,1)S(1)}, bf16[2,64,1024]{2,1,0:T(8,128)(2,1)S(1)}, u32[]{:S(2)}, u32[]{:S(2)}) collective-permute-start(bf16[2,64,1024]{2,1,0:T(8,128)(2,1)S(1)} %shard_map.91), channel_id=1, source_target_pairs={{0,128},{8,136},{16,144},{24,152},{32,160},{40,168},{48,176},{56,1... | collective-permute-start | bytes 786440 | tf_op jit(solution)/shard_map/ppermute | solution.py:314
  130.8 0.7 broadcast_select_fusion.1
  131.5 0.8 stack.46
  132.2 0.8 copy.11
  133.1 1.8 %stack.47 = bf16[1,1,512,2,128]{4,3,2,1,0:T(2,128)(2,1)} reshape(bf16[512,256]{1,0:T(8,128)(2,1)} %get-tuple-element.69) | data formatting | bytes 524288 | tf_op jit(solution)/shard_map/stack | solution.py:29
  134.9 1.8 %copy.12 = bf16[256,512]{1,0:T(8,128)(2,1)} copy(bf16[256,512]{0,1:T(8,128)(2,1)} %bitcast.34) | data formatting | bytes 524288 | tf_op jit(solution)/shard_map/dot_general | solution.py:41
  136.7 1.3 shard_map.90.own
  138.0 2.4 %collective-permute-done.14.refs_1_ = bf16[2,64,1024]{2,1,0:T(8,128)(2,1)S(1)} collective-permute-done((bf16[2,64,1024]{2,1,0:T(8,128)(2,1)S(1)}, bf16[2,64,1024]{2,1,0:T(8,128)(2,1)S(1)}, u32[]{:S(2)}, u32[]{:S(2)}) %collective-permute-start.14) | collective-permute-done | bytes 262176 | tf_op jit(solution)/shard_map/ppermute | solution.py:314
  140.4 0.8 shard_map.94
  141.2 9.3 %all-to-all-start.1 = ((bf16[16,8,1024]{2,1,0:T(8,128)(2,1)}), bf16[16,8,1024]{2,1,0:T(8,128)(2,1)S(1)}, u32[]{:S(2)}, u32[]{:S(2)}) async-start(bf16[16,8,1024]{2,1,0:T(8,128)(2,1)} %bitcast.18), calls=%async_computation.1 | async-start | bytes 524288 | tf_op jit(solution)/shard_map/all_to_all | solution.py:33
  150.6 1.3 fusion
  152.0 0.3 fusion.1
  152.4 1.3 copy.10
  153.7 1.6 pad_maximum_fusion
  155.3 8.5 %all-to-all-done.1 = bf16[16,8,1024]{2,1,0:T(8,128)(2,1)S(1)} async-done(((bf16[16,8,1024]{2,1,0:T(8,128)(2,1)}), bf16[16,8,1024]{2,1,0:T(8,128)(2,1)S(1)}, u32[]{:S(2)}, u32[]{:S(2)}) %all-to-all-start.1) | async-done | bytes 262176 | tf_op jit(solution)/shard_map/all_to_all | solution.py:33
  163.8 0.6 reshape.79
  (37 shorter events, 0.5 us)
Async XLA Ops:
  0.6 0.7 copy-start.7
  1.3 0.7 copy-start.8
  3.5 41.5 %all-to-all-start = ((bf16[64,8,512]{2,1,0:T(8,128)(2,1)}), bf16[64,8,512]{2,1,0:T(8,128)(2,1)S(1)}, u32[]{:S(2)}, u32[]{:S(2)}) async-start(bf16[64,8,512]{2,1,0:T(8,128)(2,1)} %shard_map.77), calls=%async_computation | async-start | bytes 1048576 | tf_op jit(solution)/shard_map/all_to_all | solution.py:33
  21.6 1.6 copy-start
  23.2 6.8 %copy-start.1 = (bf16[2,1,2,512,512]{4,3,2,1,0:T(8,128)(2,1)S(1)}, bf16[2,1,2,512,512]{4,3,2,1,0:T(8,128)(2,1)}, u32[]{:S(2)}) copy-start(bf16[2,1,2,512,512]{4,3,2,1,0:T(8,128)(2,1)} %param.5) | copy-start | bytes 6291460
  24.3 22.6 %collective-permute-start = (bf16[2,512,512]{2,1,0:T(8,128)(2,1)}, bf16[2,512,512]{2,1,0:T(8,128)(2,1)}, u32[]{:S(2)}, u32[]{:S(2)}) collective-permute-start(bf16[2,512,512]{2,1,0:T(8,128)(2,1)} %shard_map.76), channel_id=1, source_target_pairs={{0,1},{1,0},{2,3},{3,2},{4,5},{5,4},{6,7},{7,6},{8,9},{9,8},{10,11... | collective-permute-start | bytes 3145736 | tf_op jit(solution)/shard_map/ppermute | solution.py:20
  27.6 21.2 %copy-start.2 = (bf16[2,512,256]{2,1,0:T(8,128)(2,1)}, bf16[2,512,256]{2,1,0:T(8,128)(2,1)S(1)}, u32[]{:S(2)}) copy-start(bf16[2,512,256]{2,1,0:T(8,128)(2,1)S(1)} %reshape_squeeze.3.src.own.own_s) | copy-start | bytes 1572868
  27.6 9.0 %collective-permute-start.4 = (bf16[512,256]{1,0:T(8,128)(2,1)S(1)}, bf16[512,256]{1,0:T(8,128)(2,1)S(1)}, u32[]{:S(2)}, u32[]{:S(2)}) collective-permute-start(bf16[512,256]{1,0:T(8,128)(2,1)S(1)} %shard_map.79), channel_id=1, source_target_pairs={{0,1},{1,0},{2,3},{3,2},{4,5},{5,4},{6,7},{7,6},{8,9},{9,8},{10,11... | collective-permute-start | bytes 786440 | tf_op jit(solution)/shard_map/ppermute | solution.py:20
  30.7 10.5 %collective-permute-start.1 = (bf16[512,256]{1,0:T(8,128)(2,1)S(1)}, bf16[512,256]{1,0:T(8,128)(2,1)S(1)}, u32[]{:S(2)}, u32[]{:S(2)}) collective-permute-start(bf16[512,256]{1,0:T(8,128)(2,1)S(1)} %get-tuple-element.34), channel_id=1, source_target_pairs={{2,0},{4,2},{6,4},{10,8},{12,10},{14,12},{18,16},{20,18},{22,20},{... | collective-permute-start | bytes 786440 | tf_op jit(solution)/shard_map/ppermute | solution.py:254
  34.0 7.2 %collective-permute-start.2 = (bf16[512,256]{1,0:T(8,128)(2,1)S(1)}, bf16[512,256]{1,0:T(8,128)(2,1)S(1)}, u32[]{:S(2)}, u32[]{:S(2)}) collective-permute-start(bf16[512,256]{1,0:T(8,128)(2,1)S(1)} %get-tuple-element.35.own_first), channel_id=1, source_target_pairs={{2,1},{4,3},{6,5},{10,9},{12,11},{14,13},{18,17},{20,19},{22,21},{... | collective-permute-start | bytes 786440 | tf_op jit(solution)/shard_map/ppermute | solution.py:255
  35.3 5.9 %collective-permute-start.3 = (bf16[512,256]{1,0:T(8,128)(2,1)S(1)}, bf16[512,256]{1,0:T(8,128)(2,1)S(1)}, u32[]{:S(2)}, u32[]{:S(2)}) collective-permute-start(bf16[512,256]{1,0:T(8,128)(2,1)S(1)} %get-tuple-element.34), channel_id=1, source_target_pairs={{1,0},{3,2},{5,4},{7,6},{9,8},{11,10},{13,12},{15,14},{17,16},{19,... | collective-permute-start | bytes 786440 | tf_op jit(solution)/shard_map/ppermute | solution.py:256
  36.6 4.6 %copy-start.12 = (bf16[512,256]{1,0:T(8,128)(2,1)}, bf16[512,256]{1,0:T(8,128)(2,1)S(1)}, u32[]{:S(2)}) copy-start(bf16[512,256]{1,0:T(8,128)(2,1)S(1)} %collective-permute-done.4.got_s) | copy-start | bytes 786436
  44.9 3.8 %collective-permute-start.5 = (bf16[512,512]{1,0:T(8,128)(2,1)S(1)}, bf16[512,512]{1,0:T(8,128)(2,1)S(1)}, u32[]{:S(2)}, u32[]{:S(2)}) collective-permute-start(bf16[512,512]{1,0:T(8,128)(2,1)S(1)} %bitcast.30), channel_id=1, source_target_pairs={{0,1},{1,0},{2,3},{3,2},{4,5},{5,4},{6,7},{7,6},{8,9},{9,8},{10,11... | collective-permute-start | bytes 1572872 | tf_op jit(solution)/shard_map/ppermute | solution.py:20
  52.5 4.9 %copy-start.3 = (bf16[2,512,512]{2,1,0:T(8,128)(2,1)}, bf16[2,512,512]{2,1,0:T(8,128)(2,1)S(1)}, u32[]{:S(2)}) copy-start(bf16[2,512,512]{2,1,0:T(8,128)(2,1)S(1)} %get-tuple-element.43.ct) | copy-start | bytes 3145732
  52.5 10.2 %collective-permute-start.6 = (bf16[512,256]{1,0:T(8,128)(2,1)S(1)}, bf16[512,256]{1,0:T(8,128)(2,1)S(1)}, u32[]{:S(2)}, u32[]{:S(2)}) collective-permute-start(bf16[512,256]{1,0:T(8,128)(2,1)S(1)} %get-tuple-element.51), channel_id=1, source_target_pairs={{0,2},{1,3},{2,4},{3,5},{4,6},{5,7},{8,10},{9,11},{10,12},{11,13},... | collective-permute-start | bytes 786440 | tf_op jit(solution)/shard_map/ppermute | solution.py:15
  63.1 9.4 %collective-permute-start.7 = (bf16[512,256]{1,0:T(8,128)(2,1)S(1)}, bf16[512,256]{1,0:T(8,128)(2,1)S(1)}, u32[]{:S(2)}, u32[]{:S(2)}) collective-permute-start(bf16[512,256]{1,0:T(8,128)(2,1)S(1)} %shard_map.83), channel_id=1, source_target_pairs={{0,2},{1,3},{2,4},{3,5},{4,6},{5,7},{8,10},{9,11},{10,12},{11,13},... | collective-permute-start | bytes 786440 | tf_op jit(solution)/shard_map/ppermute | solution.py:15
  73.0 8.5 %collective-permute-start.8 = (bf16[512,256]{1,0:T(8,128)(2,1)S(1)}, bf16[512,256]{1,0:T(8,128)(2,1)S(1)}, u32[]{:S(2)}, u32[]{:S(2)}) collective-permute-start(bf16[512,256]{1,0:T(8,128)(2,1)S(1)} %shard_map.85), channel_id=1, source_target_pairs={{0,2},{1,3},{2,4},{3,5},{4,6},{5,7},{8,10},{9,11},{10,12},{11,13},... | collective-permute-start | bytes 786440 | tf_op jit(solution)/shard_map/ppermute | solution.py:15
  82.2 8.3 %collective-permute-start.9 = (bf16[512,256]{1,0:T(8,128)(2,1)S(1)}, bf16[512,256]{1,0:T(8,128)(2,1)S(1)}, u32[]{:S(2)}, u32[]{:S(2)}) collective-permute-start(bf16[512,256]{1,0:T(8,128)(2,1)S(1)} %get-tuple-element.62), channel_id=1, source_target_pairs={{2,0},{3,1},{4,2},{5,3},{6,4},{7,5},{10,8},{11,9},{12,10},{13,11},... | collective-permute-start | bytes 786440 | tf_op jit(solution)/shard_map/ppermute | solution.py:15
  90.9 8.4 %collective-permute-start.10 = (bf16[512,256]{1,0:T(8,128)(2,1)S(1)}, bf16[512,256]{1,0:T(8,128)(2,1)}, u32[]{:S(2)}, u32[]{:S(2)}) collective-permute-start(bf16[512,256]{1,0:T(8,128)(2,1)S(1)} %shard_map.87), channel_id=1, source_target_pairs={{2,0},{3,1},{4,2},{5,3},{6,4},{7,5},{10,8},{11,9},{12,10},{13,11},... | collective-permute-start | bytes 786440 | tf_op jit(solution)/shard_map/ppermute | solution.py:15
  101.4 13.7 %copy-start.13 = (s32[2]{0:T(128)S(1)}, s32[2]{0:T(128)}, u32[]{:S(2)}) copy-start(s32[2]{0:T(128)} %param.9) | copy-start | bytes 28
  101.4 8.6 %collective-permute-start.11 = (bf16[512,256]{1,0:T(8,128)(2,1)}, bf16[512,256]{1,0:T(8,128)(2,1)S(1)}, u32[]{:S(2)}, u32[]{:S(2)}) collective-permute-start(bf16[512,256]{1,0:T(8,128)(2,1)} %shard_map.88), channel_id=1, source_target_pairs={{2,0},{3,1},{4,2},{5,3},{6,4},{7,5},{10,8},{11,9},{12,10},{13,11},... | collective-permute-start | bytes 786440 | tf_op jit(solution)/shard_map/ppermute | solution.py:15
  110.0 0.7 copy-start.5
  110.7 0.9 copy-start.6
  113.1 3.6 %collective-permute-start.12 = (bf16[512,256]{1,0:T(8,128)(2,1)}, bf16[512,256]{1,0:T(8,128)(2,1)S(1)}, u32[]{:S(2)}, u32[]{:S(2)}) collective-permute-start(bf16[512,256]{1,0:T(8,128)(2,1)} %get-tuple-element.64), channel_id=1, source_target_pairs={{0,1},{1,0},{2,3},{3,2},{4,5},{5,4},{6,7},{7,6},{8,9},{9,8},{10,11... | collective-permute-start | bytes 786440 | tf_op jit(solution)/shard_map/ppermute | solution.py:20
  118.0 20.0 %collective-permute-start.15 = (bf16[2,64,1024]{2,1,0:T(8,128)(2,1)S(1)}, bf16[2,64,1024]{2,1,0:T(8,128)(2,1)S(1)}, u32[]{:S(2)}, u32[]{:S(2)}) collective-permute-start(bf16[2,64,1024]{2,1,0:T(8,128)(2,1)S(1)} %shard_map.93), channel_id=1, source_target_pairs={{0,192},{8,200},{16,208},{24,216},{32,224},{40,232},{48,240},{56,2... | collective-permute-start | bytes 786440 | tf_op jit(solution)/shard_map/ppermute | solution.py:314
  123.6 16.8 %collective-permute-start.14 = (bf16[2,64,1024]{2,1,0:T(8,128)(2,1)S(1)}, bf16[2,64,1024]{2,1,0:T(8,128)(2,1)S(1)}, u32[]{:S(2)}, u32[]{:S(2)}) collective-permute-start(bf16[2,64,1024]{2,1,0:T(8,128)(2,1)S(1)} %shard_map.92), channel_id=1, source_target_pairs={{0,64},{8,72},{16,80},{24,88},{32,96},{40,104},{48,112},{56,120},{... | collective-permute-start | bytes 786440 | tf_op jit(solution)/shard_map/ppermute | solution.py:314
  126.8 13.6 %collective-permute-start.13 = (bf16[2,64,1024]{2,1,0:T(8,128)(2,1)S(1)}, bf16[2,64,1024]{2,1,0:T(8,128)(2,1)S(1)}, u32[]{:S(2)}, u32[]{:S(2)}) collective-permute-start(bf16[2,64,1024]{2,1,0:T(8,128)(2,1)S(1)} %shard_map.91), channel_id=1, source_target_pairs={{0,128},{8,136},{16,144},{24,152},{32,160},{40,168},{48,176},{56,1... | collective-permute-start | bytes 786440 | tf_op jit(solution)/shard_map/ppermute | solution.py:314
  133.1 17.5 %copy-start.4 = (bf16[2,512,512]{2,1,0:T(8,128)(2,1)S(1)}, bf16[2,512,512]{2,1,0:T(8,128)(2,1)}, u32[]{:S(2)}) copy-start(bf16[2,512,512]{2,1,0:T(8,128)(2,1)} %copy-done.3) | copy-start | bytes 3145732
  138.0 14.0 %copy-start.11 = (bf16[256,512]{1,0:T(8,128)(2,1)S(1)}, bf16[256,512]{1,0:T(8,128)(2,1)}, u32[]{:S(2)}) copy-start(bf16[256,512]{1,0:T(8,128)(2,1)} %copy.12) | copy-start | bytes 786436
  141.2 22.5 %all-to-all-start.1 = ((bf16[16,8,1024]{2,1,0:T(8,128)(2,1)}), bf16[16,8,1024]{2,1,0:T(8,128)(2,1)S(1)}, u32[]{:S(2)}, u32[]{:S(2)}) async-start(bf16[16,8,1024]{2,1,0:T(8,128)(2,1)} %bitcast.18), calls=%async_computation.1 | async-start | bytes 524288 | tf_op jit(solution)/shard_map/all_to_all | solution.py:33
  150.6 3.1 %copy-start.9 = (bf16[1,1,512,2,128]{4,3,2,1,0:T(2,128)(2,1)S(1)}, bf16[1,1,512,2,128]{4,3,2,1,0:T(2,128)(2,1)}, u32[]{:S(2)}) copy-start(bf16[1,1,512,2,128]{4,3,2,1,0:T(2,128)(2,1)} %stack.46) | copy-start | bytes 786436
  150.6 3.1 %copy-start.10 = (bf16[1,1,512,2,128]{4,3,2,1,0:T(2,128)(2,1)S(1)}, bf16[1,1,512,2,128]{4,3,2,1,0:T(2,128)(2,1)}, u32[]{:S(2)}) copy-start(bf16[1,1,512,2,128]{4,3,2,1,0:T(2,128)(2,1)} %stack.47) | copy-start | bytes 786436
